TPU v7x, 32 devices: a whole 2x2x4 slice. The times are simulated.
32 devices in a mesh: dp: 8 (over y, x, core), mp: 4 (over z).
Axes of the slice: x: 2, y: 2, z: 4, core: 2. Of those that a mesh axis runs over, the one named last changes fastest.
Arguments:
- decoder_in: bfloat16 [8192, 768], P(('dp', 'mp')), may hold values from -6 to 6
- encoder_out: bfloat16 [4096, 768], P(('dp', 'mp')), may hold values from -6 to 6
- seq_lengths: int32 [8], P('dp'), may hold values from 1 to 1024, 6144 in all
- rel_buckets: int32 [1024], replicated, may hold values from 0 to 31, as said below
- norm_gains: bfloat16 [3, 768], replicated, may hold values from 0.5 to 1.5
- rel_bias: bfloat16 [32, 12], P(None, 'mp'), may hold values from -4 to 4
- self_query: bfloat16 [768, 768], P('dp', 'mp'), may hold values from -0.0546875 to 0.0546875
- self_key: bfloat16 [768, 768], P('dp', 'mp'), may hold values from -0.21875 to 0.21875
- self_value: bfloat16 [768, 768], P('dp', 'mp'), may hold values from -0.21875 to 0.21875
- self_out: bfloat16 [768, 768], P('mp', 'dp'), may hold values from -0.875 to 0.875
- cross_query: bfloat16 [768, 768], P('dp', 'mp'), may hold values from -0.0546875 to 0.0546875
- cross_key: bfloat16 [768, 768], P('dp', 'mp'), may hold values from -0.21875 to 0.21875
- cross_value: bfloat16 [768, 768], P('dp', 'mp'), may hold values from -0.21875 to 0.21875
- cross_out: bfloat16 [768, 768], P('mp', 'dp'), may hold values from -0.875 to 0.875
- gate_weight: bfloat16 [768, 2048], P('dp', 'mp'), may hold values from -0.21875 to 0.21875
- up_weight: bfloat16 [768, 2048], P('dp', 'mp'), may hold values from -0.21875 to 0.21875
- down_weight: bfloat16 [2048, 768], P('mp', 'dp'), may hold values from -0.125 to 0.125
- out_grad: bfloat16 [8192, 768], P(('dp', 'mp')), may hold values from -6 to 6
Outputs:
- layer_out: bfloat16 [8192, 768], P(('dp', 'mp'))
- decoder_grad: float32 [8192, 768], P(('dp', 'mp'))
- encoder_grad: float32 [4096, 768], P(('dp', 'mp'))
- gains_grad: float32 [3, 768], replicated
- bias_grad: float32 [32, 12], replicated
- self_query_grad: float32 [768, 768], P('dp', 'mp')
- self_key_grad: float32 [768, 768], P('dp', 'mp')
- self_value_grad: float32 [768, 768], P('dp', 'mp')
- self_out_grad: float32 [768, 768], P('mp', 'dp')
- cross_query_grad: float32 [768, 768], P('dp', 'mp')
- cross_key_grad: float32 [768, 768], P('dp', 'mp')
- cross_value_grad: float32 [768, 768], P('dp', 'mp')
- cross_out_grad: float32 [768, 768], P('mp', 'dp')
- gate_grad: float32 [768, 2048], P('dp', 'mp')
- up_grad: float32 [768, 2048], P('dp', 'mp')
- down_grad: float32 [2048, 768], P('mp', 'dp')
Inputs may be any that keep to these rules, and one draw needn't show every extreme that they name: `seq_lengths`: the largest length is exactly 1024; the lengths sum to 6144. `rel_buckets`: Non-decreasing in the distance; equal to the distance below 16; equal to 31 from distance 128 on.
All inputs are finite; a program needn't handle non-finite values. No bound on the sum of `seq_lengths` on one device may be relied on, other than what follows from the above.
Results may differ from a plain program's by a relative error of at most 0.04.
Values may be sent and summed in bfloat16 or wider, within the bound.
A program may use at most 576 MiB of HBM per device.

v0:
```python
import jax
import jax.numpy as jnp
from jax import lax
from jax.sharding import PartitionSpec as P

NB = 32
SLOT = 1024


epsilon = 1e-06
masked_score = -1e30


def full_rows(share):
    return lax.all_gather(share, "mp", axis=0, tiled=True)


def share_rows(total):
    return lax.psum_scatter(
        total.astype(jnp.bfloat16), "mp", scatter_dimension=0, tiled=True
    ).astype(jnp.float32)


def norm_forward(stream, gain, width):
    inverse = lax.rsqrt(jnp.sum(stream * stream, axis=1) / width + epsilon)
    normed = (stream * inverse[:, None] * gain[None, :]).astype(jnp.bfloat16)
    return (full_rows(normed), inverse)


def norm_backward(stream, gain, inverse, upstream, width):
    scaled = upstream * gain[None, :]
    dotted = jnp.sum(scaled * stream, axis=1)
    back = (
        inverse[:, None] * scaled - stream * (inverse * inverse * inverse * dotted / width)[:, None]
    )
    gain_grad = jnp.sum(upstream * stream * inverse[:, None], axis=0)
    return (back, gain_grad)


def heads_first(value, heads):
    return value.reshape(value.shape[0], heads, -1).transpose(1, 0, 2)


def heads_last(value):
    return value.transpose(1, 0, 2).reshape(value.shape[1], -1)


def block_scores(query_block, keys_seq, masking, index, start):
    scores = jnp.einsum("hqd,hkd->hqk", query_block, keys_seq, preferred_element_type=jnp.float32)
    reducer = None
    if masking is not None:
        extra, allowed, reducer = masking(index, start)
        scores = jnp.where(allowed[None], scores + extra, masked_score)
    return (scores, reducer)


def attention_forward(query, keys, values, heads, masking):
    block = min(512, SLOT)
    outputs = []
    totals = []
    keys_seq = heads_first(keys, heads)
    values_seq = heads_first(values, heads)
    for start in range(0, SLOT, block):
        query_block = heads_first(query[start : start + block], heads)
        scores, reducer = block_scores(query_block, keys_seq, masking, 0, start)
        top = jnp.max(scores, axis=2, keepdims=True)
        log_total = top + jnp.log(jnp.sum(jnp.exp(scores - top), axis=2, keepdims=True))
        probs = jnp.exp(scores - log_total).astype(jnp.bfloat16)
        mixed = jnp.einsum("hqk,hkd->hqd", probs, values_seq, preferred_element_type=jnp.float32)
        outputs.append(heads_last(mixed))
        totals.append(log_total)
    return (jnp.concatenate(outputs, axis=0), totals)


def attention_backward(query, keys, values, totals, d_mixed, heads, masking):
    block = min(512, SLOT)
    query_parts = []
    bucket_grad = jnp.zeros((NB, heads), jnp.float32)
    count = 0
    keys_seq = heads_first(keys, heads)
    values_seq = heads_first(values, heads)
    key_acc = jnp.zeros(keys_seq.shape, jnp.float32)
    value_acc = jnp.zeros(values_seq.shape, jnp.float32)
    for start in range(0, SLOT, block):
        query_block = heads_first(query[start : start + block], heads)
        grad_block = heads_first(d_mixed[start : start + block], heads)
        scores, reducer = block_scores(query_block, keys_seq, masking, 0, start)
        probs = jnp.exp(scores - totals[count])
        count = count + 1
        d_probs = jnp.einsum(
            "hqd,hkd->hqk", grad_block, values_seq, preferred_element_type=jnp.float32
        )
        delta = jnp.sum(probs * d_probs, axis=2, keepdims=True)
        d_scores = (probs * (d_probs - delta)).astype(jnp.bfloat16)
        query_parts.append(
            heads_last(
                jnp.einsum("hqk,hkd->hqd", d_scores, keys_seq, preferred_element_type=jnp.float32)
            )
        )
        key_acc = key_acc + jnp.einsum(
            "hqk,hqd->hkd", d_scores, query_block, preferred_element_type=jnp.float32
        )
        value_acc = value_acc + jnp.einsum(
            "hqk,hqd->hkd",
            probs.astype(jnp.bfloat16),
            grad_block,
            preferred_element_type=jnp.float32,
        )
        if reducer is not None:
            bucket_grad = bucket_grad + reducer(d_scores)
    key_parts = heads_last(key_acc)
    value_parts = heads_last(value_acc)
    return (jnp.concatenate(query_parts, axis=0), key_parts, value_parts, bucket_grad)


def contract_rows(left, right):
    return jnp.einsum("tc,th->ch", left, right, preferred_element_type=jnp.float32)


def times_transposed(left, weight):
    return jnp.einsum("th,ch->tc", left, weight, preferred_element_type=jnp.float32)


def per_device(
    decoder_in,
    encoder_out,
    seq_lengths,
    rel_buckets,
    norm_gains,
    rel_bias,
    self_query,
    self_key,
    self_value,
    self_out,
    cross_query,
    cross_key,
    cross_value,
    cross_out,
    gate_weight,
    up_weight,
    down_weight,
    out_grad,
):
    width = decoder_in.shape[1]
    local_rows = decoder_in.shape[0]
    heads = rel_bias.shape[1]
    seqs = seq_lengths.shape[0]
    gains = norm_gains.astype(jnp.float32)
    w_query, w_key, w_value, w_out, c_query, c_key, c_value, c_out, w_gate, w_up, w_down = (
        lax.all_gather(self_query, "dp", axis=0, tiled=True),
        lax.all_gather(self_key, "dp", axis=0, tiled=True),
        lax.all_gather(self_value, "dp", axis=0, tiled=True),
        lax.all_gather(self_out, "dp", axis=1, tiled=True),
        lax.all_gather(cross_query, "dp", axis=0, tiled=True),
        lax.all_gather(cross_key, "dp", axis=0, tiled=True),
        lax.all_gather(cross_value, "dp", axis=0, tiled=True),
        lax.all_gather(cross_out, "dp", axis=1, tiled=True),
        lax.all_gather(gate_weight, "dp", axis=0, tiled=True),
        lax.all_gather(up_weight, "dp", axis=0, tiled=True),
        lax.all_gather(down_weight, "dp", axis=1, tiled=True),
    )
    position = jnp.arange(SLOT, dtype=jnp.int32)
    bucket_ids = jnp.arange(NB, dtype=jnp.int32)
    block = min(512, SLOT)
    dist_onehot = (rel_buckets[:, None] == bucket_ids[None, :]).astype(jnp.bfloat16)
    dist_bias = jnp.dot(dist_onehot, rel_bias, preferred_element_type=jnp.float32).T
    diag_count = SLOT + block - 1

    def self_mask(index, start):
        row_pos = start + jnp.arange(block, dtype=jnp.int32)
        distance = row_pos[:, None] - position[None, :]
        allowed = (distance >= 0) & (position[None, :] < seq_lengths[index])
        extra = jnp.take(dist_bias, jnp.clip(distance, 0, SLOT - 1), axis=1)

        def reducer(d_scores):
            flipped = d_scores[:, :, ::-1]
            padded = jnp.pad(flipped, ((0, 0), (0, 0), (0, block)))
            flat = padded.reshape(heads, block * (SLOT + block))[:, : block * diag_count]
            skewed = flat.reshape(heads, block, diag_count)
            diag_sums = jnp.sum(skewed, axis=1, dtype=jnp.float32)
            diag_dist = jnp.arange(diag_count, dtype=jnp.int32) + start - SLOT + 1
            picked = jnp.take(rel_buckets, jnp.clip(diag_dist, 0, SLOT - 1), axis=0)
            diag_onehot = (
                (picked[:, None] == bucket_ids[None, :]) & (diag_dist[:, None] >= 0)
            ).astype(jnp.float32)
            return jnp.einsum(
                "hc,cb->bh", diag_sums, diag_onehot, preferred_element_type=jnp.float32
            )

        return (extra, allowed, reducer)

    valid_group = (jnp.tile(position, seqs) < jnp.repeat(seq_lengths, SLOT)).astype(jnp.float32)
    valid = lax.dynamic_slice_in_dim(valid_group, lax.axis_index("mp") * local_rows, local_rows)
    stream = decoder_in.astype(jnp.float32)
    first, inverse_one = norm_forward(stream, gains[0], width)
    query = jnp.dot(first, w_query, preferred_element_type=jnp.float32).astype(jnp.bfloat16)
    keys = jnp.dot(first, w_key, preferred_element_type=jnp.float32).astype(jnp.bfloat16)
    values = jnp.dot(first, w_value, preferred_element_type=jnp.float32).astype(jnp.bfloat16)
    mixed, totals_self = attention_forward(query, keys, values, heads, self_mask)
    mixed = mixed.astype(jnp.bfloat16)
    middle = stream + share_rows(jnp.dot(mixed, w_out, preferred_element_type=jnp.float32))
    second, inverse_two = norm_forward(middle, gains[1], width)
    enc_full = full_rows(encoder_out)
    cross_q = jnp.dot(second, c_query, preferred_element_type=jnp.float32).astype(jnp.bfloat16)
    cross_k = jnp.dot(enc_full, c_key, preferred_element_type=jnp.float32).astype(jnp.bfloat16)
    cross_v = jnp.dot(enc_full, c_value, preferred_element_type=jnp.float32).astype(jnp.bfloat16)
    mixed_two, totals_cross = attention_forward(cross_q, cross_k, cross_v, heads, None)
    mixed_two = mixed_two.astype(jnp.bfloat16)
    later = middle + share_rows(jnp.dot(mixed_two, c_out, preferred_element_type=jnp.float32))
    third, inverse_three = norm_forward(later, gains[2], width)
    gate = jnp.dot(third, w_gate, preferred_element_type=jnp.float32)
    upper = jnp.dot(third, w_up, preferred_element_type=jnp.float32)

    def gated(gate_in, up_in):
        return jax.nn.gelu(gate_in, approximate=True) * up_in

    product, gated_back = jax.vjp(gated, gate, upper)
    hidden = product.astype(jnp.bfloat16)
    result = later + share_rows(jnp.dot(hidden, w_down, preferred_element_type=jnp.float32))
    layer_out = result.astype(jnp.bfloat16)
    grad = out_grad.astype(jnp.float32) * valid[:, None]
    grad_full = full_rows(grad.astype(jnp.bfloat16))
    d_hidden = times_transposed(grad_full, w_down)
    g_down = contract_rows(hidden, grad_full)
    d_gate, d_up = gated_back(d_hidden)
    d_gate = d_gate.astype(jnp.bfloat16)
    d_up = d_up.astype(jnp.bfloat16)
    g_gate = contract_rows(third, d_gate)
    g_up = contract_rows(third, d_up)
    d_third = share_rows(times_transposed(d_gate, w_gate) + times_transposed(d_up, w_up))
    back_three, gain_three = norm_backward(later, gains[2], inverse_three, d_third, width)
    grad = grad + back_three
    grad_full = full_rows(grad.astype(jnp.bfloat16))
    d_mixed_two = times_transposed(grad_full, c_out).astype(jnp.bfloat16)
    g_cout = contract_rows(mixed_two, grad_full)
    d_cq, d_ck, d_cv, unused = attention_backward(
        cross_q, cross_k, cross_v, totals_cross, d_mixed_two, heads, None
    )
    d_cq = d_cq.astype(jnp.bfloat16)
    d_ck = d_ck.astype(jnp.bfloat16)
    d_cv = d_cv.astype(jnp.bfloat16)
    g_cq = contract_rows(second, d_cq)
    g_ck = contract_rows(enc_full, d_ck)
    g_cv = contract_rows(enc_full, d_cv)
    encoder_grad = share_rows(times_transposed(d_ck, c_key) + times_transposed(d_cv, c_value))
    d_second = share_rows(times_transposed(d_cq, c_query))
    back_two, gain_two = norm_backward(middle, gains[1], inverse_two, d_second, width)
    grad = grad + back_two
    grad_full = full_rows(grad.astype(jnp.bfloat16))
    d_mixed = times_transposed(grad_full, w_out).astype(jnp.bfloat16)
    g_out = contract_rows(mixed, grad_full)
    d_query, d_keys, d_values, g_bias = attention_backward(
        query, keys, values, totals_self, d_mixed, heads, self_mask
    )
    d_query = d_query.astype(jnp.bfloat16)
    d_keys = d_keys.astype(jnp.bfloat16)
    d_values = d_values.astype(jnp.bfloat16)
    g_query = contract_rows(first, d_query)
    g_key = contract_rows(first, d_keys)
    g_value = contract_rows(first, d_values)
    d_first = share_rows(
        times_transposed(d_query, w_query)
        + times_transposed(d_keys, w_key)
        + times_transposed(d_values, w_value)
    )
    back_one, gain_one = norm_backward(stream, gains[0], inverse_one, d_first, width)
    decoder_grad = grad + back_one
    bias_table = jnp.zeros((NB, heads * lax.axis_size("mp")), jnp.float32)
    bias_table = lax.dynamic_update_slice_in_dim(
        bias_table, g_bias, lax.axis_index("mp") * heads, 1
    )
    gains_grad, bias_grad = lax.psum(
        (jnp.stack([gain_one, gain_two, gain_three]), bias_table), ("dp", "mp")
    )
    weight_parts = (
        lax.psum_scatter(g_query, "dp", scatter_dimension=0, tiled=True),
        lax.psum_scatter(g_key, "dp", scatter_dimension=0, tiled=True),
        lax.psum_scatter(g_value, "dp", scatter_dimension=0, tiled=True),
        lax.psum_scatter(g_out, "dp", scatter_dimension=1, tiled=True),
        lax.psum_scatter(g_cq, "dp", scatter_dimension=0, tiled=True),
        lax.psum_scatter(g_ck, "dp", scatter_dimension=0, tiled=True),
        lax.psum_scatter(g_cv, "dp", scatter_dimension=0, tiled=True),
        lax.psum_scatter(g_cout, "dp", scatter_dimension=1, tiled=True),
        lax.psum_scatter(g_gate, "dp", scatter_dimension=0, tiled=True),
        lax.psum_scatter(g_up, "dp", scatter_dimension=0, tiled=True),
        lax.psum_scatter(g_down, "dp", scatter_dimension=1, tiled=True),
    )
    return (
        layer_out,
        decoder_grad,
        encoder_grad,
        gains_grad,
        bias_grad,
        weight_parts[0],
        weight_parts[1],
        weight_parts[2],
        weight_parts[3],
        weight_parts[4],
        weight_parts[5],
        weight_parts[6],
        weight_parts[7],
        weight_parts[8],
        weight_parts[9],
        weight_parts[10],
    )


def solution(mesh):
    return jax.shard_map(
        per_device,
        mesh=mesh,
        in_specs=(
            P(("dp", "mp"), None),
            P(("dp", "mp"), None),
            P("dp"),
            P(),
            P(),
            P(None, "mp"),
            P("dp", "mp"),
            P("dp", "mp"),
            P("dp", "mp"),
            P("mp", "dp"),
            P("dp", "mp"),
            P("dp", "mp"),
            P("dp", "mp"),
            P("mp", "dp"),
            P("dp", "mp"),
            P("dp", "mp"),
            P("mp", "dp"),
            P(("dp", "mp"), None),
        ),
        out_specs=(
            P(("dp", "mp"), None),
            P(("dp", "mp"), None),
            P(("dp", "mp"), None),
            P(),
            P(),
            P("dp", "mp"),
            P("dp", "mp"),
            P("dp", "mp"),
            P("mp", "dp"),
            P("dp", "mp"),
            P("dp", "mp"),
            P("dp", "mp"),
            P("mp", "dp"),
            P("dp", "mp"),
            P("dp", "mp"),
            P("mp", "dp"),
        ),
        check_vma=False,
    )
```

profile of v0, /device:TPU:1, one launch (start us, length us, event | category | flops | bytes accessed | tf_op | source)
XLA Modules:
  0.0 4727.7 jit_solution(15189394785793770615)
XLA Ops:
  16.8 1719.3 %gather_fusion.1 = f32[524288,3]{1,0:T(8,128)} fusion(f32[3,1024]{0,1:T(8,128)S(1)} %copy.62, s32[524288]{0:T(1024)S(1)} %broadcast_clamp_fusion), kind=kCustom, calls=%fused_computation.2.clone | custom fusion | bytes 14680064 | tf_op jit(solution)/shard_map/jit(_take)/gather | solution.py:173
  1736.1 140.2 %copy.87 = f32[512,1024,3]{1,0,2:T(8,128)} copy(f32[512,1024,3]{2,1,0:T(8,128)} %bitcast.15) | data formatting | bytes 12582912 | tf_op jit(solution)/shard_map/jit(_take)/gather | solution.py:173
  1876.3 1719.3 %gather_fusion = f32[524288,3]{1,0:T(8,128)} fusion(f32[3,1024]{0,1:T(8,128)S(1)} %copy.62, s32[524288]{0:T(1024)S(1)} %copy-done.22), kind=kCustom, calls=%fused_computation.clone | custom fusion | bytes 14680064 | tf_op jit(solution)/shard_map/jit(_take)/gather | solution.py:173
  3595.6 140.1 %copy.86 = f32[512,1024,3]{1,0,2:T(8,128)} copy(f32[512,1024,3]{2,1,0:T(8,128)} %bitcast.6) | data formatting | bytes 12582912 | tf_op jit(solution)/shard_map/jit(_take)/gather | solution.py:173
  3735.8 10.9 all_gather.56
  3746.7 9.6 all_gather.55
  3756.3 8.6 all_gather.57
  3764.9 9.7 all_gather.58
  3774.9 2.4 fusion.24
  3780.7 5.2 fusion.100
  3796.8 35.0 reduce-scatter.27.cloned.1.call-done
  3835.2 10.2 all_gather.60
  3845.4 9.6 all_gather.62
  3855.0 8.6 all_gather.63
  3863.6 10.5 all_gather.64
  3874.1 16.6 all_gather.61
  3902.6 34.6 reduce-scatter.29.cloned.1.call-done
  3944.5 13.0 all_gather.66
  3957.5 11.8 all_gather.67
  3969.3 12.2 all_gather.68
  3981.5 4.1 fusion.104
  3987.8 28.3 all-gather.13.cloned.1.call-done
  4016.1 6.4 multiply_convert_fusion.4
  4026.5 34.2 reduce-scatter.33.cloned.1.call-done
  4064.2 2.5 fusion.93
  4066.8 36.2 all-gather.15.cloned.1.call-done
  4115.0 3.7 convolution_convert_fusion
  4118.9 30.3 reduce-scatter.35.cloned.1.call-done
  4152.5 33.2 reduce-scatter.31.cloned.1.call-done
  4185.7 3.4 fusion.94
  4195.2 3.5 fusion.65
  4203.8 21.5 all-gather.17.cloned.1.call-done
  4227.5 3.9 multiply_reduce_fusion.1
  4242.1 2.8 fusion.115
  4253.9 4.1 fusion.26
  4260.7 3.9 fusion.113
  4264.7 3.9 fusion.112
  4269.0 4.0 fusion.114
  4273.1 3.0 fusion.75
  4276.8 6.0 gather_fusion.2
  4282.8 2.4 convolution_bitcast_fusion.2
  4288.1 9.4 gather_fusion.3
  4299.2 2.4 convolution_bitcast_fusion.3
  4307.9 47.4 %rev.6 = bf16[3,512,1024]{2,1,0:T(8,128)(2,1)} reverse(bf16[3,512,1024]{2,1,0:T(8,128)(2,1)} %copy-done.9), dimensions={2} | reverse | bytes 6291456 | tf_op jit(solution)/shard_map/rev | solution.py:176
  4355.4 2.4 pad_bitcast_fusion.1
  4357.7 6.6 copy.98
  4364.3 2.5 fusion.73
  4366.9 8.6 slice_convert_fusion.1
  4375.6 33.9 rev.7
  4409.4 2.3 pad_bitcast_fusion
  4411.8 6.7 copy.99
  4420.2 8.5 slice_convert_fusion
  4428.8 13.2 reshape.393
  4442.0 15.8 reshape.330
  4457.8 13.6 reshape.395
  4471.5 15.7 reshape.331
  4487.2 4.3 reduce_sum.188
  4491.5 4.3 reduce_sum.189
  4501.7 39.6 all-reduce.2
  4543.5 22.3 reduce-scatter.59.cloned.1.call-done
  4565.8 38.8 reduce-scatter.57.cloned.1.call-done
  4604.5 38.7 reduce-scatter.41.cloned.1.call-done
  4643.3 38.7 reduce-scatter.45.cloned.1.call-done
  4682.0 38.6 reduce-scatter.43.cloned.1.call-done
  (428 shorter events, 127.9 us)
Async XLA Ops:
  7.2 9.1 copy-start
  7.2 3770.1 %all-gather.7.cloned.1.call-start = ((), (), s32[]{:S(2)}) async-start(), calls=%async_computation.18 | async-start | bytes 1966080 | tf_op jit(solution)/shard_map/all_gather | solution.py:15
  11.7 3820.1 %reduce-scatter.27.cloned.1.call-start = ((), (), s32[]{:S(2)}) async-start(), calls=%async_computation.19 | async-start | bytes 1966080 | tf_op jit(solution)/shard_map/reduce_scatter | solution.py:19
  1736.1 140.2 %copy-start.22 = (s32[524288]{0:T(1024)S(1)}, s32[524288]{0:T(1024)}, u32[]{:S(2)}) copy-start(s32[524288]{0:T(1024)} %broadcast_clamp_fusion.1) | copy-start | bytes 6291460
  3595.5 140.1 %copy-start.96 = (bf16[192,96]{1,0:T(8,128)(2,1)S(1)}, bf16[192,96]{1,0:T(8,128)(2,1)}, u32[]{:S(2)}) copy-start(bf16[192,96]{1,0:T(8,128)(2,1)} %param.31) | copy-start | bytes 110596
  3595.5 140.2 %copy-start.90 = (bf16[96,192]{1,0:T(8,128)(2,1)S(1)}, bf16[96,192]{1,0:T(8,128)(2,1)}, u32[]{:S(2)}) copy-start(bf16[96,192]{1,0:T(8,128)(2,1)} %param.29) | copy-start | bytes 110596
  3595.6 151.2 %copy-start.91 = (bf16[96,192]{1,0:T(8,128)(2,1)S(1)}, bf16[96,192]{1,0:T(8,128)(2,1)}, u32[]{:S(2)}) copy-start(bf16[96,192]{1,0:T(8,128)(2,1)} %param.28) | copy-start | bytes 110596
  3595.6 160.7 %copy-start.92 = (bf16[96,192]{1,0:T(8,128)(2,1)S(1)}, bf16[96,192]{1,0:T(8,128)(2,1)}, u32[]{:S(2)}) copy-start(bf16[96,192]{1,0:T(8,128)(2,1)} %param.30) | copy-start | bytes 110596
  3735.7 39.2 copy-start.101
  3746.7 32.8 copy-start.45
  3756.3 23.2 copy-start.44
  3764.9 26.1 copy-start.34
  3774.6 19.6 copy-start.36
  3779.6 7.8 copy-start.54
  3780.3 7.1 copy-start.18
  3780.3 7.1 slice-start.6
  3780.7 6.7 slice-start.7
  3794.2 37.5 copy-start.8
  3794.9 38.1 copy-start.89
  3796.7 38.4 copy-start.97
  3796.7 38.5 copy-start.93
  3796.7 48.7 %copy-start.94 = (bf16[96,192]{1,0:T(8,128)(2,1)S(1)}, bf16[96,192]{1,0:T(8,128)(2,1)}, u32[]{:S(2)}) copy-start(bf16[96,192]{1,0:T(8,128)(2,1)} %param.33) | copy-start | bytes 110596
  3796.7 58.3 %copy-start.95 = (bf16[96,192]{1,0:T(8,128)(2,1)S(1)}, bf16[96,192]{1,0:T(8,128)(2,1)}, u32[]{:S(2)}) copy-start(bf16[96,192]{1,0:T(8,128)(2,1)} %param.34) | copy-start | bytes 110596
  3796.7 77.4 %copy-start.85 = (bf16[128,768]{1,0:T(8,128)(2,1)S(1)}, bf16[128,768]{1,0:T(8,128)(2,1)}, u32[]{:S(2)}) copy-start(bf16[128,768]{1,0:T(8,128)(2,1)} %param.23) | copy-start | bytes 589828
  3796.7 96.0 %all-gather.9.cloned.1.call-start = ((), (), s32[]{:S(2)}) async-start(), calls=%async_computation.20 | async-start | bytes 1966080 | tf_op jit(solution)/shard_map/all_gather | solution.py:15
  3833.0 57.7 %copy-start.107 = (f32[256]{0:T(256)}, f32[256]{0:T(256)S(1)}, u32[]{:S(2)}) copy-start(f32[256]{0:T(256)S(1)} %add_rsqrt_fusion.1) | copy-start | bytes 3076
  3835.0 102.3 %reduce-scatter.29.cloned.1.call-start = ((), (), s32[]{:S(2)}) async-start(), calls=%async_computation.21 | async-start | bytes 1966080 | tf_op jit(solution)/shard_map/reduce_scatter | solution.py:19
  3845.4 47.3 %copy-start.38 = (bf16[768,192]{1,0:T(8,128)(2,1)}, bf16[768,192]{1,0:T(8,128)(2,1)S(1)}, u32[]{:S(2)}) copy-start(bf16[768,192]{1,0:T(8,128)(2,1)S(1)} %all_gather.60) | copy-start | bytes 884740
  3855.0 35.8 copy-start.43
  3863.6 27.6 copy-start.41
  3900.8 39.0 copy-start.86
  3902.6 78.9 %all-gather.11.cloned.1.call-start = ((), (), s32[]{:S(2)}) async-start(), calls=%async_computation.22 | async-start | bytes 1966080 | tf_op jit(solution)/shard_map/all_gather | solution.py:15
  3941.9 74.3 %all-gather.13.cloned.1.call-start = ((), (), s32[]{:S(2)}) async-start(), calls=%async_computation.24 | async-start | bytes 1966080 | tf_op jit(solution)/shard_map/all_gather | solution.py:15
  3944.5 116.2 %reduce-scatter.33.cloned.1.call-start = ((), (), s32[]{:S(2)}) async-start(), calls=%async_computation.25 | async-start | bytes 1966080 | tf_op jit(solution)/shard_map/reduce_scatter | solution.py:19
  4026.5 76.5 %all-gather.15.cloned.1.call-start = ((), (), s32[]{:S(2)}) async-start(), calls=%async_computation.26 | async-start | bytes 1966080 | tf_op jit(solution)/shard_map/all_gather | solution.py:15
  4066.7 82.5 %reduce-scatter.35.cloned.1.call-start = ((), (), s32[]{:S(2)}) async-start(), calls=%async_computation.27 | async-start | bytes 1966080 | tf_op jit(solution)/shard_map/reduce_scatter | solution.py:19
  4114.9 70.7 %reduce-scatter.31.cloned.1.call-start = ((), (), s32[]{:S(2)}) async-start(), calls=%async_computation.23 | async-start | bytes 1966080 | tf_op jit(solution)/shard_map/reduce_scatter | solution.py:19
  4118.7 106.6 %all-gather.17.cloned.1.call-start = ((), (), s32[]{:S(2)}) async-start(), calls=%async_computation.28 | async-start | bytes 1966080 | tf_op jit(solution)/shard_map/all_gather | solution.py:15
  4189.1 115.5 %reduce-scatter.61.cloned.1.call-start = ((), (), s32[]{:S(2)}) async-start(), calls=%async_computation.41 | async-start | bytes 884736
  4198.7 107.5 %reduce-scatter.39.cloned.1.call-start = ((), (), s32[]{:S(2)}) async-start(), calls=%async_computation.30 | async-start | bytes 983040 | tf_op jit(solution)/shard_map/reduce_scatter | solution.py:19
  4201.7 23.6 copy-start.37
  4203.8 23.7 copy-start.21
  4203.8 23.8 copy-start.79
  4203.8 295.0 %reduce-scatter.55.cloned.1.call-start = ((), (), s32[]{:S(2)}) async-start(), calls=%async_computation.38 | async-start | bytes 884736
  4227.5 8.0 copy-start.69
  4242.1 7.6 slice-start.4
  4251.9 248.5 %reduce-scatter.37.cloned.1.call-start = ((), (), s32[]{:S(2)}) async-start(), calls=%async_computation.29 | async-start | bytes 1966080 | tf_op jit(solution)/shard_map/reduce_scatter | solution.py:19
  4260.6 282.9 %reduce-scatter.51.cloned.1.call-start = ((), (), s32[]{:S(2)}) async-start(), calls=%async_computation.36 | async-start | bytes 1769472 | tf_op jit(solution)/shard_map/reduce_scatter | solution.py:285
  4264.6 278.9 %reduce-scatter.49.cloned.1.call-start = ((), (), s32[]{:S(2)}) async-start(), calls=%async_computation.35 | async-start | bytes 1769472 | tf_op jit(solution)/shard_map/reduce_scatter | solution.py:284
  4268.6 274.9 %reduce-scatter.53.cloned.1.call-start = ((), (), s32[]{:S(2)}) async-start(), calls=%async_computation.37 | async-start | bytes 1769472 | tf_op jit(solution)/shard_map/reduce_scatter | solution.py:286
  4273.0 270.5 %reduce-scatter.47.cloned.1.call-start = ((), (), s32[]{:S(2)}) async-start(), calls=%async_computation.34 | async-start | bytes 884736 | tf_op jit(solution)/shard_map/reduce_scatter | solution.py:280
  4276.1 289.7 %reduce-scatter.59.cloned.1.call-start = ((), (), s32[]{:S(2)}) async-start(), calls=%async_computation.40 | async-start | bytes 884736
  4287.4 317.1 %reduce-scatter.57.cloned.1.call-start = ((), (), s32[]{:S(2)}) async-start(), calls=%async_computation.39 | async-start | bytes 884736
  4297.4 7.1 copy-start.104
  4299.2 8.7 copy-start.105
  4303.9 339.4 %reduce-scatter.41.cloned.1.call-start = ((), (), s32[]{:S(2)}) async-start(), calls=%async_computation.31 | async-start | bytes 884736 | tf_op jit(solution)/shard_map/reduce_scatter | solution.py:276
  4357.7 6.6 copy-start.11
  4366.9 315.1 %reduce-scatter.45.cloned.1.call-start = ((), (), s32[]{:S(2)}) async-start(), calls=%async_computation.33 | async-start | bytes 884736 | tf_op jit(solution)/shard_map/reduce_scatter | solution.py:278
  4411.8 6.7 copy-start.12
  4411.8 6.7 copy-start.33
  4420.0 300.6 %reduce-scatter.43.cloned.1.call-start = ((), (), s32[]{:S(2)}) async-start(), calls=%async_computation.32 | async-start | bytes 884736 | tf_op jit(solution)/shard_map/reduce_scatter | solution.py:277
  4495.8 45.5 copy-start.109
  4495.9 45.5 copy-start.51
  4497.4 223.2 %copy-start.1 = (bf16[32,3]{0,1:T(4,128)(2,1)S(1)}, bf16[32,3]{0,1:T(4,128)(2,1)}, u32[]{:S(2)}) copy-start(bf16[32,3]{0,1:T(4,128)(2,1)} %param.27) | copy-start | bytes 580
  (86 other events, 207.4 us)
Sparse Core Ops, SparseCore 0:
  11.8 39.0 all-gather.6
  3796.8 34.8 reduce-scatter.26
  3835.1 36.1 all-gather.8
  3902.7 34.4 reduce-scatter.28
  3942.0 36.1 all-gather.10
  3980.1 35.9 all-gather.12
  4026.6 34.1 reduce-scatter.32
  4066.8 36.0 all-gather.14
  4115.1 34.0 reduce-scatter.34
  4151.4 34.2 reduce-scatter.30
  4189.2 36.0 all-gather.16
  4228.3 33.6 reduce-scatter.60
  4264.4 22.2 reduce-scatter.38
  4289.7 35.2 reduce-scatter.54
  4327.1 35.4 reduce-scatter.36
  4366.3 37.8 reduce-scatter.50
  4407.9 38.4 reduce-scatter.48
  4450.1 38.4 reduce-scatter.52
  4492.3 34.8 reduce-scatter.46
  4530.7 34.9 reduce-scatter.58
  4569.5 34.9 reduce-scatter.56
  4608.2 34.9 reduce-scatter.40
  4647.0 34.9 reduce-scatter.44
  4685.6 34.9 reduce-scatter.42
where the time goes:
time: 4750 us; the launch traced here: 4730 us
  local copies, waits for them, and re-layouts  3910 us (82%)
  waiting for transfers between devices  431 us (9%)
  blocking collectives  171 us (4%)
  matrix products  120 us (3%)
  other arithmetic  72.5 us (2%)
    gather x4, local copies, waits for them, and re-layouts, self_mask(): extra = jnp.take(dist_bias, jnp.clip(distance, 0, SLOT - 1), axis=1)  3720 us
    reduce_scatter x7, waiting for transfers between devices, share_rows(): lax.psum_scatter(total.astype(jnp.bfloat16), 'mp', scatter_dimension=0, t...  167 us
  transfers between devices with their start and end apart: 24, of which 13 were waited for; matrix products, arithmetic and copies ran while one was open for 85% of the time, Pallas kernels for 0%

commit v1 on v0

v1 whole, which is shorter than its diff:
```python
import functools

import jax
import jax.numpy as jnp
from jax import lax
from jax.experimental import pallas as pl
from jax.experimental.pallas import tpu as pltpu
from jax.sharding import PartitionSpec as P

NB = 32
EPS = 1e-06

F32=jnp.float32; BF16=jnp.bfloat16
NEG=-1e30
NN=(((1,),(0,)),((),())); NT=(((1,),(1,)),((),())); TN=(((0,),(0,)),((),()))
def mm(a,b,dims=NN): return lax.dot_general(a,b,dims,preferred_element_type=F32)
TILE=256

def rows_of(i): return pl.ds(pl.multiple_of(i*TILE,TILE),TILE)

def split_heads(src, dst, heads):
    hd=dst.shape[2]
    for h in range(heads): dst[h]=src[:, h*hd:(h+1)*hd]

def bias_tiles(vecs, tiles, heads):
    key=lax.broadcasted_iota(jnp.int32,(TILE,TILE),0); qry=lax.broadcasted_iota(jnp.int32,(TILE,TILE),1)
    for h in range(heads):
        for d in range(3):
            wide=jnp.broadcast_to(vecs[h*3+d:h*3+d+1,:],(TILE,2*TILE))
            t=pltpu.roll(wide,0,1,stride=1,stride_axis=0)[:,:TILE]
            if d==0: t=jnp.where(qry>=key,t,NEG)
            tiles[h,d]=t

def fwd_attention(q3,k3,v3,vt3,out_t,lse,heads,nq,nk,tiles,kmask):
    hd=q3.shape[2]
    causal=tiles is not None
    def qblock(I,_):
        ri=rows_of(I)
        def kblock(J,carry):
            rj=rows_of(J)
            new=[]
            for h in range(heads):
                m,l,acc=carry[h]
                s=mm(k3[h,rj,:],q3[h,ri,:],NT)
                if causal:
                    s=s+tiles[h,jnp.minimum(I-J,2)]+kmask[rj,:1]
                m2=jnp.maximum(m,jnp.max(s,axis=0,keepdims=True))
                a=jnp.exp(m-m2); p=jnp.exp(s-m2)
                l2=l*a+jnp.sum(p,axis=0,keepdims=True)
                acc2=acc*a+mm(vt3[h,:,rj],p.astype(BF16))
                new.append((m2,l2,acc2))
            return tuple(new)
        init=tuple((jnp.full((1,TILE),NEG,F32),jnp.zeros((1,TILE),F32),jnp.zeros((hd,TILE),F32)) for _ in range(heads))
        res=lax.fori_loop(0,(I+1) if causal else nk//TILE,kblock,init)
        for h in range(heads):
            m,l,acc=res[h]
            out_t[h*hd:(h+1)*hd,ri]=acc/l
            lse[h:h+1,ri]=m+jnp.log(l)
        return 0
    lax.fori_loop(0,nq//TILE,qblock,0)

def bwd_attention(q3,k3,v3,kt3,do3,lse,delta,dqt,dk,dv,heads,nq,nk,tiles,kmask,dtile):
    hd=q3.shape[2]
    causal=tiles is not None
    dqt[...]=jnp.zeros_like(dqt)
    dk[...]=jnp.zeros_like(dk); dv[...]=jnp.zeros_like(dv)
    if causal: dtile[...]=jnp.zeros_like(dtile)
    def kblock(J,_):
        rj=rows_of(J)
        def qblock(I,_):
            ri=rows_of(I)
            for h in range(heads):
                s=mm(k3[h,rj,:],q3[h,ri,:],NT)
                if causal:
                    d=jnp.minimum(I-J,2)
                    s=s+tiles[h,d]+kmask[rj,:1]
                p=jnp.exp(s-lse[h:h+1,ri])
                dp=mm(v3[h,rj,:],do3[h,ri,:],NT)
                ds=(p*(dp-delta[h:h+1,ri])).astype(BF16)
                dv[h,rj,:]+=mm(p.astype(BF16),do3[h,ri,:])
                dk[h,rj,:]+=mm(ds,q3[h,ri,:])
                dqt[h*hd:(h+1)*hd,ri]+=mm(kt3[h,:,rj],ds)
                if causal: dtile[h,d]+=ds.astype(F32)
            return 0
        lax.fori_loop(J if causal else 0,nq//TILE,qblock,0)
        return 0
    lax.fori_loop(0,nk//TILE,kblock,0)

def bias_diag(dtile,out,heads):
    r=lax.broadcasted_iota(jnp.int32,(TILE,TILE),0); c=lax.broadcasted_iota(jnp.int32,(TILE,TILE),1)
    flip=(r+c==TILE-1).astype(F32)
    z=jnp.zeros((TILE,TILE),F32)
    for h in range(heads):
        for d in range(3):
            rev=lax.dot_general(flip,dtile[h,d],NN,precision=lax.Precision.HIGHEST,preferred_element_type=F32)
            t=pltpu.roll(jnp.concatenate([rev,z],axis=1),0,1,stride=1,stride_axis=0)
            out[h*3+d:h*3+d+1,:]=jnp.sum(t,axis=0,keepdims=True)

def fwd_kernel(heads,nq,nk,causal,*refs):
    if causal:
        length,vecs,q,k,v,out,out_t,lse,q3,k3,v3,vt3,tiles,kmask=refs
    else:
        q,k,v,out,out_t,lse,q3,k3,v3,vt3=refs; tiles=kmask=None
    hd=q3.shape[2]
    split_heads(q,q3,heads);split_heads(k,k3,heads);split_heads(v,v3,heads)
    for h in range(heads): vt3[h]=v3[h].T
    if causal:
        bias_tiles(vecs,tiles,heads)
        kmask[...]=jnp.where(lax.broadcasted_iota(jnp.int32,kmask.shape,0)<length[0],0.0,NEG)
    fwd_attention(q3,k3,v3,vt3,out_t,lse,heads,nq,nk,tiles,kmask)
    out[...]=out_t[...].T.astype(BF16)

def bwd_kernel(heads,nq,nk,causal,*refs):
    if causal:
        length,vecs,q,k,v,do,out_t,lse,dq,dk,dv,dvec,q3,k3,v3,kt3,do3,delta,dqt,dk3,dv3,tiles,kmask,dtile=refs
    else:
        q,k,v,do,out_t,lse,dq,dk,dv,q3,k3,v3,kt3,do3,delta,dqt,dk3,dv3=refs; tiles=kmask=dtile=None
    hd=q3.shape[2]
    for s,d in ((q,q3),(k,k3),(v,v3),(do,do3)): split_heads(s,d,heads)
    for h in range(heads): kt3[h]=k3[h].T
    dot=do[...].astype(F32).T
    for h in range(heads):
        delta[h:h+1,:]=jnp.sum(dot[h*hd:(h+1)*hd,:]*out_t[h*hd:(h+1)*hd,:],axis=0,keepdims=True)
    if causal:
        bias_tiles(vecs,tiles,heads)
        kmask[...]=jnp.where(lax.broadcasted_iota(jnp.int32,kmask.shape,0)<length[0],0.0,NEG)
    bwd_attention(q3,k3,v3,kt3,do3,lse,delta,dqt,dk3,dv3,heads,nq,nk,tiles,kmask,dtile)
    dq[...]=dqt[...].T.astype(BF16)
    for h in range(heads):
        dk[:,h*hd:(h+1)*hd]=dk3[h].astype(BF16); dv[:,h*hd:(h+1)*hd]=dv3[h].astype(BF16)
    if causal: bias_diag(dtile,dvec,heads)

V=pl.BlockSpec(memory_space=pltpu.VMEM); S=pl.BlockSpec(memory_space=pltpu.SMEM)
def attention_forward(q,k,v,heads,length=None,vecs=None):
    nq,w=q.shape; nk=k.shape[0]; hd=w//heads; causal=length is not None
    sc=[pltpu.VMEM((heads,nq,hd),BF16)]+[pltpu.VMEM((heads,nk,hd),BF16)]*2+[pltpu.VMEM((heads,hd,nk),BF16)]
    if causal: sc+=[pltpu.VMEM((heads,3,TILE,TILE),F32),pltpu.VMEM((nk,128),F32)]
    outs=[jax.ShapeDtypeStruct((nq,w),BF16),jax.ShapeDtypeStruct((w,nq),F32),jax.ShapeDtypeStruct((heads,nq),F32)]
    args=([length,vecs] if causal else [])+[q,k,v]
    return pl.pallas_call(functools.partial(fwd_kernel,heads,nq,nk,causal),out_shape=outs,
        in_specs=([S,V] if causal else [])+[V]*3,out_specs=[V]*3,scratch_shapes=sc,name="attn_fwd")(*args)
def attention_backward(q,k,v,do,out_t,lse,heads,length=None,vecs=None):
    nq,w=q.shape; nk=k.shape[0]; hd=w//heads; causal=length is not None
    sc=[pltpu.VMEM((heads,nq,hd),BF16)]+[pltpu.VMEM((heads,nk,hd),BF16)]*2+[pltpu.VMEM((heads,hd,nk),BF16),pltpu.VMEM((heads,nq,hd),BF16),
        pltpu.VMEM((heads,nq),F32),pltpu.VMEM((w,nq),F32),pltpu.VMEM((heads,nk,hd),F32),pltpu.VMEM((heads,nk,hd),F32)]
    if causal: sc+=[pltpu.VMEM((heads,3,TILE,TILE),F32),pltpu.VMEM((nk,128),F32),pltpu.VMEM((heads,3,TILE,TILE),F32)]
    outs=[jax.ShapeDtypeStruct((nq,w),BF16),jax.ShapeDtypeStruct((nk,w),BF16),jax.ShapeDtypeStruct((nk,w),BF16)]
    if causal: outs.append(jax.ShapeDtypeStruct((heads*3,2*TILE),F32))
    args=([length,vecs] if causal else [])+[q,k,v,do,out_t,lse]
    return pl.pallas_call(functools.partial(bwd_kernel,heads,nq,nk,causal),out_shape=outs,
        in_specs=([S,V] if causal else [])+[V]*6,out_specs=[V]*len(outs),scratch_shapes=sc,name="attn_bwd")(*args)
def bias_vectors(t):
    h=t.shape[0]; far=t[:,TILE:TILE+1]
    z=jnp.broadcast_to(far,(h,TILE))
    v0=jnp.concatenate([t[:,:TILE],z],1)
    v1=jnp.concatenate([t[:,TILE:2*TILE],t[:,:TILE]],1)
    v2=jnp.concatenate([z,z],1)
    return jnp.stack([v0,v1,v2],1).reshape(h*3,2*TILE)


def full_rows(share):
    return lax.all_gather(share, "mp", axis=0, tiled=True)


def share_rows(total):
    return lax.psum_scatter(total.astype(BF16), "mp", scatter_dimension=0, tiled=True).astype(F32)


def norm_forward(stream, gain, width):
    inverse = lax.rsqrt(jnp.sum(stream * stream, axis=1) / width + EPS)
    return (stream * inverse[:, None] * gain[None, :]).astype(BF16), inverse


def norm_backward(stream, gain, inverse, upstream, width):
    scaled = upstream * gain[None, :]
    dotted = jnp.sum(scaled * stream, axis=1)
    back = inverse[:, None] * scaled - stream * (inverse * inverse * inverse * dotted / width)[:, None]
    return back, jnp.sum(upstream * stream * inverse[:, None], axis=0)


def distance_bias(rel_buckets, rel_bias):
    onehot = (rel_buckets[:, None] == jnp.arange(NB, dtype=jnp.int32)[None, :]).astype(BF16)
    return jnp.dot(onehot, rel_bias, preferred_element_type=F32).T


def bucket_sums(diag, rel_buckets, heads):
    d3 = diag.reshape(heads, 3, 2 * TILE)
    n = rel_buckets.shape[0]
    near = jnp.pad(d3[:, 0, TILE - 1 : 2 * TILE - 1], ((0, 0), (0, n - TILE)))
    next_one = jnp.pad(d3[:, 1, : 2 * TILE - 1], ((0, 0), (1, n - 2 * TILE)))
    by_distance = near + next_one
    far = jnp.sum(d3[:, 2], axis=1)
    onehot = (rel_buckets[:, None] == jnp.arange(NB, dtype=jnp.int32)[None, :]).astype(F32)
    total = jnp.einsum("hn,nb->bh", by_distance, onehot, precision=lax.Precision.HIGHEST)
    last = (jnp.arange(NB, dtype=jnp.int32)[:, None] == rel_buckets[n - 1]).astype(F32)
    return total + last * far[None, :]


def per_device(
    decoder_in, encoder_out, seq_lengths, rel_buckets, norm_gains, rel_bias,
    self_query, self_key, self_value, self_out, cross_query, cross_key, cross_value, cross_out,
    gate_weight, up_weight, down_weight, out_grad,
):
    width = decoder_in.shape[1]
    local_rows = decoder_in.shape[0]
    heads = rel_bias.shape[1]
    gains = norm_gains.astype(F32)
    w = self_query.shape[1]
    f = gate_weight.shape[1]
    part_self = jnp.concatenate([self_query, self_key, self_value, self_out.T], axis=1)
    part_cross = jnp.concatenate([cross_query, cross_key, cross_value, cross_out.T], axis=1)
    part_ff = jnp.concatenate([gate_weight, up_weight, down_weight.T], axis=1)
    full_self = lax.all_gather(part_self, "dp", axis=0, tiled=True)
    full_rest = lax.all_gather(jnp.concatenate([part_cross, part_ff], axis=1), "dp", axis=0, tiled=True)
    w_qkv, w_out = full_self[:, : 3 * w], full_self[:, 3 * w :]
    c_query, c_kv, c_out = full_rest[:, :w], full_rest[:, w : 3 * w], full_rest[:, 3 * w : 4 * w]
    w_gate, w_up, w_down = full_rest[:, 4 * w : 4 * w + f], full_rest[:, 4 * w + f : 4 * w + 2 * f], full_rest[:, 4 * w + 2 * f :]
    vecs = bias_vectors(distance_bias(rel_buckets, rel_bias))
    slot = rel_buckets.shape[0]
    position = lax.axis_index("mp") * local_rows + jnp.arange(local_rows, dtype=jnp.int32)
    valid = (position < seq_lengths[0]).astype(F32)[:, None]

    def dot(a, b, dims=NN):
        return lax.dot_general(a, b, dims, preferred_element_type=F32)

    stream = decoder_in.astype(F32)
    grad = out_grad.astype(F32) * valid
    grad_one = full_rows(grad.astype(BF16))
    enc_full = full_rows(encoder_out)
    first, inverse_one = norm_forward(stream, gains[0], width)
    first = full_rows(first)
    qkv = dot(first, w_qkv).astype(BF16)
    query, keys, values = qkv[:, :w], qkv[:, w : 2 * w], qkv[:, 2 * w :]
    mixed, mixed_t, lse = attention_forward(query, keys, values, heads, seq_lengths, vecs)
    middle = stream + share_rows(dot(mixed, w_out, NT))
    second, inverse_two = norm_forward(middle, gains[1], width)
    second = full_rows(second)
    cross_q = dot(second, c_query).astype(BF16)
    cross_kv = dot(enc_full, c_kv).astype(BF16)
    cross_k, cross_v = cross_kv[:, :w], cross_kv[:, w:]
    mixed_two, mixed_two_t, lse_two = attention_forward(cross_q, cross_k, cross_v, heads)
    later = middle + share_rows(dot(mixed_two, c_out, NT))
    third, inverse_three = norm_forward(later, gains[2], width)
    third = full_rows(third)
    gate = dot(third, w_gate)
    upper = dot(third, w_up)

    def gated(gate_in, up_in):
        return jax.nn.gelu(gate_in, approximate=True) * up_in

    product, gated_back = jax.vjp(gated, gate, upper)
    hidden = product.astype(BF16)
    layer_out = (later + share_rows(dot(hidden, w_down, NT))).astype(BF16)
    d_gate, d_up = gated_back(dot(grad_one, w_down))
    d_gate, d_up = d_gate.astype(BF16), d_up.astype(BF16)
    g_down = dot(grad_one, hidden, TN)
    g_gate = dot(third, d_gate, TN)
    g_up = dot(third, d_up, TN)
    d_third = share_rows(dot(d_gate, w_gate, NT) + dot(d_up, w_up, NT))
    back_three, gain_three = norm_backward(later, gains[2], inverse_three, d_third, width)
    grad = grad + back_three
    grad_two = full_rows(grad.astype(BF16))
    d_mixed_two = dot(grad_two, c_out).astype(BF16)
    g_cout = dot(grad_two, mixed_two, TN)
    d_cq, d_ck, d_cv = attention_backward(cross_q, cross_k, cross_v, d_mixed_two, mixed_two_t, lse_two, heads)
    d_second = share_rows(dot(d_cq, c_query, NT))
    d_ckv = jnp.concatenate([d_ck, d_cv], axis=1)
    encoder_grad = share_rows(dot(d_ckv, c_kv, NT))
    g_cq = dot(second, d_cq, TN)
    g_ckv = dot(enc_full, d_ckv, TN)
    rest = jnp.concatenate([g.astype(BF16) for g in (g_cq, g_ckv, g_cout, g_gate, g_up, g_down)], axis=1)
    rest = lax.psum_scatter(rest, "dp", scatter_dimension=0, tiled=True)
    back_two, gain_two = norm_backward(middle, gains[1], inverse_two, d_second, width)
    grad = grad + back_two
    grad_three = full_rows(grad.astype(BF16))
    d_mixed = dot(grad_three, w_out).astype(BF16)
    g_out = dot(grad_three, mixed, TN)
    d_query, d_keys, d_values, diag = attention_backward(
        query, keys, values, d_mixed, mixed_t, lse, heads, seq_lengths, vecs
    )
    d_qkv = jnp.concatenate([d_query, d_keys, d_values], axis=1)
    d_first = share_rows(dot(d_qkv, w_qkv, NT))
    g_qkv = dot(first, d_qkv, TN)
    own = jnp.concatenate([g_qkv.astype(BF16), g_out.astype(BF16)], axis=1)
    own = lax.psum_scatter(own, "dp", scatter_dimension=0, tiled=True)
    back_one, gain_one = norm_backward(stream, gains[0], inverse_one, d_first, width)
    decoder_grad = grad + back_one
    bias_table = jnp.zeros((NB, heads * lax.axis_size("mp")), F32)
    bias_table = lax.dynamic_update_slice_in_dim(
        bias_table, bucket_sums(diag, rel_buckets, heads), lax.axis_index("mp") * heads, 1
    )
    gains_grad, bias_grad = lax.psum((jnp.stack([gain_one, gain_two, gain_three]), bias_table), ("dp", "mp"))
    own = own.astype(F32)
    rest = rest.astype(F32)
    return (
        layer_out, decoder_grad, encoder_grad, gains_grad, bias_grad,
        own[:, :w], own[:, w : 2 * w], own[:, 2 * w : 3 * w], own[:, 3 * w :].T,
        rest[:, :w], rest[:, w : 2 * w], rest[:, 2 * w : 3 * w], rest[:, 3 * w : 4 * w].T,
        rest[:, 4 * w : 4 * w + f], rest[:, 4 * w + f : 4 * w + 2 * f], rest[:, 4 * w + 2 * f :].T,
    )


def solution(mesh):
    return jax.shard_map(
        per_device,
        mesh=mesh,
        in_specs=(
            P(("dp", "mp"), None),
            P(("dp", "mp"), None),
            P("dp"),
            P(),
            P(),
            P(None, "mp"),
            P("dp", "mp"),
            P("dp", "mp"),
            P("dp", "mp"),
            P("mp", "dp"),
            P("dp", "mp"),
            P("dp", "mp"),
            P("dp", "mp"),
            P("mp", "dp"),
            P("dp", "mp"),
            P("dp", "mp"),
            P("mp", "dp"),
            P(("dp", "mp"), None),
        ),
        out_specs=(
            P(("dp", "mp"), None),
            P(("dp", "mp"), None),
            P(("dp", "mp"), None),
            P(),
            P(),
            P("dp", "mp"),
            P("dp", "mp"),
            P("dp", "mp"),
            P("mp", "dp"),
            P("dp", "mp"),
            P("dp", "mp"),
            P("dp", "mp"),
            P("mp", "dp"),
            P("dp", "mp"),
            P("dp", "mp"),
            P("mp", "dp"),
        ),
        check_vma=False,
    )
```

time: 4750 us -> 760 us (0.16)
  local copies, waits for them, and re-layouts: 3910 us -> 27.2 us
  blocking collectives: 171 us -> 55.1 us
  waiting for transfers between devices: 431 us -> 505 us
  matrix products: 120 us -> 67 us
  Pallas kernels: 0 us -> 51.6 us
    gather x6 -> x0, local copies, waits for them, and re-layouts: 3730 us -> none  [the longest x4 3720 us: self_mask(): extra = jnp.take(dist_bias, jnp.clip(distance, 0, SLOT - 1), axis=1)]
    all_gather x11 -> x0, blocking collectives: 115 us -> none  [the longest x1 13 us: per_device(): lax.all_gather(gate_weight, 'dp', axis=0, tiled=True)]
    all_gather x6, waiting for transfers between devices: 86 us -> 191 us  [full_rows(): return lax.all_gather(share, 'mp', axis=0, tiled=True)]
    reduce_scatter x14 -> x7, waiting for transfers between devices: 283 us -> 199 us  [share_rows(): lax.psum_scatter(total.astype(BF16), 'mp', scatter_dimension=0, tiled=True)]
    rev x2 -> x0, local copies, waits for them, and re-layouts: 81.3 us -> none  [reducer(): flipped = d_scores[:, :, ::-1]]
    pallas_call x0 -> x4, Pallas kernels: none -> 51.6 us  [the longest x2 26.9 us: attention_backward(): pl.pallas_call(functools.partial(bwd_kernel, heads, nq, nk, causal), out_...]
    dot_general x58 -> x26, matrix products: 117 us -> 67 us  [the longest x24 66.3 us: dot(): return lax.dot_general(a, b, dims, preferred_element_type=F32)]
    unnamed x266 -> x109, local copies, waits for them, and re-layouts: 66.6 us -> 18.9 us
  transfers between devices with their start and end apart: 24 -> 17, of which waited for: 13 -> 16; matrix products, arithmetic and copies ran while one was open for 85% -> 10% of each run, Pallas kernels for 0% -> 2%
where the time goes in v1:
time: 760 us; the launch traced here: 750 us
  waiting for transfers between devices  505 us (66%)
  matrix products  67 us (9%)
  blocking collectives  55.1 us (7%)
  Pallas kernels  51.6 us (7%)
  other arithmetic  27.9 us (4%)
  local copies, waits for them, and re-layouts  27.2 us (4%)
  between operations  15.7 us (2%)
    reduce_scatter x7, waiting for transfers between devices, share_rows(): lax.psum_scatter(total.astype(BF16), 'mp', scatter_dimension=0, tiled=True)  199 us
    all_gather x6, waiting for transfers between devices, full_rows(): return lax.all_gather(share, 'mp', axis=0, tiled=True)  191 us
    unnamed x19, waiting for transfers between devices  75.9 us
    dot_general x24, matrix products, dot(): return lax.dot_general(a, b, dims, preferred_element_type=F32)  66.3 us
    psum x1, blocking collectives, per_device(): lax.psum((jnp.stack([gain_one, gain_two, gain_three]), bias_table), ('dp'...  39.5 us
    pallas_call x2, Pallas kernels, attention_backward(): pl.pallas_call(functools.partial(bwd_kernel, heads, nq, nk, causal), out_...  26.9 us
    pallas_call x2, Pallas kernels, attention_forward(): pl.pallas_call(functools.partial(fwd_kernel, heads, nq, nk, causal), out_...  24.7 us
    all_gather x1, waiting for transfers between devices, per_device(): full_self = lax.all_gather(part_self, 'dp', axis=0, tiled=True)  21.5 us
  transfers between devices with their start and end apart: 17, of which 16 were waited for; matrix products, arithmetic and copies ran while one was open for 10% of the time, Pallas kernels for 2%

profile of v1, /device:TPU:1, one launch (start us, length us, event | category | flops | bytes accessed | tf_op | source)
XLA Modules:
  0.0 750.5 jit_solution(2704327311717873338)
XLA Ops:
  8.2 1.6 pad_maximum_fusion.7
  10.6 1.2 fusion.34
  11.8 1.9 fusion.36
  15.6 21.5 %all-gather.11.cloned.1.call-done = bf16[768,768]{1,0:T(8,128)(2,1)} async-done(((bf16[96,768]{1,0:T(8,128)(2,1)}), bf16[768,768]{1,0:T(8,128)(2,1)}) %all-gather.11.cloned.1.call-update) | async-done | bytes 1179664 | tf_op jit(solution)/shard_map/all_gather | solution.py:213
  37.1 38.7 %all-gather.9.cloned.1.call-done = bf16[1024,768]{1,0:T(8,128)(2,1)} async-done(((bf16[256,768]{1,0:T(8,128)(2,1)}), bf16[1024,768]{1,0:T(8,128)(2,1)}) %all-gather.9.cloned.1.call-update) | async-done | bytes 1572880 | tf_op jit(solution)/shard_map/all_gather | solution.py:162
  75.8 3.1 convolution_convert_fusion.5
  78.9 1.4 fusion.80
  80.3 13.9 %attn_fwd.2 = (bf16[1024,192]{1,0:T(8,128)(2,1)}, f32[192,1024]{1,0:T(8,128)}, f32[3,1024]{1,0:T(4,128)}) custom-call(s32[1]{0:T(128)} %copy.129.refs_0_, f32[9,512]{1,0:T(8,128)} %reshape.92.refs_1_, bf16[1024,192]{1,0:T(8,128)(2,1)} %get-tuple-element.124.refs_2_, bf16[1024,192]{1,0:T(8,128)(2,1)} %get-tuple-element.123.refs_3_, ...), custom_call_target="tpu_custom_call" | custom-call | tf_op jit(solution)/shard_map/attn_fwd/pallas_call | solution.py:140
  94.2 3.1 convolution_convert_fusion.4
  98.5 33.1 %reduce-scatter.14.cloned.1.call-done = bf16[256,768]{1,0:T(8,128)(2,1)} async-done(((bf16[1024,768]{1,0:T(8,128)(2,1)}), bf16[256,768]{1,0:T(8,128)(2,1)}) %reduce-scatter.14.cloned.1.call-update) | async-done | bytes 393232 | tf_op jit(solution)/shard_map/reduce_scatter | solution.py:166
  131.6 1.2 multiply_reduce_fusion.1
  132.8 1.9 multiply_convert_fusion.3
  134.8 15.6 %all_gather.31 = bf16[512,768]{1,0:T(8,128)(2,1)S(1)} all-gather(bf16[128,768]{1,0:T(8,128)(2,1)S(1)} %copy-done.16), channel_id=1, replica_groups=mesh['dp'=8,'mp'=4] {'mp'}, dimensions={0}, use_global_device_ids=true | all-gather | bytes 983040 | tf_op jit(solution)/shard_map/all_gather | solution.py:162
  150.5 16.4 %all-gather.15.cloned.1.call-done = bf16[768,2304]{1,0:T(8,128)(2,1)} async-done(((bf16[96,2304]{1,0:T(8,128)(2,1)}), bf16[768,2304]{1,0:T(8,128)(2,1)}) %all-gather.15.cloned.1.call-update) | async-done | bytes 3538960 | tf_op jit(solution)/shard_map/all_gather | solution.py:214
  166.9 1.8 fusion.14
  169.6 35.9 %all-gather.13.cloned.1.call-done = bf16[1024,768]{1,0:T(8,128)(2,1)} async-done(((bf16[256,768]{1,0:T(8,128)(2,1)}), bf16[1024,768]{1,0:T(8,128)(2,1)}) %all-gather.13.cloned.1.call-update) | async-done | bytes 1572880 | tf_op jit(solution)/shard_map/all_gather | solution.py:162
  205.5 2.9 convolution_convert_fusion.12.refs_0_
  208.3 10.8 %attn_fwd.3 = (bf16[1024,192]{1,0:T(8,128)(2,1)}, f32[192,1024]{1,0:T(8,128)}, f32[3,1024]{1,0:T(4,128)}) custom-call(bf16[1024,192]{1,0:T(8,128)(2,1)} %convolution_convert_fusion.12.refs_0_, bf16[512,192]{1,0:T(8,128)(2,1)} %get-tuple-element.132.refs_1_, bf16[512,192]{1,0:T(8,128)(2,1)} %get-tuple-element.131.refs_2_), custom_call_target="tpu_custom_call" | custom-call | tf_op jit(solution)/shard_map/attn_fwd/pallas_call | solution.py:140
  219.2 3.1 convolution_convert_fusion.3
  222.3 34.2 %reduce-scatter.16.cloned.1.call-done = bf16[256,768]{1,0:T(8,128)(2,1)} async-done(((bf16[1024,768]{1,0:T(8,128)(2,1)}), bf16[256,768]{1,0:T(8,128)(2,1)}) %reduce-scatter.16.cloned.1.call-update) | async-done | bytes 393232 | tf_op jit(solution)/shard_map/reduce_scatter | solution.py:166
  256.6 1.3 multiply_reduce_fusion
  257.8 2.0 multiply_convert_fusion.2
  261.0 35.0 %all-gather.17.cloned.1.call-done = bf16[1024,768]{1,0:T(8,128)(2,1)} async-done(((bf16[256,768]{1,0:T(8,128)(2,1)}), bf16[1024,768]{1,0:T(8,128)(2,1)}) %all-gather.17.cloned.1.call-update) | async-done | bytes 1572880 | tf_op jit(solution)/shard_map/all_gather | solution.py:162
  296.1 4.0 fusion.49
  300.1 3.5 fusion.45
  303.6 30.6 %all-gather.19.cloned.1.call-done = bf16[1024,768]{1,0:T(8,128)(2,1)} async-done(((bf16[256,768]{1,0:T(8,128)(2,1)}), bf16[1024,768]{1,0:T(8,128)(2,1)}) %all-gather.19.cloned.1.call-update) | async-done | bytes 1572880 | tf_op jit(solution)/shard_map/all_gather | solution.py:162
  334.2 6.3 multiply_convert_fusion
  340.5 2.7 fusion.47
  343.3 3.4 add_convert_fusion
  346.7 34.2 %reduce-scatter.20.cloned.1.call-done = bf16[256,768]{1,0:T(8,128)(2,1)} async-done(((bf16[1024,768]{1,0:T(8,128)(2,1)}), bf16[256,768]{1,0:T(8,128)(2,1)}) %reduce-scatter.20.cloned.1.call-update) | async-done | bytes 393232 | tf_op jit(solution)/shard_map/reduce_scatter | solution.py:166
  380.9 2.0 fusion.31
  382.9 2.1 fusion.77
  385.1 36.2 %all-gather.21.cloned.1.call-done = bf16[1024,768]{1,0:T(8,128)(2,1)} async-done(((bf16[256,768]{1,0:T(8,128)(2,1)}), bf16[1024,768]{1,0:T(8,128)(2,1)}) %all-gather.21.cloned.1.call-update) | async-done | bytes 1572880 | tf_op jit(solution)/shard_map/all_gather | solution.py:162
  421.3 2.3 convolution_convert_fusion.15
  424.7 10.8 %attn_bwd.2 = (bf16[1024,192]{1,0:T(8,128)(2,1)}, bf16[512,192]{1,0:T(8,128)(2,1)}, bf16[512,192]{1,0:T(8,128)(2,1)}) custom-call(bf16[1024,192]{1,0:T(8,128)(2,1)} %convolution_convert_fusion.12.refs_0_, bf16[512,192]{1,0:T(8,128)(2,1)} %get-tuple-element.132.refs_1_, bf16[512,192]{1,0:T(8,128)(2,1)} %get-tuple-element.131.refs_2_, ...), custom_call_target="tpu_custom_call" | custom-call | tf_op jit(solution)/shard_map/attn_bwd/pallas_call | solution.py:150
  435.5 3.0 convolution_convert_fusion.2
  438.5 3.7 convolution_convert_fusion.1
  442.3 30.4 %reduce-scatter.22.cloned.1.call-done = bf16[256,768]{1,0:T(8,128)(2,1)} async-done(((bf16[1024,768]{1,0:T(8,128)(2,1)}), bf16[256,768]{1,0:T(8,128)(2,1)}) %reduce-scatter.22.cloned.1.call-update) | async-done | bytes 393232 | tf_op jit(solution)/shard_map/reduce_scatter | solution.py:166
  472.8 1.9 fusion.33
  475.2 33.9 %reduce-scatter.18.cloned.1.call-done = bf16[256,768]{1,0:T(8,128)(2,1)} async-done(((bf16[1024,768]{1,0:T(8,128)(2,1)}), bf16[256,768]{1,0:T(8,128)(2,1)}) %reduce-scatter.18.cloned.1.call-update) | async-done | bytes 393232 | tf_op jit(solution)/shard_map/reduce_scatter | solution.py:166
  509.2 2.7 fusion.78
  511.9 2.9 convolution_convert_fusion.10
  515.2 2.7 fusion.12
  517.8 1.5 fusion.11
  519.7 1.2 fusion.13
  521.5 1.9 fusion.7
  523.5 1.9 fusion.8
  525.4 2.0 fusion.9
  527.4 5.8 copy.115
  533.3 14.8 %all-gather.23.cloned.1.call-done = bf16[1024,768]{1,0:T(8,128)(2,1)} async-done(((bf16[256,768]{1,0:T(8,128)(2,1)}), bf16[1024,768]{1,0:T(8,128)(2,1)}) %all-gather.23.cloned.1.call-update) | async-done | bytes 1572880 | tf_op jit(solution)/shard_map/all_gather | solution.py:162
  548.1 2.2 convolution_convert_fusion.14
  551.4 16.1 %attn_bwd.3 = (bf16[1024,192]{1,0:T(8,128)(2,1)}, bf16[1024,192]{1,0:T(8,128)(2,1)}, bf16[1024,192]{1,0:T(8,128)(2,1)}, f32[9,512]{1,0:T(8,128)}) custom-call(s32[1]{0:T(128)} %copy.129.refs_0_, f32[9,512]{1,0:T(8,128)} %reshape.92.refs_1_, bf16[1024,192]{1,0:T(8,128)(2,1)} %get-tuple-element.124.refs_2_, bf16[1024,192]{1,0:T(8,128)(2,1)} %get-tuple-element.123.refs_3_, ...), custom_call_target="tpu_custom_call" | custom-call | tf_op jit(solution)/shard_map/attn_bwd/pallas_call | solution.py:150
  567.5 1.7 convolution_convert_fusion.18
  569.5 1.4 convolution_convert_fusion.6
  571.0 1.4 copy.113
  572.8 4.0 convolution_convert_fusion
  578.2 1.7 convert_element_type.186
  579.9 43.4 %reduce-scatter.30.cloned.1.call-done = bf16[96,2304]{1,0:T(8,128)(2,1)} async-done(((bf16[768,2304]{1,0:T(8,128)(2,1)}), bf16[96,2304]{1,0:T(8,128)(2,1)}) %reduce-scatter.30.cloned.1.call-update) | async-done | bytes 442384
  623.3 1.3 copy.116
  630.8 32.2 %reduce-scatter.28.cloned.1.call-done = bf16[96,768]{1,0:T(8,128)(2,1)} async-done(((bf16[768,768]{1,0:T(8,128)(2,1)}), bf16[96,768]{1,0:T(8,128)(2,1)}) %reduce-scatter.28.cloned.1.call-update) | async-done | bytes 147472
  667.0 33.5 %reduce-scatter.24.cloned.1.call-done = bf16[256,768]{1,0:T(8,128)(2,1)} async-done(((bf16[1024,768]{1,0:T(8,128)(2,1)}), bf16[256,768]{1,0:T(8,128)(2,1)}) %reduce-scatter.24.cloned.1.call-update) | async-done | bytes 393232 | tf_op jit(solution)/shard_map/reduce_scatter | solution.py:166
  700.5 1.3 fusion.39
  701.9 39.5 %all-reduce.2 = (f32[3,768]{1,0:T(4,128)}, f32[32,12]{0,1:T(8,128)}) all-reduce(f32[3,768]{1,0:T(4,128)S(1)} %pad_maximum_fusion.9, f32[32,12]{0,1:T(8,128)S(1)} %dynamic_update_slice.3), channel_id=1, replica_groups=mesh['dp'=8,'mp'=4] {'dp','mp'}, use_global_device_ids=true, to_apply=%region_16.0 | all-reduce | flops 2688 | bytes 21504 | tf_op jit(solution)/shard_map/psum | solution.py:292
  741.4 2.1 fusion.23
  (185 shorter events, 22.7 us)
Async XLA Ops:
  7.2 7.2 copy-start
  7.2 7.2 copy-start.43
  7.2 29.9 %all-gather.11.cloned.1.call-start = ((), (), s32[]{:S(2)}) async-start(), calls=%async_computation.10 | async-start | bytes 1327104 | tf_op jit(solution)/shard_map/all_gather | solution.py:213
  9.8 66.0 %all-gather.9.cloned.1.call-start = ((), (), s32[]{:S(2)}) async-start(), calls=%async_computation.9 | async-start | bytes 1966080 | tf_op jit(solution)/shard_map/all_gather | solution.py:162
  11.7 3.0 copy-start.31
  11.7 3.2 copy-start.25
  13.7 117.9 %reduce-scatter.14.cloned.1.call-start = ((), (), s32[]{:S(2)}) async-start(), calls=%async_computation.11 | async-start | bytes 1966080 | tf_op jit(solution)/shard_map/reduce_scatter | solution.py:166
  94.2 3.2 copy-start.23
  94.2 3.3 copy-start.17
  94.2 3.4 copy-start.18
  94.2 3.4 copy-start.19
  94.2 3.4 copy-start.20
  94.2 3.3 copy-start.21
  94.2 3.3 copy-start.22
  97.3 34.3 %copy-start.2 = (bf16[256,768]{1,0:T(8,128)(2,1)S(1)}, bf16[256,768]{1,0:T(8,128)(2,1)}, u32[]{:S(2)}) copy-start(bf16[256,768]{1,0:T(8,128)(2,1)} %param.18) | copy-start | bytes 1179652
  97.3 37.5 %copy-start.16 = (bf16[128,768]{1,0:T(8,128)(2,1)S(1)}, bf16[128,768]{1,0:T(8,128)(2,1)}, u32[]{:S(2)}) copy-start(bf16[128,768]{1,0:T(8,128)(2,1)} %param.19) | copy-start | bytes 589828
  97.3 69.5 %all-gather.15.cloned.1.call-start = ((), (), s32[]{:S(2)}) async-start(), calls=%async_computation.13 | async-start | bytes 3981312 | tf_op jit(solution)/shard_map/all_gather | solution.py:214
  98.5 107.0 %all-gather.13.cloned.1.call-start = ((), (), s32[]{:S(2)}) async-start(), calls=%async_computation.12 | async-start | bytes 1966080 | tf_op jit(solution)/shard_map/all_gather | solution.py:162
  132.8 339.9 %copy-start.30 = (f32[256]{0:T(256)}, f32[256]{0:T(256)S(1)}, u32[]{:S(2)}) copy-start(f32[256]{0:T(256)S(1)} %add_rsqrt_fusion.1) | copy-start | bytes 3076
  134.8 121.8 %reduce-scatter.16.cloned.1.call-start = ((), (), s32[]{:S(2)}) async-start(), calls=%async_computation.14 | async-start | bytes 1966080 | tf_op jit(solution)/shard_map/reduce_scatter | solution.py:166
  219.2 37.4 %copy-start.3 = (bf16[256,768]{1,0:T(8,128)(2,1)S(1)}, bf16[256,768]{1,0:T(8,128)(2,1)}, u32[]{:S(2)}) copy-start(bf16[256,768]{1,0:T(8,128)(2,1)} %reduce-scatter.14.cloned.1.call-done) | copy-start | bytes 1179652
  222.3 37.6 %copy-start.5 = (bf16[256,768]{1,0:T(8,128)(2,1)S(1)}, bf16[256,768]{1,0:T(8,128)(2,1)}, u32[]{:S(2)}) copy-start(bf16[256,768]{1,0:T(8,128)(2,1)} %param.35) | copy-start | bytes 1179652
  222.3 73.8 %all-gather.17.cloned.1.call-start = ((), (), s32[]{:S(2)}) async-start(), calls=%async_computation.15 | async-start | bytes 1966080 | tf_op jit(solution)/shard_map/all_gather | solution.py:162
  259.8 74.4 %all-gather.19.cloned.1.call-start = ((), (), s32[]{:S(2)}) async-start(), calls=%async_computation.17 | async-start | bytes 1966080 | tf_op jit(solution)/shard_map/all_gather | solution.py:162
  259.9 123.0 %copy-start.29 = (f32[256]{0:T(256)}, f32[256]{0:T(256)S(1)}, u32[]{:S(2)}) copy-start(f32[256]{0:T(256)S(1)} %compare_convert_fusion.1) | copy-start | bytes 3076
  260.8 120.1 %reduce-scatter.20.cloned.1.call-start = ((), (), s32[]{:S(2)}) async-start(), calls=%async_computation.18 | async-start | bytes 1966080 | tf_op jit(solution)/shard_map/reduce_scatter | solution.py:166
  296.1 4.0 copy-start.35
  340.5 2.7 copy-start.11
  340.5 2.7 copy-start.9
  343.3 37.7 %copy-start.4 = (bf16[256,768]{1,0:T(8,128)(2,1)S(1)}, bf16[256,768]{1,0:T(8,128)(2,1)}, u32[]{:S(2)}) copy-start(bf16[256,768]{1,0:T(8,128)(2,1)} %reduce-scatter.16.cloned.1.call-done) | copy-start | bytes 1179652
  346.7 74.7 %all-gather.21.cloned.1.call-start = ((), (), s32[]{:S(2)}) async-start(), calls=%async_computation.19 | async-start | bytes 1966080 | tf_op jit(solution)/shard_map/all_gather | solution.py:162
  382.9 40.7 %copy-start.33 = (f32[256]{0:T(256)}, f32[256]{0:T(256)S(1)}, u32[]{:S(2)}) copy-start(f32[256]{0:T(256)S(1)} %fusion.67) | copy-start | bytes 3076
  385.1 87.7 %reduce-scatter.22.cloned.1.call-start = ((), (), s32[]{:S(2)}) async-start(), calls=%async_computation.20 | async-start | bytes 1966080 | tf_op jit(solution)/shard_map/reduce_scatter | solution.py:166
  438.5 70.7 %reduce-scatter.18.cloned.1.call-start = ((), (), s32[]{:S(2)}) async-start(), calls=%async_computation.16 | async-start | bytes 1966080 | tf_op jit(solution)/shard_map/reduce_scatter | solution.py:166
  442.2 67.0 %copy-start.6 = (bf16[256,768]{1,0:T(8,128)(2,1)S(1)}, bf16[256,768]{1,0:T(8,128)(2,1)}, u32[]{:S(2)}) copy-start(bf16[256,768]{1,0:T(8,128)(2,1)} %reduce-scatter.20.cloned.1.call-done) | copy-start | bytes 1179652
  442.3 105.9 %all-gather.23.cloned.1.call-start = ((), (), s32[]{:S(2)}) async-start(), calls=%async_computation.21 | async-start | bytes 1966080 | tf_op jit(solution)/shard_map/all_gather | solution.py:162
  511.8 3.3 copy-start.15
  511.9 66.3 %reduce-scatter.26.cloned.1.call-start = ((), (), s32[]{:S(2)}) async-start(), calls=%async_computation.23 | async-start | bytes 983040 | tf_op jit(solution)/shard_map/reduce_scatter | solution.py:166
  514.9 3.0 copy-start.41
  514.9 2.9 copy-start.42
  514.9 108.4 %reduce-scatter.30.cloned.1.call-start = ((), (), s32[]{:S(2)}) async-start(), calls=%async_computation.25 | async-start | bytes 3981312
  517.8 1.5 copy-start.7
  517.8 1.8 copy-start.14
  519.7 1.3 copy-start.12
  519.7 1.9 copy-start.36
  521.5 1.9 copy-start.10
  523.5 1.9 copy-start.37
  523.5 1.9 copy-start.45
  533.3 129.7 %reduce-scatter.28.cloned.1.call-start = ((), (), s32[]{:S(2)}) async-start(), calls=%async_computation.24 | async-start | bytes 1327104
  550.4 17.1 %copy-start.8 = (bf16[1024,768]{1,0:T(8,128)(2,1)S(1)}, bf16[1024,768]{1,0:T(8,128)(2,1)}, u32[]{:S(2)}) copy-start(bf16[1024,768]{1,0:T(8,128)(2,1)} %all-gather.23.cloned.1.call-done) | copy-start | bytes 4718596
  567.5 1.8 copy-start.34
  567.5 1.8 copy-start.38
  567.5 1.8 copy-start.39
  567.5 2.0 copy-start.40
  571.0 1.8 copy-start.13
  572.5 4.4 copy-start.44
  572.5 5.6 copy-start.27
  572.5 128.0 %reduce-scatter.24.cloned.1.call-start = ((), (), s32[]{:S(2)}) async-start(), calls=%async_computation.22 | async-start | bytes 1966080 | tf_op jit(solution)/shard_map/reduce_scatter | solution.py:166
  576.8 3.0 copy-start.28
  624.7 5.4 copy-start.24
  627.7 72.8 %copy-start.26 = (f32[256]{0:T(256)S(1)}, f32[256]{0:T(256)}, u32[]{:S(2)}) copy-start(f32[256]{0:T(256)} %copy-done.25) | copy-start | bytes 3076
  628.6 73.3 %copy-start.32 = (f32[256]{0:T(256)S(1)}, f32[256]{0:T(256)}, u32[]{:S(2)}) copy-start(f32[256]{0:T(256)} %copy-done.31) | copy-start | bytes 3076
  664.1 79.4 %copy-start.1 = (bf16[32,3]{0,1:T(4,128)(2,1)S(1)}, bf16[32,3]{0,1:T(4,128)(2,1)}, u32[]{:S(2)}) copy-start(bf16[32,3]{0,1:T(4,128)(2,1)} %param.23) | copy-start | bytes 580
Sparse Core Ops, SparseCore 0:
  10.5 26.5 all-gather.10
  39.3 36.5 all-gather.8
  97.5 34.0 reduce-scatter.13
  133.3 33.4 all-gather.14
  168.9 36.5 all-gather.12
  222.4 34.1 reduce-scatter.15
  259.9 36.0 all-gather.16
  298.2 35.9 all-gather.18
  346.8 34.0 reduce-scatter.19
  385.2 36.1 all-gather.20
  438.6 34.0 reduce-scatter.21
  474.9 34.2 reduce-scatter.17
  512.0 36.0 all-gather.22
  550.3 20.9 reduce-scatter.25
  574.6 48.5 reduce-scatter.29
  626.3 36.6 reduce-scatter.27
  665.3 35.2 reduce-scatter.23

commit v2 on v1

--- a/solution.py
+++ b/solution.py
@@ -112,7 +112,13 @@
 
 def bwd_kernel(heads,nq,nk,causal,*refs):
     if causal:
-        length,vecs,q,k,v,do,out_t,lse,dq,dk,dv,dvec,q3,k3,v3,kt3,do3,delta,dqt,dk3,dv3,tiles,kmask,dtile=refs
+        length,vecs,q,k,v,do,out_t,lse,dq,dk,dv,dvec,q3,k3,v3,kt3,do3,delta,dqt,dk3,dv3,tiles,kmask,dtile,land,sems=refs
+        other={"mp": lax.axis_index("mp")^1}
+        barrier=pltpu.get_barrier_semaphore()
+        pl.semaphore_signal(barrier,inc=1,device_id=other,device_id_type=pl.DeviceIdType.MESH)
+        pl.semaphore_wait(barrier,1)
+        copy=pltpu.make_async_remote_copy(src_ref=do,dst_ref=land,send_sem=sems.at[0],recv_sem=sems.at[1],device_id=other,device_id_type=pl.DeviceIdType.MESH)
+        copy.start()
     else:
         q,k,v,do,out_t,lse,dq,dk,dv,q3,k3,v3,kt3,do3,delta,dqt,dk3,dv3=refs; tiles=kmask=dtile=None
     hd=q3.shape[2]
@@ -128,7 +134,9 @@
     dq[...]=dqt[...].T.astype(BF16)
     for h in range(heads):
         dk[:,h*hd:(h+1)*hd]=dk3[h].astype(BF16); dv[:,h*hd:(h+1)*hd]=dv3[h].astype(BF16)
-    if causal: bias_diag(dtile,dvec,heads)
+    if causal:
+        bias_diag(dtile,dvec,heads)
+        copy.wait()
 
 V=pl.BlockSpec(memory_space=pltpu.VMEM); S=pl.BlockSpec(memory_space=pltpu.SMEM)
 def attention_forward(q,k,v,heads,length=None,vecs=None):
@@ -143,12 +151,12 @@
     nq,w=q.shape; nk=k.shape[0]; hd=w//heads; causal=length is not None
     sc=[pltpu.VMEM((heads,nq,hd),BF16)]+[pltpu.VMEM((heads,nk,hd),BF16)]*2+[pltpu.VMEM((heads,hd,nk),BF16),pltpu.VMEM((heads,nq,hd),BF16),
         pltpu.VMEM((heads,nq),F32),pltpu.VMEM((w,nq),F32),pltpu.VMEM((heads,nk,hd),F32),pltpu.VMEM((heads,nk,hd),F32)]
-    if causal: sc+=[pltpu.VMEM((heads,3,TILE,TILE),F32),pltpu.VMEM((nk,128),F32),pltpu.VMEM((heads,3,TILE,TILE),F32)]
+    if causal: sc+=[pltpu.VMEM((heads,3,TILE,TILE),F32),pltpu.VMEM((nk,128),F32),pltpu.VMEM((heads,3,TILE,TILE),F32),pltpu.VMEM((nq,w),BF16),pltpu.SemaphoreType.DMA((2,))]
     outs=[jax.ShapeDtypeStruct((nq,w),BF16),jax.ShapeDtypeStruct((nk,w),BF16),jax.ShapeDtypeStruct((nk,w),BF16)]
     if causal: outs.append(jax.ShapeDtypeStruct((heads*3,2*TILE),F32))
     args=([length,vecs] if causal else [])+[q,k,v,do,out_t,lse]
     return pl.pallas_call(functools.partial(bwd_kernel,heads,nq,nk,causal),out_shape=outs,
-        in_specs=([S,V] if causal else [])+[V]*6,out_specs=[V]*len(outs),scratch_shapes=sc,name="attn_bwd")(*args)
+        in_specs=([S,V] if causal else [])+[V]*6,out_specs=[V]*len(outs),scratch_shapes=sc,name="attn_bwd",compiler_params=pltpu.CompilerParams(collective_id=0,has_side_effects=True) if causal else None)(*args)
 def bias_vectors(t):
     h=t.shape[0]; far=t[:,TILE:TILE+1]
     z=jnp.broadcast_to(far,(h,TILE))

time: 760 us -> 768 us (1.011)
  Pallas kernels: 51.6 us -> 62.2 us
    pallas_call x2, Pallas kernels: 26.9 us -> 37.5 us  [attention_backward(): pl.pallas_call(functools.partial(bwd_kernel, heads, nq, nk, causal), out_...]
  transfers between devices with their start and end apart: 17 -> 17, of which waited for: 16 -> 16; matrix products, arithmetic and copies ran while one was open for 10% -> 10% of each run, Pallas kernels for 2% -> 4%
where the time goes in v2:
time: 768 us; the launch traced here: 759 us
  waiting for transfers between devices  502 us (65%)
  matrix products  67 us (9%)
  Pallas kernels  62.2 us (8%)
  blocking collectives  55.1 us (7%)
  other arithmetic  28 us (4%)
  local copies, waits for them, and re-layouts  27.2 us (4%)
  between operations  15.7 us (2%)
    reduce_scatter x7, waiting for transfers between devices, share_rows(): lax.psum_scatter(total.astype(BF16), 'mp', scatter_dimension=0, tiled=True)  199 us
    all_gather x6, waiting for transfers between devices, full_rows(): return lax.all_gather(share, 'mp', axis=0, tiled=True)  191 us
    unnamed x19, waiting for transfers between devices  73.6 us
    dot_general x24, matrix products, dot(): return lax.dot_general(a, b, dims, preferred_element_type=F32)  66.3 us
    psum x1, blocking collectives, per_device(): lax.psum((jnp.stack([gain_one, gain_two, gain_three]), bias_table), ('dp'...  39.5 us
    pallas_call x2, Pallas kernels, attention_backward(): pl.pallas_call(functools.partial(bwd_kernel, heads, nq, nk, causal), out_...  37.5 us
    pallas_call x2, Pallas kernels, attention_forward(): pl.pallas_call(functools.partial(fwd_kernel, heads, nq, nk, causal), out_...  24.7 us
    all_gather x1, waiting for transfers between devices, per_device(): full_self = lax.all_gather(part_self, 'dp', axis=0, tiled=True)  21.5 us
  transfers between devices with their start and end apart: 17, of which 16 were waited for; matrix products, arithmetic and copies ran while one was open for 10% of the time, Pallas kernels for 4%

profile of v2, /device:TPU:1, one launch (start us, length us, event | category | flops | bytes accessed | tf_op | source)
XLA Modules:
  0.0 758.8 jit_solution(8809638470164934200)
XLA Ops:
  8.2 1.6 pad_maximum_fusion.7
  10.6 1.2 fusion.34
  11.8 1.9 fusion.36
  15.6 21.5 %all-gather.11.cloned.1.call-done = bf16[768,768]{1,0:T(8,128)(2,1)} async-done(((bf16[96,768]{1,0:T(8,128)(2,1)}), bf16[768,768]{1,0:T(8,128)(2,1)}) %all-gather.11.cloned.1.call-update) | async-done | bytes 1179664 | tf_op jit(solution)/shard_map/all_gather | solution.py:221
  37.1 38.7 %all-gather.9.cloned.1.call-done = bf16[1024,768]{1,0:T(8,128)(2,1)} async-done(((bf16[256,768]{1,0:T(8,128)(2,1)}), bf16[1024,768]{1,0:T(8,128)(2,1)}) %all-gather.9.cloned.1.call-update) | async-done | bytes 1572880 | tf_op jit(solution)/shard_map/all_gather | solution.py:170
  75.8 3.1 convolution_convert_fusion.5
  78.9 1.4 fusion.80
  80.3 13.9 %attn_fwd.2 = (bf16[1024,192]{1,0:T(8,128)(2,1)}, f32[192,1024]{1,0:T(8,128)}, f32[3,1024]{1,0:T(4,128)}) custom-call(s32[1]{0:T(128)} %copy.129.refs_0_, f32[9,512]{1,0:T(8,128)} %reshape.92.refs_1_, bf16[1024,192]{1,0:T(8,128)(2,1)} %get-tuple-element.124.refs_2_, bf16[1024,192]{1,0:T(8,128)(2,1)} %get-tuple-element.123.refs_3_, ...), custom_call_target="tpu_custom_call" | custom-call | tf_op jit(solution)/shard_map/attn_fwd/pallas_call | solution.py:148
  94.2 3.1 convolution_convert_fusion.4
  98.5 33.1 %reduce-scatter.14.cloned.1.call-done = bf16[256,768]{1,0:T(8,128)(2,1)} async-done(((bf16[1024,768]{1,0:T(8,128)(2,1)}), bf16[256,768]{1,0:T(8,128)(2,1)}) %reduce-scatter.14.cloned.1.call-update) | async-done | bytes 393232 | tf_op jit(solution)/shard_map/reduce_scatter | solution.py:174
  131.6 1.2 multiply_reduce_fusion.1
  132.8 1.9 multiply_convert_fusion.3
  134.8 15.6 %all_gather.31 = bf16[512,768]{1,0:T(8,128)(2,1)S(1)} all-gather(bf16[128,768]{1,0:T(8,128)(2,1)S(1)} %copy-done.16), channel_id=1, replica_groups=mesh['dp'=8,'mp'=4] {'mp'}, dimensions={0}, use_global_device_ids=true | all-gather | bytes 983040 | tf_op jit(solution)/shard_map/all_gather | solution.py:170
  150.5 16.4 %all-gather.15.cloned.1.call-done = bf16[768,2304]{1,0:T(8,128)(2,1)} async-done(((bf16[96,2304]{1,0:T(8,128)(2,1)}), bf16[768,2304]{1,0:T(8,128)(2,1)}) %all-gather.15.cloned.1.call-update) | async-done | bytes 3538960 | tf_op jit(solution)/shard_map/all_gather | solution.py:222
  166.9 1.8 fusion.14
  169.6 35.9 %all-gather.13.cloned.1.call-done = bf16[1024,768]{1,0:T(8,128)(2,1)} async-done(((bf16[256,768]{1,0:T(8,128)(2,1)}), bf16[1024,768]{1,0:T(8,128)(2,1)}) %all-gather.13.cloned.1.call-update) | async-done | bytes 1572880 | tf_op jit(solution)/shard_map/all_gather | solution.py:170
  205.5 2.9 convolution_convert_fusion.12.refs_0_
  208.3 10.8 %attn_fwd.3 = (bf16[1024,192]{1,0:T(8,128)(2,1)}, f32[192,1024]{1,0:T(8,128)}, f32[3,1024]{1,0:T(4,128)}) custom-call(bf16[1024,192]{1,0:T(8,128)(2,1)} %convolution_convert_fusion.12.refs_0_, bf16[512,192]{1,0:T(8,128)(2,1)} %get-tuple-element.132.refs_1_, bf16[512,192]{1,0:T(8,128)(2,1)} %get-tuple-element.131.refs_2_), custom_call_target="tpu_custom_call" | custom-call | tf_op jit(solution)/shard_map/attn_fwd/pallas_call | solution.py:148
  219.2 3.1 convolution_convert_fusion.3
  222.4 34.2 %reduce-scatter.16.cloned.1.call-done = bf16[256,768]{1,0:T(8,128)(2,1)} async-done(((bf16[1024,768]{1,0:T(8,128)(2,1)}), bf16[256,768]{1,0:T(8,128)(2,1)}) %reduce-scatter.16.cloned.1.call-update) | async-done | bytes 393232 | tf_op jit(solution)/shard_map/reduce_scatter | solution.py:174
  256.6 1.3 multiply_reduce_fusion
  257.8 2.0 multiply_convert_fusion.2
  261.0 35.0 %all-gather.17.cloned.1.call-done = bf16[1024,768]{1,0:T(8,128)(2,1)} async-done(((bf16[256,768]{1,0:T(8,128)(2,1)}), bf16[1024,768]{1,0:T(8,128)(2,1)}) %all-gather.17.cloned.1.call-update) | async-done | bytes 1572880 | tf_op jit(solution)/shard_map/all_gather | solution.py:170
  296.1 4.0 fusion.49
  300.1 3.5 fusion.45
  303.6 30.6 %all-gather.19.cloned.1.call-done = bf16[1024,768]{1,0:T(8,128)(2,1)} async-done(((bf16[256,768]{1,0:T(8,128)(2,1)}), bf16[1024,768]{1,0:T(8,128)(2,1)}) %all-gather.19.cloned.1.call-update) | async-done | bytes 1572880 | tf_op jit(solution)/shard_map/all_gather | solution.py:170
  334.2 6.3 multiply_convert_fusion
  340.5 2.7 fusion.47
  343.3 3.4 add_convert_fusion
  346.7 34.2 %reduce-scatter.20.cloned.1.call-done = bf16[256,768]{1,0:T(8,128)(2,1)} async-done(((bf16[1024,768]{1,0:T(8,128)(2,1)}), bf16[256,768]{1,0:T(8,128)(2,1)}) %reduce-scatter.20.cloned.1.call-update) | async-done | bytes 393232 | tf_op jit(solution)/shard_map/reduce_scatter | solution.py:174
  380.9 2.0 fusion.31
  382.9 2.1 fusion.77
  385.1 36.2 %all-gather.21.cloned.1.call-done = bf16[1024,768]{1,0:T(8,128)(2,1)} async-done(((bf16[256,768]{1,0:T(8,128)(2,1)}), bf16[1024,768]{1,0:T(8,128)(2,1)}) %all-gather.21.cloned.1.call-update) | async-done | bytes 1572880 | tf_op jit(solution)/shard_map/all_gather | solution.py:170
  421.3 2.3 convolution_convert_fusion.15
  424.7 10.8 %attn_bwd.2 = (bf16[1024,192]{1,0:T(8,128)(2,1)}, bf16[512,192]{1,0:T(8,128)(2,1)}, bf16[512,192]{1,0:T(8,128)(2,1)}) custom-call(bf16[1024,192]{1,0:T(8,128)(2,1)} %convolution_convert_fusion.12.refs_0_, bf16[512,192]{1,0:T(8,128)(2,1)} %get-tuple-element.132.refs_1_, bf16[512,192]{1,0:T(8,128)(2,1)} %get-tuple-element.131.refs_2_, ...), custom_call_target="tpu_custom_call" | custom-call | tf_op jit(solution)/shard_map/attn_bwd/pallas_call | solution.py:158
  435.5 3.0 convolution_convert_fusion.2
  438.5 3.7 convolution_convert_fusion.1
  442.3 30.4 %reduce-scatter.22.cloned.1.call-done = bf16[256,768]{1,0:T(8,128)(2,1)} async-done(((bf16[1024,768]{1,0:T(8,128)(2,1)}), bf16[256,768]{1,0:T(8,128)(2,1)}) %reduce-scatter.22.cloned.1.call-update) | async-done | bytes 393232 | tf_op jit(solution)/shard_map/reduce_scatter | solution.py:174
  472.8 1.9 fusion.33
  475.2 33.9 %reduce-scatter.18.cloned.1.call-done = bf16[256,768]{1,0:T(8,128)(2,1)} async-done(((bf16[1024,768]{1,0:T(8,128)(2,1)}), bf16[256,768]{1,0:T(8,128)(2,1)}) %reduce-scatter.18.cloned.1.call-update) | async-done | bytes 393232 | tf_op jit(solution)/shard_map/reduce_scatter | solution.py:174
  509.2 2.7 fusion.78
  511.9 2.9 convolution_convert_fusion.10
  515.2 2.6 fusion.12
  517.8 1.5 fusion.11
  519.7 1.2 fusion.13
  521.5 1.9 fusion.7
  523.5 1.9 fusion.8
  525.4 2.0 fusion.9
  527.4 5.8 copy.115
  533.3 14.8 %all-gather.23.cloned.1.call-done = bf16[1024,768]{1,0:T(8,128)(2,1)} async-done(((bf16[256,768]{1,0:T(8,128)(2,1)}), bf16[1024,768]{1,0:T(8,128)(2,1)}) %all-gather.23.cloned.1.call-update) | async-done | bytes 1572880 | tf_op jit(solution)/shard_map/all_gather | solution.py:170
  548.1 2.2 convolution_convert_fusion.14
  551.4 26.7 %attn_bwd.3 = (bf16[1024,192]{1,0:T(8,128)(2,1)}, bf16[1024,192]{1,0:T(8,128)(2,1)}, bf16[1024,192]{1,0:T(8,128)(2,1)}, f32[9,512]{1,0:T(8,128)}) custom-call(s32[1]{0:T(128)} %copy.129.refs_0_, f32[9,512]{1,0:T(8,128)} %reshape.92.refs_1_, bf16[1024,192]{1,0:T(8,128)(2,1)} %get-tuple-element.124.refs_2_, bf16[1024,192]{1,0:T(8,128)(2,1)} %get-tuple-element.123.refs_3_, ...), custom_call_target="tpu_custom_call" | custom-call | tf_op jit(solution)/shard_map/attn_bwd/pallas_call | solution.py:158
  578.2 1.7 convolution_convert_fusion.18
  580.1 1.4 convolution_convert_fusion.6
  581.6 1.5 copy.113
  583.5 4.0 convolution_convert_fusion
  588.8 1.7 convert_element_type.186
  590.5 41.1 %reduce-scatter.30.cloned.1.call-done = bf16[96,2304]{1,0:T(8,128)(2,1)} async-done(((bf16[768,2304]{1,0:T(8,128)(2,1)}), bf16[96,2304]{1,0:T(8,128)(2,1)}) %reduce-scatter.30.cloned.1.call-update) | async-done | bytes 442384
  631.6 1.3 copy.116
  639.1 32.2 %reduce-scatter.28.cloned.1.call-done = bf16[96,768]{1,0:T(8,128)(2,1)} async-done(((bf16[768,768]{1,0:T(8,128)(2,1)}), bf16[96,768]{1,0:T(8,128)(2,1)}) %reduce-scatter.28.cloned.1.call-update) | async-done | bytes 147472
  675.4 33.5 %reduce-scatter.24.cloned.1.call-done = bf16[256,768]{1,0:T(8,128)(2,1)} async-done(((bf16[1024,768]{1,0:T(8,128)(2,1)}), bf16[256,768]{1,0:T(8,128)(2,1)}) %reduce-scatter.24.cloned.1.call-update) | async-done | bytes 393232 | tf_op jit(solution)/shard_map/reduce_scatter | solution.py:174
  708.9 1.3 fusion.39
  710.2 39.5 %all-reduce.2 = (f32[3,768]{1,0:T(4,128)}, f32[32,12]{0,1:T(8,128)}) all-reduce(f32[3,768]{1,0:T(4,128)S(1)} %pad_maximum_fusion.9, f32[32,12]{0,1:T(8,128)S(1)} %dynamic_update_slice.3), channel_id=1, replica_groups=mesh['dp'=8,'mp'=4] {'dp','mp'}, use_global_device_ids=true, to_apply=%region_16.0 | all-reduce | flops 2688 | bytes 21504 | tf_op jit(solution)/shard_map/psum | solution.py:300
  749.7 2.1 fusion.23
  (185 shorter events, 22.7 us)
Async XLA Ops:
  7.2 7.2 copy-start
  7.2 7.2 copy-start.43
  7.2 29.9 %all-gather.11.cloned.1.call-start = ((), (), s32[]{:S(2)}) async-start(), calls=%async_computation.10 | async-start | bytes 1327104 | tf_op jit(solution)/shard_map/all_gather | solution.py:221
  9.8 66.0 %all-gather.9.cloned.1.call-start = ((), (), s32[]{:S(2)}) async-start(), calls=%async_computation.9 | async-start | bytes 1966080 | tf_op jit(solution)/shard_map/all_gather | solution.py:170
  11.7 3.0 copy-start.31
  11.7 3.2 copy-start.25
  13.7 117.9 %reduce-scatter.14.cloned.1.call-start = ((), (), s32[]{:S(2)}) async-start(), calls=%async_computation.11 | async-start | bytes 1966080 | tf_op jit(solution)/shard_map/reduce_scatter | solution.py:174
  94.2 3.2 copy-start.23
  94.2 3.3 copy-start.17
  94.2 3.4 copy-start.18
  94.2 3.4 copy-start.19
  94.2 3.4 copy-start.20
  94.2 3.3 copy-start.21
  94.2 3.3 copy-start.22
  97.3 34.3 %copy-start.2 = (bf16[256,768]{1,0:T(8,128)(2,1)S(1)}, bf16[256,768]{1,0:T(8,128)(2,1)}, u32[]{:S(2)}) copy-start(bf16[256,768]{1,0:T(8,128)(2,1)} %param.18) | copy-start | bytes 1179652
  97.3 37.5 %copy-start.16 = (bf16[128,768]{1,0:T(8,128)(2,1)S(1)}, bf16[128,768]{1,0:T(8,128)(2,1)}, u32[]{:S(2)}) copy-start(bf16[128,768]{1,0:T(8,128)(2,1)} %param.19) | copy-start | bytes 589828
  97.3 69.5 %all-gather.15.cloned.1.call-start = ((), (), s32[]{:S(2)}) async-start(), calls=%async_computation.13 | async-start | bytes 3981312 | tf_op jit(solution)/shard_map/all_gather | solution.py:222
  98.5 107.0 %all-gather.13.cloned.1.call-start = ((), (), s32[]{:S(2)}) async-start(), calls=%async_computation.12 | async-start | bytes 1966080 | tf_op jit(solution)/shard_map/all_gather | solution.py:170
  132.8 339.9 %copy-start.30 = (f32[256]{0:T(256)}, f32[256]{0:T(256)S(1)}, u32[]{:S(2)}) copy-start(f32[256]{0:T(256)S(1)} %add_rsqrt_fusion.1) | copy-start | bytes 3076
  134.8 121.8 %reduce-scatter.16.cloned.1.call-start = ((), (), s32[]{:S(2)}) async-start(), calls=%async_computation.14 | async-start | bytes 1966080 | tf_op jit(solution)/shard_map/reduce_scatter | solution.py:174
  219.2 37.4 %copy-start.3 = (bf16[256,768]{1,0:T(8,128)(2,1)S(1)}, bf16[256,768]{1,0:T(8,128)(2,1)}, u32[]{:S(2)}) copy-start(bf16[256,768]{1,0:T(8,128)(2,1)} %reduce-scatter.14.cloned.1.call-done) | copy-start | bytes 1179652
  222.3 37.6 %copy-start.5 = (bf16[256,768]{1,0:T(8,128)(2,1)S(1)}, bf16[256,768]{1,0:T(8,128)(2,1)}, u32[]{:S(2)}) copy-start(bf16[256,768]{1,0:T(8,128)(2,1)} %param.35) | copy-start | bytes 1179652
  222.3 73.8 %all-gather.17.cloned.1.call-start = ((), (), s32[]{:S(2)}) async-start(), calls=%async_computation.15 | async-start | bytes 1966080 | tf_op jit(solution)/shard_map/all_gather | solution.py:170
  259.8 74.4 %all-gather.19.cloned.1.call-start = ((), (), s32[]{:S(2)}) async-start(), calls=%async_computation.17 | async-start | bytes 1966080 | tf_op jit(solution)/shard_map/all_gather | solution.py:170
  259.9 123.0 %copy-start.29 = (f32[256]{0:T(256)}, f32[256]{0:T(256)S(1)}, u32[]{:S(2)}) copy-start(f32[256]{0:T(256)S(1)} %compare_convert_fusion.1) | copy-start | bytes 3076
  260.8 120.1 %reduce-scatter.20.cloned.1.call-start = ((), (), s32[]{:S(2)}) async-start(), calls=%async_computation.18 | async-start | bytes 1966080 | tf_op jit(solution)/shard_map/reduce_scatter | solution.py:174
  296.1 4.0 copy-start.35
  340.5 2.7 copy-start.11
  340.5 2.7 copy-start.9
  343.3 37.7 %copy-start.4 = (bf16[256,768]{1,0:T(8,128)(2,1)S(1)}, bf16[256,768]{1,0:T(8,128)(2,1)}, u32[]{:S(2)}) copy-start(bf16[256,768]{1,0:T(8,128)(2,1)} %reduce-scatter.16.cloned.1.call-done) | copy-start | bytes 1179652
  346.7 74.7 %all-gather.21.cloned.1.call-start = ((), (), s32[]{:S(2)}) async-start(), calls=%async_computation.19 | async-start | bytes 1966080 | tf_op jit(solution)/shard_map/all_gather | solution.py:170
  382.9 40.7 %copy-start.33 = (f32[256]{0:T(256)}, f32[256]{0:T(256)S(1)}, u32[]{:S(2)}) copy-start(f32[256]{0:T(256)S(1)} %fusion.67) | copy-start | bytes 3076
  385.1 87.7 %reduce-scatter.22.cloned.1.call-start = ((), (), s32[]{:S(2)}) async-start(), calls=%async_computation.20 | async-start | bytes 1966080 | tf_op jit(solution)/shard_map/reduce_scatter | solution.py:174
  438.5 70.7 %reduce-scatter.18.cloned.1.call-start = ((), (), s32[]{:S(2)}) async-start(), calls=%async_computation.16 | async-start | bytes 1966080 | tf_op jit(solution)/shard_map/reduce_scatter | solution.py:174
  442.2 67.0 %copy-start.6 = (bf16[256,768]{1,0:T(8,128)(2,1)S(1)}, bf16[256,768]{1,0:T(8,128)(2,1)}, u32[]{:S(2)}) copy-start(bf16[256,768]{1,0:T(8,128)(2,1)} %reduce-scatter.20.cloned.1.call-done) | copy-start | bytes 1179652
  442.3 105.9 %all-gather.23.cloned.1.call-start = ((), (), s32[]{:S(2)}) async-start(), calls=%async_computation.21 | async-start | bytes 1966080 | tf_op jit(solution)/shard_map/all_gather | solution.py:170
  511.8 3.3 copy-start.15
  511.9 76.9 %reduce-scatter.26.cloned.1.call-start = ((), (), s32[]{:S(2)}) async-start(), calls=%async_computation.23 | async-start | bytes 983040 | tf_op jit(solution)/shard_map/reduce_scatter | solution.py:174
  514.9 2.9 copy-start.41
  514.9 2.9 copy-start.42
  514.9 116.7 %reduce-scatter.30.cloned.1.call-start = ((), (), s32[]{:S(2)}) async-start(), calls=%async_computation.25 | async-start | bytes 3981312
  517.8 1.5 copy-start.7
  517.8 1.8 copy-start.14
  519.7 1.3 copy-start.12
  519.7 1.9 copy-start.36
  521.5 1.9 copy-start.10
  523.5 1.9 copy-start.37
  523.5 1.9 copy-start.45
  533.3 138.1 %reduce-scatter.28.cloned.1.call-start = ((), (), s32[]{:S(2)}) async-start(), calls=%async_computation.24 | async-start | bytes 1327104
  550.4 27.8 %copy-start.8 = (bf16[1024,768]{1,0:T(8,128)(2,1)S(1)}, bf16[1024,768]{1,0:T(8,128)(2,1)}, u32[]{:S(2)}) copy-start(bf16[1024,768]{1,0:T(8,128)(2,1)} %all-gather.23.cloned.1.call-done) | copy-start | bytes 4718596
  578.1 1.8 copy-start.34
  578.1 1.8 copy-start.38
  578.2 1.8 copy-start.39
  578.2 2.0 copy-start.40
  581.6 1.8 copy-start.13
  583.1 4.3 copy-start.44
  583.1 5.6 copy-start.27
  583.2 125.7 %reduce-scatter.24.cloned.1.call-start = ((), (), s32[]{:S(2)}) async-start(), calls=%async_computation.22 | async-start | bytes 1966080 | tf_op jit(solution)/shard_map/reduce_scatter | solution.py:174
  587.4 3.0 copy-start.28
  633.0 5.4 copy-start.24
  636.1 72.8 %copy-start.26 = (f32[256]{0:T(256)S(1)}, f32[256]{0:T(256)}, u32[]{:S(2)}) copy-start(f32[256]{0:T(256)} %copy-done.25) | copy-start | bytes 3076
  636.9 73.3 %copy-start.32 = (f32[256]{0:T(256)S(1)}, f32[256]{0:T(256)}, u32[]{:S(2)}) copy-start(f32[256]{0:T(256)} %copy-done.31) | copy-start | bytes 3076
  672.5 79.4 %copy-start.1 = (bf16[32,3]{0,1:T(4,128)(2,1)S(1)}, bf16[32,3]{0,1:T(4,128)(2,1)}, u32[]{:S(2)}) copy-start(bf16[32,3]{0,1:T(4,128)(2,1)} %param.23) | copy-start | bytes 580
Sparse Core Ops, SparseCore 0:
  10.5 26.5 all-gather.10
  39.3 36.5 all-gather.8
  97.5 34.0 reduce-scatter.13
  133.3 33.4 all-gather.14
  168.9 36.5 all-gather.12
  222.4 34.0 reduce-scatter.15
  259.9 36.0 all-gather.16
  298.2 35.9 all-gather.18
  346.8 34.0 reduce-scatter.19
  385.2 36.1 all-gather.20
  438.6 34.0 reduce-scatter.21
  474.9 34.2 reduce-scatter.17
  512.0 36.0 all-gather.22
  550.3 30.6 reduce-scatter.25
  584.3 47.2 reduce-scatter.29
  634.7 36.6 reduce-scatter.27
  673.6 35.2 reduce-scatter.23

commit v3 on v1

v3 whole, which is shorter than its diff:
```python
import functools
import types

import jax
import jax.numpy as jnp
from jax import lax
from jax.experimental import pallas as pl
from jax.experimental.pallas import tpu as pltpu
from jax.sharding import PartitionSpec as P

NB = 32
EPS = 1e-06

F32=jnp.float32; BF16=jnp.bfloat16
NEG=-1e30
NN=(((1,),(0,)),((),())); NT=(((1,),(1,)),((),())); TN=(((0,),(0,)),((),()))
def mm(a,b,dims=NN): return lax.dot_general(a,b,dims,preferred_element_type=F32)
TILE=256

def rows_of(i): return pl.ds(pl.multiple_of(i*TILE,TILE),TILE)

def split_heads(src, dst, heads):
    hd=dst.shape[2]
    for h in range(heads): dst[h]=src[:, h*hd:(h+1)*hd]

def bias_tiles(vecs, tiles, heads):
    key=lax.broadcasted_iota(jnp.int32,(TILE,TILE),0); qry=lax.broadcasted_iota(jnp.int32,(TILE,TILE),1)
    for h in range(heads):
        for d in range(3):
            wide=jnp.broadcast_to(vecs[h*3+d:h*3+d+1,:],(TILE,2*TILE))
            t=pltpu.roll(wide,0,1,stride=1,stride_axis=0)[:,:TILE]
            if d==0: t=jnp.where(qry>=key,t,NEG)
            tiles[h,d]=t

def fwd_attention(q3,k3,v3,vt3,out_t,lse,heads,nq,nk,tiles,kmask):
    hd=q3.shape[2]
    causal=tiles is not None
    def qblock(I,_):
        ri=rows_of(I)
        def kblock(J,carry):
            rj=rows_of(J)
            new=[]
            for h in range(heads):
                m,l,acc=carry[h]
                s=mm(k3[h,rj,:],q3[h,ri,:],NT)
                if causal:
                    s=s+tiles[h,jnp.minimum(I-J,2)]+kmask[rj,:1]
                m2=jnp.maximum(m,jnp.max(s,axis=0,keepdims=True))
                a=jnp.exp(m-m2); p=jnp.exp(s-m2)
                l2=l*a+jnp.sum(p,axis=0,keepdims=True)
                acc2=acc*a+mm(vt3[h,:,rj],p.astype(BF16))
                new.append((m2,l2,acc2))
            return tuple(new)
        init=tuple((jnp.full((1,TILE),NEG,F32),jnp.zeros((1,TILE),F32),jnp.zeros((hd,TILE),F32)) for _ in range(heads))
        res=lax.fori_loop(0,(I+1) if causal else nk//TILE,kblock,init)
        for h in range(heads):
            m,l,acc=res[h]
            out_t[h*hd:(h+1)*hd,ri]=acc/l
            lse[h:h+1,ri]=m+jnp.log(l)
        return 0
    lax.fori_loop(0,nq//TILE,qblock,0)

def bwd_attention(q3,k3,v3,kt3,do3,lse,delta,dqt,dk,dv,heads,nq,nk,tiles,kmask,dtile):
    hd=q3.shape[2]
    causal=tiles is not None
    dqt[...]=jnp.zeros_like(dqt)
    dk[...]=jnp.zeros_like(dk); dv[...]=jnp.zeros_like(dv)
    if causal: dtile[...]=jnp.zeros_like(dtile)
    def kblock(J,_):
        rj=rows_of(J)
        def qblock(I,_):
            ri=rows_of(I)
            for h in range(heads):
                s=mm(k3[h,rj,:],q3[h,ri,:],NT)
                if causal:
                    d=jnp.minimum(I-J,2)
                    s=s+tiles[h,d]+kmask[rj,:1]
                p=jnp.exp(s-lse[h:h+1,ri])
                dp=mm(v3[h,rj,:],do3[h,ri,:],NT)
                ds=(p*(dp-delta[h:h+1,ri])).astype(BF16)
                dv[h,rj,:]+=mm(p.astype(BF16),do3[h,ri,:])
                dk[h,rj,:]+=mm(ds,q3[h,ri,:])
                dqt[h*hd:(h+1)*hd,ri]+=mm(kt3[h,:,rj],ds)
                if causal: dtile[h,d]+=ds.astype(F32)
            return 0
        lax.fori_loop(J if causal else 0,nq//TILE,qblock,0)
        return 0
    lax.fori_loop(0,nk//TILE,kblock,0)

MESH_ID = pl.DeviceIdType.MESH


def layer_kernel(dims, names, *refs):
    D, Hn, hd, FFL, N, NE, NQ, NK, g, part = dims
    s = types.SimpleNamespace(**dict(zip(names, refs)))
    hw = Hn * hd
    o_qkv, o_out, o_cq, o_co, o_ckv, o_ff, o_up, o_down = (
        0, 3 * hw, 4 * hw, 5 * hw, 6 * hw, 8 * hw, 8 * hw + FFL, 8 * hw + 2 * FFL,
    )
    dp, z = lax.axis_index("dp"), lax.axis_index("mp")
    a, low = dp // g, dp % g
    c, r = a % 2, a // 2
    p, zb = z // 2, z % 2
    j = 2 * c + zb
    rx, ry = r + 1 - 2 * (r % 2), (r + 2) % 4
    rd = 3 - r
    z1, z2 = z + 1 - 2 * zb, (z + 2) % 4
    stay = c == p
    moved = c != p

    def device(r_, c_, z_):
        return {"dp": (2 * r_ + c_) * g + low, "mp": z_}

    sibling, across = device(r, 1 - c, z), device(r, c, z1)
    home = device(r, p, j)
    x_chip, y_chip = device(rx, c, z), device(ry, c, z)
    counter = [0]

    def slots(k):
        counter[0] += k
        return counter[0] - k

    def remote(src, dst, dev, send=None, recv=None):
        send = slots(1) if send is None else send
        recv = slots(1) if recv is None else recv
        return pltpu.make_async_remote_copy(
            src_ref=src, dst_ref=dst, send_sem=s.sems.at[send], recv_sem=s.sems.at[recv],
            device_id=dev, device_id_type=MESH_ID,
        )

    def local(src, dst):
        return pltpu.make_async_copy(src, dst, s.sems.at[slots(1)])

    unsent = []

    def go(copy):
        copy.start()
        unsent.append(copy)
        return copy

    def block(i, n):
        return pl.ds(pl.multiple_of(i * n, n), n)

    def order(k):
        return 2 * ((c + k % 2) % 2) + (zb + k // 2) % 2

    barrier = pltpu.get_barrier_semaphore()
    peers = [device(r, (c + dc) % 2, (z + dz) % 4) for dz in range(4) for dc in range(2) if dz or dc] + [x_chip, y_chip]
    for peer in peers:
        pl.semaphore_signal(barrier, inc=1, device_id=peer, device_id_type=MESH_ID)
    pl.semaphore_wait(barrier, len(peers))

    def swap(src, dst):
        far, near = remote(src, dst, home), local(src, dst)

        @pl.when(moved)
        def _():
            far.start()

        @pl.when(stay)
        def _():
            near.start()

        def wait():
            @pl.when(moved)
            def _():
                far.wait()

            @pl.when(stay)
            def _():
                near.wait()

        return wait

    rows_a = D // 8

    def weights_start(col, wide):
        src = s.wpack.at[:, pl.ds(col, wide)]
        near = local(src, s.W.at[block(a, rows_a), pl.ds(col, wide)])
        beside = remote(src, s.W.at[block(a, rows_a), pl.ds(col, wide)], sibling)
        base = slots(2)
        far = remote(src, s.W.at[block(a, rows_a), pl.ds(col, wide)], device(r, p, z2), recv=base + c)

        @pl.when(stay)
        def _():
            near.start()

        @pl.when(moved)
        def _():
            beside.start()

        go(far)

        def wait():
            @pl.when(stay)
            def _():
                near.wait()
                beside.wait_recv()

            @pl.when(moved)
            def _():
                beside.wait_send()
                for k in range(2):
                    remote(src, s.W.at[block(2 * r + k, rows_a), pl.ds(col, wide)], sibling, 0, base + k).wait_recv()

        half = wide // 2
        A, B = pl.ds(col, half), pl.ds(col + half, half)
        chip = 2 * rows_a

        def first_hop():
            wait()
            hop_a = go(remote(s.W.at[block(r, chip), A], s.W.at[block(r, chip), A], x_chip))
            hop_b = go(remote(s.W.at[block(r, chip), B], s.W.at[block(r, chip), B], y_chip))

            def second_hop():
                hop_a.wait_recv()
                two = block(r // 2, 2 * chip)
                last = [go(remote(s.W.at[two, A], s.W.at[two, A], y_chip))]
                hop_b.wait_recv()
                for q in (r, ry):
                    last.append(go(remote(s.W.at[block(q, chip), B], s.W.at[block(q, chip), B], x_chip)))

                def finish():
                    for copy in last:
                        copy.wait_recv()

                return finish

            return second_hop

        return first_hop

    chip = 2 * rows_a

    def grads_start(col, wide):
        half = wide // 2
        A, B = pl.ds(col, half), pl.ds(col + half, half)
        hA = pl.ds(col // 2, half)
        G = s.dW
        one = [
            go(remote(G.at[block(ry // 2, 2 * chip), A], s.ra1.at[:, hA], y_chip)),
            go(remote(G.at[block(rx, chip), B], s.rb1.at[0, :, hA], x_chip)),
            go(remote(G.at[block(rd, chip), B], s.rb1.at[1, :, hA], x_chip)),
        ]

        def add(dst, src):
            n = 96
            for q in range(dst.shape[0] // n):
                w = pl.ds(q * n, n)
                dst[w, :] = (dst[w, :].astype(F32) + src[w, :].astype(F32)).astype(BF16)

        def second():
            one[0].wait_recv()
            add(G.at[block(r // 2, 2 * chip), A], s.ra1.at[:, hA])
            two = [go(remote(G.at[block(rx, chip), A], s.ra2.at[:, hA], x_chip))]
            one[1].wait_recv()
            add(G.at[block(r, chip), B], s.rb1.at[0, :, hA])
            one[2].wait_recv()
            add(G.at[block(ry, chip), B], s.rb1.at[1, :, hA])
            two.append(go(remote(G.at[block(ry, chip), B], s.rb2.at[:, hA], y_chip)))

            def third():
                C = pl.ds(col, wide)
                two[0].wait_recv()
                add(G.at[block(r, chip), A], s.ra2.at[:, hA])
                two[1].wait_recv()
                add(G.at[block(r, chip), B], s.rb2.at[:, hA])
                near = remote(G.at[block(2 * r + 1 - c, rows_a), C], s.rzs.at[:, C], sibling)
                recv = slots(1)
                got = remote(G.at[block(2 * r, rows_a), C], s.rzz.at[:, C], device(r, 0, z2), 0, recv)
                far = [
                    remote(G.at[block(2 * r + k, rows_a), C], s.rzz.at[:, C], device(r, k, z2), None, recv)
                    for k in range(2)
                ]

                @pl.when(stay)
                def _():
                    near.start()
                    s.rzs[:, C] = G[block(a, rows_a), C]

                @pl.when(moved)
                def _():
                    for copy in far:
                        copy.start()

                def finish():
                    @pl.when(stay)
                    def _():
                        near.wait_send()

                    @pl.when(moved)
                    def _():
                        near.wait_recv()
                        for copy in far:
                            copy.wait_send()

                    got.wait_recv()
                    s.gw[:, C] = s.rzs[:, C].astype(F32) + s.rzz[:, C].astype(F32)

                return finish

            return third

        return second

    def gather(buf, n):
        own = buf.at[block(j, n), :]
        side = remote(own, own, sibling)
        cross = remote(own, own, across)
        there = buf.at[block(2 * c + 1 - zb, n), :]
        fwd = remote(there, there, sibling)
        cross.start()
        side.start()

        def forward():
            cross.wait_recv()
            fwd.start()

        def far():
            fwd.wait_recv()
            for copy in (side, cross, fwd):
                copy.wait_send()

        return types.SimpleNamespace(side=side.wait_recv, forward=forward, far=far)

    def each_block(h, body):
        h.side()
        lax.fori_loop(0, 2, lambda k, _: (body(order(k)), 0)[1], 0)
        h.forward()
        h.far()
        lax.fori_loop(2, 4, lambda k, _: (body(order(k)), 0)[1], 0)

    def scatter(fn, bufs, res):
        s0, s1, zs, r0, r1, rz = bufs
        s0[...] = fn(order(3)).astype(BF16)
        d0 = remote(s0, r0, sibling)
        d0.start()
        res[...] = fn(order(2))
        d0.wait_recv()
        zs[...] = (res[...] + r0[...].astype(F32)).astype(BF16)
        dz = remote(zs, rz, across)
        dz.start()
        s1[...] = fn(order(1)).astype(BF16)
        d1 = remote(s1, r1, sibling)
        d1.start()
        res[...] = fn(order(0))

        def finish():
            d1.wait_recv()
            dz.wait_recv()
            res[...] += r1[...].astype(F32) + rz[...].astype(F32)
            for copy in (d0, d1, dz):
                copy.wait_send()

        return finish

    CH = 64

    def chunks(n, body, init=0):
        return lax.fori_loop(0, n // CH, lambda i, v: body(pl.ds(pl.multiple_of(i * CH, CH), CH), v), init)

    gains = [s.gains[k : k + 1, :] for k in range(3)]

    def norm_rows(v, which, inv_ref, w, dst, dst_at):
        inv = lax.rsqrt(jnp.sum(v * v, axis=1, keepdims=True) / D + EPS)
        inv_ref[w, :] = jnp.broadcast_to(inv, (CH, 128))
        dst[dst_at, :] = (v * inv * gains[which]).astype(BF16)

    def own_rows(w, n):
        return pl.ds(pl.multiple_of(j * n + w.start, CH), CH)

    def norm_back_rows(d, v, which, inv):
        scaled = d * gains[which]
        dotted = jnp.sum(scaled * v, axis=1, keepdims=True)
        back = inv * scaled - v * (inv * inv * inv * dotted / D)
        return back, jnp.sum(d * v * inv, axis=0, keepdims=True)

    zero_gain = jnp.zeros((1, D), F32)

    wait_x = swap(s.x, s.XN)
    first_hop_s = weights_start(0, 4 * hw)
    tab = go(remote(s.table, s.table_in, device(r, c, z2)))
    lens = go(remote(s.length, s.length_in, sibling))
    lens.wait_recv()
    s.len_row[...] = jnp.where(stay, s.length[...], s.length_in[...])
    tab.wait_recv()
    table = jnp.where(stay, s.table[...], s.table_in[...])
    span = 2 * TILE
    ids = lax.broadcasted_iota(jnp.int32, (128, span), 0)

    def onehot(row):
        return (ids == s.buckets[row : row + 1, :]).astype(F32)

    for k in range(3):
        s.vecs[8 * k : 8 * k + 8, :] = mm(table, onehot(k))
    key_at = lax.broadcasted_iota(jnp.int32, (TILE, TILE), 0)
    query_at = lax.broadcasted_iota(jnp.int32, (TILE, TILE), 1)
    for h in range(Hn):
        for k in range(3):
            wide = jnp.broadcast_to(s.vecs[8 * k + h : 8 * k + h + 1, :], (TILE, span))
            tile = pltpu.roll(wide, 0, 1, stride=1, stride_axis=0)[:, :TILE]
            s.tiles[h, k] = jnp.where(query_at >= key_at, tile, NEG) if k == 0 else tile
    length = s.len_row[0:1, :]
    s.kmask[...] = jnp.where(
        lax.broadcasted_iota(jnp.int32, s.kmask.shape, 0).astype(F32) < length, 0.0, NEG
    )
    wait_x()
    wait_e = swap(s.enc, s.EN)
    first_hop_c = weights_start(4 * hw, 4 * hw)

    def norm_one(w, _):
        norm_rows(s.XN[w, :].astype(F32), 0, s.inv1, w, s.FIRST, own_rows(w, N))
        return 0

    chunks(N, norm_one)
    ga = gather(s.FIRST, N)
    second_hop_s = first_hop_s()
    wait_o = swap(s.og, s.ON)
    wait_e()
    s.ENC[block(j, NE), :] = s.EN[...]
    ge = gather(s.ENC, NE)
    done_s = second_hop_s()
    first_hop_f = weights_start(8 * hw, 3 * FFL)
    done_s()
    s.WO[...] = s.W[:, o_out : o_out + hw]

    def split(dst, value, rows):
        for h in range(Hn):
            dst[h, rows, :] = value[:, h * hd : (h + 1) * hd]

    def project_one(i):
        w = block(i, N)
        y = mm(s.FIRST[w, :], s.W[:, : 3 * hw]).astype(BF16)
        for k, dst in enumerate((s.q3, s.k3, s.v3)):
            split(dst, y[:, k * hw : (k + 1) * hw], w)

    each_block(ga, project_one)
    second_hop_c = first_hop_c()
    for h in range(Hn):
        s.t3[h] = s.v3[h].T
    fwd_attention(s.q3, s.k3, s.v3, s.t3, s.out_t, s.lse, Hn, NQ, NQ, s.tiles, s.kmask)
    done_c = second_hop_c()
    s.MIX[...] = s.out_t[...].T.astype(BF16)
    end = scatter(lambda i: mm(s.MIX[block(i, N), :], s.WO[...], NT), (s.s0, s.s1, s.zs, s.a0, s.a1, s.az), s.res)
    wait_o()
    own_pos = lax.broadcasted_iota(jnp.int32, (N, 128), 0) + j * N
    s.ok[...] = (own_pos.astype(F32) < length).astype(F32)

    def mask_rows(w, _):
        s.GF[own_rows(w, N), :] = (s.ON[w, :].astype(F32) * s.ok[w, :1]).astype(BF16)
        return 0

    chunks(N, mask_rows)
    done_c()
    s.WCO[...] = s.W[:, o_co : o_co + hw]

    def project_enc(i):
        w = block(i, NE)
        y = mm(s.ENC[w, :], s.W[:, o_ckv : o_ckv + 2 * hw]).astype(BF16)
        split(s.ck3, y[:, :hw], w)
        split(s.cv3, y[:, hw:], w)

    each_block(ge, project_enc)
    end()

    def norm_two(w, _):
        v = s.XN[w, :].astype(F32) + s.res[w, :]
        s.MID[w, :] = v
        norm_rows(v, 1, s.inv2, w, s.SECOND, own_rows(w, N))
        return 0

    chunks(N, norm_two)
    gs = gather(s.SECOND, N)
    second_hop_f = first_hop_f()
    gg = gather(s.GF, N)
    for h in range(Hn):
        s.ct3[h] = s.cv3[h].T

    def project_two(i):
        w = block(i, N)
        split(s.cq3, mm(s.SECOND[w, :], s.W[:, o_cq : o_cq + hw]).astype(BF16), w)

    each_block(gs, project_two)
    fwd_attention(s.cq3, s.ck3, s.cv3, s.ct3, s.out_t2, s.lse2, Hn, NQ, NK, None, None)
    done_f = second_hop_f()
    s.MIX2[...] = s.out_t2[...].T.astype(BF16)
    end = scatter(lambda i: mm(s.MIX2[block(i, N), :], s.WCO[...], NT), (s.s0, s.s1, s.zs, s.b0, s.b1, s.bz), s.res)
    gg.side()
    gg.forward()
    end()

    def norm_three(w, _):
        v = s.MID[w, :] + s.res[w, :]
        s.LAT[w, :] = v
        norm_rows(v, 2, s.inv3, w, s.THIRD, own_rows(w, N))
        return 0

    chunks(N, norm_three)
    gt = gather(s.THIRD, N)
    gg.far()
    done_f()
    root = 0.7978845608028654
    SUB = 128

    def feed(i):
        def sub(u, _):
            w = pl.ds(pl.multiple_of(i * N + u * SUB, SUB), SUB)
            t = s.THIRD[w, :]
            gate = mm(t, s.W[:, o_ff : o_ff + FFL])
            up = mm(t, s.W[:, o_up : o_up + FFL])
            dh = mm(s.GF[w, :], s.W[:, o_down : o_down + FFL])
            sq = gate * gate
            th = jnp.tanh(root * gate * (1.0 + 0.044715 * sq))
            half = 0.5 * (1.0 + th)
            act = gate * half
            slope = half + 0.5 * gate * (1.0 - th * th) * root * (1.0 + 3 * 0.044715 * sq)
            s.HID[w, :] = (act * up).astype(BF16)
            s.DGU[w, :FFL] = (dh * up * slope).astype(BF16)
            s.DGU[w, FFL:] = (dh * act).astype(BF16)
            return 0

        lax.fori_loop(0, N // SUB, sub, 0)

    each_block(gt, feed)
    end = scatter(
        lambda i: mm(s.DGU[block(i, N), :], s.W[:, o_ff : o_ff + 2 * FFL], NT), (s.s0, s.s1, s.zs, s.a0, s.a1, s.az), s.res
    )
    end_out = scatter(
        lambda i: mm(s.HID[block(i, N), :], s.W[:, o_down : o_down + FFL], NT),
        (s.t0, s.t1, s.ts, s.b0, s.b1, s.bz), s.res2,
    )

    def weight_grad(left, right, col, n):
        def step(q, _):
            m = pl.ds(pl.multiple_of(q * 256, 256), 256)
            s.dW[m, pl.ds(col, n)] = mm(left[:, m], right, TN).astype(BF16)
            return 0

        lax.fori_loop(0, D // 256, step, 0)

    weight_grad(s.GF, s.HID[...], o_down, FFL)
    weight_grad(s.THIRD, s.DGU[...], o_ff, 2 * FFL)
    grad_f = grads_start(8 * hw, 3 * FFL)
    end()

    def back_three(w, acc):
        back, part_gain = norm_back_rows(s.res[w, :], s.LAT[w, :], 2, s.inv3[w, :1])
        d = s.GF[own_rows(w, N), :].astype(F32) + back
        s.GR[w, :] = d
        s.DL[own_rows(w, N), :] = d.astype(BF16)
        return acc + part_gain

    gain_three = chunks(N, back_three, zero_gain)
    gd = gather(s.DL, N)
    end_out()

    def put_out(w, _):
        s.LO[w, :] = (s.LAT[w, :] + s.res2[w, :]).astype(BF16)
        return 0

    chunks(N, put_out)
    wait_lo = swap(s.LO, s.lo)

    for h in range(Hn):
        s.ct3[h] = s.ck3[h].T

    def back_heads(src, weight, out_t):
        def body(i):
            w = block(i, N)
            y = mm(src[w, :], weight[...]).astype(BF16)
            split(s.do3, y, w)
            yt = y.astype(F32).T
            for h in range(Hn):
                hh = slice(h * hd, (h + 1) * hd)
                s.delta[h : h + 1, w] = jnp.sum(yt[hh, :] * out_t[hh, w], axis=0, keepdims=True)

        return body

    each_block(gd, back_heads(s.DL, s.WCO, s.out_t2))
    grad_f = grad_f()
    bwd_attention(
        s.cq3, s.ck3, s.cv3, s.ct3, s.do3, s.lse2, s.delta, s.dqt, s.dk3, s.dv3, Hn, NQ, NK, None, None, None
    )
    grad_f = grad_f()
    s.DCQ[...] = s.dqt[...].T.astype(BF16)
    end = scatter(
        lambda i: mm(s.DCQ[block(i, N), :], s.W[:, o_cq : o_cq + hw], NT), (s.s0, s.s1, s.zs, s.a0, s.a1, s.az), s.res
    )
    for h in range(Hn):
        s.DCKV[:, h * hd : (h + 1) * hd] = s.dk3[h, :NK, :].astype(BF16)
        s.DCKV[:, hw + h * hd : hw + (h + 1) * hd] = s.dv3[h, :NK, :].astype(BF16)
    end_enc = scatter(
        lambda i: mm(s.DCKV[block(i, NE), :], s.W[:, o_ckv : o_ckv + 2 * hw], NT),
        (s.e0, s.e1, s.es, s.f0, s.f1, s.fz), s.rese,
    )
    weight_grad(s.SECOND, s.DCQ[...], o_cq, hw)
    weight_grad(s.DL, s.MIX2[...], o_co, hw)
    weight_grad(s.ENC, s.DCKV[...], o_ckv, 2 * hw)
    grad_c = grads_start(4 * hw, 4 * hw)
    end()

    def back_two(w, acc):
        back, part_gain = norm_back_rows(s.res[w, :], s.MID[w, :], 1, s.inv2[w, :1])
        d = s.GR[w, :] + back
        s.GR[w, :] = d
        s.GF[own_rows(w, N), :] = d.astype(BF16)
        return acc + part_gain

    gain_two = chunks(N, back_two, zero_gain)
    gm = gather(s.GF, N)
    end_enc()
    s.EO[...] = s.rese[...].astype(BF16)
    wait_eo = swap(s.EO, s.EO_in)
    for h in range(Hn):
        s.t3[h] = s.k3[h].T
    grad_f()

    each_block(gm, back_heads(s.GF, s.WO, s.out_t))
    grad_c = grad_c()
    bwd_attention(
        s.q3, s.k3, s.v3, s.t3, s.do3, s.lse, s.delta, s.dqt, s.dk3, s.dv3, Hn, NQ, NQ, s.tiles, s.kmask, s.dtile
    )
    grad_c = grad_c()
    s.DQKV[:, :hw] = s.dqt[...].T.astype(BF16)
    for h in range(Hn):
        s.DQKV[:, hw + h * hd : hw + (h + 1) * hd] = s.dk3[h].astype(BF16)
        s.DQKV[:, 2 * hw + h * hd : 2 * hw + (h + 1) * hd] = s.dv3[h].astype(BF16)
    end = scatter(
        lambda i: mm(s.DQKV[block(i, N), :], s.W[:, : 3 * hw], NT), (s.s0, s.s1, s.zs, s.a0, s.a1, s.az), s.res
    )
    weight_grad(s.FIRST, s.DQKV[...], o_qkv, 3 * hw)
    weight_grad(s.GF, s.MIX[...], o_out, hw)
    grad_s = grads_start(0, 4 * hw)
    end()

    def back_one(w, acc):
        back, part_gain = norm_back_rows(s.res[w, :], s.XN[w, :].astype(F32), 0, s.inv1[w, :1])
        s.LO2[w, :] = (s.GR[w, :] + back).astype(BF16)
        return acc + part_gain

    gain_one = chunks(N, back_one, zero_gain)
    wait_dg = swap(s.LO2, s.LO2_in)
    grad_c()

    s.small[...] = jnp.zeros_like(s.small)
    s.small[0:1, :D] = gain_one
    s.small[1:2, :D] = gain_two
    s.small[2:3, :D] = gain_three
    flip = (key_at + query_at == TILE - 1).astype(F32)
    blank = jnp.zeros((TILE, TILE), F32)
    head_row = lax.broadcasted_iota(jnp.int32, (16, span), 0)
    bias_rows = jnp.zeros((16, 128), F32)
    for k in range(3):
        diag = jnp.zeros((16, span), F32)
        for h in range(Hn):
            turned = lax.dot_general(
                flip, s.dtile[h, k], NN, precision=lax.Precision.HIGHEST, preferred_element_type=F32
            )
            lined = pltpu.roll(jnp.concatenate([turned, blank], axis=1), 0, 1, stride=1, stride_axis=0)
            diag = jnp.where(head_row == Hn * j + h, jnp.sum(lined, axis=0, keepdims=True), diag)
        bias_rows = bias_rows + lax.dot_general(
            diag, onehot(3 + k), NT, precision=lax.Precision.HIGHEST, preferred_element_type=F32
        )
    s.small[:, D:] = bias_rows
    for k, peer in enumerate((sibling, across, device(r, c, z2), x_chip, y_chip)):
        s.small_out[k] = s.small[...]
        hop = remote(s.small_out.at[k], s.small_in.at[k], peer)
        hop.start()
        if k == 0:
            grad_s = grad_s()
        hop.wait()
        s.small[...] += s.small_in[k]
    s.sm[...] = s.small[...]
    grad_s = grad_s()
    wait_eo()
    s.eg[...] = s.EO_in[...].astype(F32)
    wait_dg()
    s.dg[...] = s.LO2_in[...].astype(F32)
    grad_s()
    wait_lo()
    for copy in unsent:
        copy.wait_send()
    assert counter[0] <= part, counter[0]


def layer_call(wpack, x, enc, og, gains, table, length, buckets, dims):
    D, Hn, hd, FFL, N, NE, NQ, NK, g, part = dims
    hw = Hn * hd
    cols = wpack.shape[1]
    vm, any_ = pl.BlockSpec(memory_space=pltpu.VMEM), pl.BlockSpec(memory_space=pl.ANY)
    ins = dict(wpack=any_, x=any_, enc=any_, og=any_, gains=vm, table=vm, length=vm, buckets=vm)
    outs = dict(
        lo=((N, D), BF16, any_), dg=((N, D), F32, vm), eg=((NE, D), F32, vm),
        gw=((wpack.shape[0], cols), F32, vm), sm=((16, D + 128), F32, vm),
    )
    sc = {}

    def add(dtype, **shapes):
        for name, shape in shapes.items():
            sc[name] = pltpu.VMEM(shape, dtype)

    add(BF16, W=(D, cols), dW=(D, cols), WO=(D, hw), WCO=(D, hw))
    half = cols // 2
    add(BF16, ra1=(D // 2, half), rb1=(2, D // 4, half), ra2=(D // 4, half), rb2=(D // 4, half))
    add(BF16, rzs=(D // 8, cols), rzz=(D // 8, cols))
    add(BF16, **{k: (NQ, D) for k in ("FIRST", "SECOND", "THIRD", "GF", "DL")}, ENC=(NK, D))
    add(BF16, **{k: (N, D) for k in ("s0", "s1", "zs", "t0", "t1", "ts", "a0", "a1", "az", "b0", "b1", "bz")})
    add(BF16, **{k: (NE, D) for k in ("e0", "e1", "es", "f0", "f1", "fz", "EN", "EO", "EO_in")})
    add(BF16, **{k: (N, D) for k in ("XN", "ON", "LO", "LO2", "LO2_in")})
    add(F32, **{k: (N, D) for k in ("MID", "LAT", "GR", "res", "res2")}, rese=(NE, D))
    add(F32, inv1=(N, 128), inv2=(N, 128), inv3=(N, 128), ok=(N, 128))
    add(BF16, q3=(Hn, NQ, hd), k3=(Hn, NQ, hd), v3=(Hn, NQ, hd), cq3=(Hn, NQ, hd), ck3=(Hn, NK, hd), cv3=(Hn, NK, hd))
    add(BF16, do3=(Hn, NQ, hd), t3=(Hn, hd, NQ), ct3=(Hn, hd, NK))
    add(F32, out_t=(hw, NQ), out_t2=(hw, NQ), dqt=(hw, NQ), lse=(8, NQ), lse2=(8, NQ), delta=(8, NQ))
    add(F32, dk3=(Hn, NQ, hd), dv3=(Hn, NQ, hd))
    add(BF16, MIX=(NQ, hw), MIX2=(NQ, hw), HID=(NQ, FFL), DGU=(NQ, 2 * FFL), DCQ=(NQ, hw), DCKV=(NK, 2 * hw), DQKV=(NQ, 3 * hw))
    add(F32, tiles=(Hn, 3, TILE, TILE), dtile=(Hn, 3, TILE, TILE), kmask=(NQ, 128), vecs=(24, 2 * TILE))
    add(F32, table_in=(8, 128), length_in=(8, 128), len_row=(8, 128))
    add(F32, small=(16, D + 128), small_out=(5, 16, D + 128), small_in=(5, 16, D + 128))
    names = list(ins) + list(outs) + list(sc) + ["sems"]
    return pl.pallas_call(
        functools.partial(layer_kernel, dims, names),
        out_shape=[jax.ShapeDtypeStruct(o[0], o[1]) for o in outs.values()],
        in_specs=list(ins.values()),
        out_specs=[o[2] for o in outs.values()],
        scratch_shapes=list(sc.values()) + [pltpu.SemaphoreType.DMA((part,))],
        compiler_params=pltpu.CompilerParams(collective_id=0, has_side_effects=True, vmem_limit_bytes=67043328),
        name="layer",
    )(wpack, x, enc, og, gains, table, length, buckets)


def exchange(value, step, size):
    return lax.ppermute(value, "dp", [(i, i ^ step) for i in range(size)])


def per_device_fast(
    decoder_in, encoder_out, seq_lengths, rel_buckets, norm_gains, rel_bias,
    self_query, self_key, self_value, self_out, cross_query, cross_key, cross_value, cross_out,
    gate_weight, up_weight, down_weight, out_grad,
):
    width = decoder_in.shape[1]
    heads, w, f = rel_bias.shape[1], self_query.shape[1], gate_weight.shape[1]
    size = lax.axis_size("dp")
    g = size // 8
    rows, erows = decoder_in.shape[0], encoder_out.shape[0]
    slot = rel_buckets.shape[0]
    wpack = jnp.concatenate(
        [self_query, self_key, self_value, self_out.T, cross_query, cross_out.T, cross_key, cross_value,
         gate_weight, up_weight, down_weight.T], axis=1,
    )
    step = 1
    while step < g:
        other = exchange(wpack, step, size)
        upper = (lax.axis_index("dp") // step) % 2
        wpack = jnp.where(upper == 1, jnp.concatenate([other, wpack], 0), jnp.concatenate([wpack, other], 0))
        step *= 2
    far = rel_buckets[TILE : 2 * TILE]
    none = jnp.full((TILE,), -1, jnp.int32)
    near, after = rel_buckets[:TILE], rel_buckets[TILE : 2 * TILE]
    last = jnp.broadcast_to(rel_buckets[slot - 1 :], (TILE,))
    buckets = jnp.stack(
        [jnp.concatenate(v) for v in (
            (near, far), (after, near), (last, last),
            (none[1:], near, none[:1]), (rel_buckets[1 : 2 * TILE], none[:1]), (last, last), (none, none), (none, none),
        )]
    )
    table = jnp.pad(rel_bias.astype(F32).T, ((0, 8 - heads), (0, 128 - NB)))
    length = jnp.broadcast_to(seq_lengths.astype(F32)[:, None], (8, 128))
    gains = jnp.pad(norm_gains.astype(F32), ((0, 5), (0, 0)))
    dims = (width, heads, w // heads, f, rows, erows, 4 * rows, 4 * erows, g, 256)
    lo, dg, eg, gw, sm = layer_call(wpack, decoder_in, encoder_out, out_grad, gains, table, length, buckets, dims)
    step = g // 2
    while step >= 1:
        upper = (lax.axis_index("dp") // step) % 2
        n = gw.shape[0] // 2
        keep = jnp.where(upper == 1, gw[n:], gw[:n])
        give = jnp.where(upper == 1, gw[:n], gw[n:])
        gw = keep + exchange(give, step, size)
        sm = sm + exchange(sm, step, size)
        step //= 2
    hw = w
    return (
        lo, dg, eg, sm[:3, :width], sm[: 4 * heads, width : width + NB].T,
        gw[:, :hw], gw[:, hw : 2 * hw], gw[:, 2 * hw : 3 * hw], gw[:, 3 * hw : 4 * hw].T,
        gw[:, 4 * hw : 5 * hw], gw[:, 6 * hw : 7 * hw], gw[:, 7 * hw : 8 * hw], gw[:, 5 * hw : 6 * hw].T,
        gw[:, 8 * hw : 8 * hw + f], gw[:, 8 * hw + f : 8 * hw + 2 * f], gw[:, 8 * hw + 2 * f :].T,
    )


def solution(mesh):
    return jax.shard_map(
        per_device_fast,
        mesh=mesh,
        in_specs=(
            P(("dp", "mp"), None),
            P(("dp", "mp"), None),
            P("dp"),
            P(),
            P(),
            P(None, "mp"),
            P("dp", "mp"),
            P("dp", "mp"),
            P("dp", "mp"),
            P("mp", "dp"),
            P("dp", "mp"),
            P("dp", "mp"),
            P("dp", "mp"),
            P("mp", "dp"),
            P("dp", "mp"),
            P("dp", "mp"),
            P("mp", "dp"),
            P(("dp", "mp"), None),
        ),
        out_specs=(
            P(("dp", "mp"), None),
            P(("dp", "mp"), None),
            P(("dp", "mp"), None),
            P(),
            P(),
            P("dp", "mp"),
            P("dp", "mp"),
            P("dp", "mp"),
            P("mp", "dp"),
            P("dp", "mp"),
            P("dp", "mp"),
            P("dp", "mp"),
            P("mp", "dp"),
            P("dp", "mp"),
            P("dp", "mp"),
            P("mp", "dp"),
        ),
        check_vma=False,
    )
```

time: 760 us -> 270 us (0.36); the launches traced: 750 us -> 270 us
  waiting for transfers between devices: 505 us -> 0 us
  Pallas kernels: 51.6 us -> 250 us
  matrix products: 67 us -> 0 us
  blocking collectives: 55.1 us -> 0 us
  other arithmetic: 27.9 us -> 1.29 us
  between operations: 15.7 us -> 1.42 us
  local copies, waits for them, and re-layouts: 27.2 us -> 16.6 us
    all_gather x8 -> x0, waiting for transfers between devices: 229 us -> none  [the longest x6 191 us: full_rows(): return lax.all_gather(share, 'mp', axis=0, tiled=True)]
    reduce_scatter x7 -> x0, waiting for transfers between devices: 199 us -> none  [share_rows(): lax.psum_scatter(total.astype(BF16), 'mp', scatter_dimension=0, tiled=True)]
    pallas_call x4 -> x1, Pallas kernels: 51.6 us -> 250 us  [layer_call(): pl.pallas_call(functools.partial(layer_kernel, dims, names), out_shape=[j...]
    unnamed x19 -> x0, waiting for transfers between devices: 75.9 us -> none
    dot_general x26 -> x0, matrix products: 67 us -> none  [the longest x24 66.3 us: dot(): return lax.dot_general(a, b, dims, preferred_element_type=F32)]
    psum x1 -> x0, blocking collectives: 39.5 us -> none  [per_device(): lax.psum((jnp.stack([gain_one, gain_two, gain_three]), bias_table), ('dp'...]
    all_gather x1 -> x0, blocking collectives: 15.6 us -> none  [full_rows(): return lax.all_gather(share, 'mp', axis=0, tiled=True)]
    convert_element_type x12 -> x0, other arithmetic: 14.6 us -> none  [the longest x3 5.79 us: norm_forward(): return ((stream * inverse[:, None] * gain[None, :]).astype(BF16), inverse)]
  transfers between devices with their start and end apart: 17 -> 0, of which waited for: 16 -> 0; matrix products, arithmetic and copies ran while one was open for 10% -> 0% of each run, Pallas kernels for 2% -> 0%
where the time goes in v3:
time: 270 us
  Pallas kernels  250 us (93%)
  local copies, waits for them, and re-layouts  16.6 us (6%)
    pallas_call x1, Pallas kernels, layer_call(): pl.pallas_call(functools.partial(layer_kernel, dims, names), out_shape=[j...  250 us
    unnamed x21, local copies, waits for them, and re-layouts  5.68 us

profile of v3, /device:TPU:1, one launch (start us, length us, event | category | flops | bytes accessed | tf_op | source)
XLA Modules:
  0.0 269.6 jit_solution(7138229591278464362)
XLA Ops:
  0.6 0.0 copy-start.5
  0.7 0.0 copy-start.6
  0.7 0.0 copy-start.4
  0.7 0.0 slice-start
  0.7 0.9 copy.34
  1.6 0.9 copy.35
  2.5 1.9 concatenate.19.refs_0_
  4.4 0.0 copy-done.5
  4.4 0.6 pad_convert_fusion.refs_4_
  5.1 0.0 copy-done.6
  5.1 0.6 pad_convert_fusion.1.refs_5_
  6.3 0.6 broadcast_in_dim.16.refs_6_
  6.9 0.0 copy-done.4
  6.9 0.1 slice.60
  7.0 0.1 pad_add_fusion.1
  7.1 0.6 slice.58
  7.7 0.6 broadcast_in_dim.18
  8.3 0.7 concatenate.22
  9.0 0.0 slice-done
  9.0 0.6 stack.28.refs_7_
  9.6 250.3 %layer.1 = (bf16[256,768]{1,0:T(8,128)(2,1)}, f32[256,768]{1,0:T(8,128)}, f32[128,768]{1,0:T(8,128)}, f32[96,3072]{1,0:T(8,128)}, f32[16,896]{1,0:T(8,128)}) custom-call(bf16[96,3072]{1,0:T(8,128)(2,1)} %concatenate.19.refs_0_, bf16[256,768]{1,0:T(8,128)(2,1)} %refs_1_.1, bf16[128,768]{1,0:T(8,128)(2,1)} %refs_2_.1, bf16[256,768]{1,0:T(8,128)(2,1)} %refs_3_.1, ...), custom_call_target="tpu_custom_call" | custom-call | tf_op jit(solution)/shard_map/layer/pallas_call | solution.py:721
  260.0 0.0 copy-start
  260.0 1.4 slice.61
  261.4 1.3 slice_bitcast_fusion.3
  262.7 2.2 slice_bitcast_fusion.1
  264.9 0.0 copy-start.3
  264.9 0.0 copy-start.1
  264.9 0.7 copy.36
  265.7 0.7 copy.37
  266.4 0.0 copy-done
  266.4 0.8 slice_bitcast_fusion
  267.2 0.0 copy-done.3
  267.2 0.0 copy-start.2
  267.2 0.7 copy.42
  268.0 0.0 copy-done.1
  268.0 0.9 copy.43
  268.9 0.0 copy-done.2
  268.9 0.7 copy.44
  (3 shorter events, 0.0 us)
Async XLA Ops:
  0.6 3.8 %copy-start.5 = (bf16[3,768]{1,0:T(4,128)(2,1)S(1)}, bf16[3,768]{1,0:T(4,128)(2,1)}, u32[]{:S(2)}) copy-start(bf16[3,768]{1,0:T(4,128)(2,1)} %param.22) | copy-start | bytes 13828
  0.7 4.4 %copy-start.6 = (bf16[32,3]{0,1:T(4,128)(2,1)S(1)}, bf16[32,3]{0,1:T(4,128)(2,1)}, u32[]{:S(2)}) copy-start(bf16[32,3]{0,1:T(4,128)(2,1)} %param.23) | copy-start | bytes 580
  0.7 6.2 %copy-start.4 = (s32[1024]{0:T(1024)S(1)}, s32[1024]{0:T(1024)}, u32[]{:S(2)}) copy-start(s32[1024]{0:T(1024)} %param.21) | copy-start | bytes 12292
  0.7 8.3 %slice-start = ((s32[1024]{0:T(1024)}), s32[512]{0:T(512)S(1)}, s32[]{:S(2)}) async-start(s32[1024]{0:T(1024)} %param.21), calls=%async_computation | async-start | bytes 4096 | tf_op jit(solution)/shard_map/concatenate | solution.py:762
  260.0 6.4 %copy-start = (f32[96,3072]{1,0:T(8,128)S(1)}, f32[96,3072]{1,0:T(8,128)}, u32[]{:S(2)}) copy-start(f32[96,3072]{1,0:T(8,128)} %get-tuple-element.25) | copy-start | bytes 3538948
  264.9 2.3 copy-start.3
  264.9 3.1 %copy-start.1 = (f32[256,768]{1,0:T(8,128)S(1)}, f32[256,768]{1,0:T(8,128)}, u32[]{:S(2)}) copy-start(f32[256,768]{1,0:T(8,128)} %get-tuple-element.75) | copy-start | bytes 2359300
  267.2 1.6 copy-start.2

commit v4 on v3

v4 whole, which is shorter than its diff:
```python
import functools
import types

import jax
import jax.numpy as jnp
from jax import lax
from jax.experimental import pallas as pl
from jax.experimental.pallas import tpu as pltpu
from jax.sharding import PartitionSpec as P

NB = 32
EPS = 1e-06
F32 = jnp.float32
BF16 = jnp.bfloat16
NEG = -1e30
TILE = 256
NN = (((1,), (0,)), ((), ()))
NT = (((1,), (1,)), ((), ()))
TN = (((0,), (0,)), ((), ()))
MESH_ID = pl.DeviceIdType.MESH


def mm(a, b, dims=NN):
    return lax.dot_general(a, b, dims, preferred_element_type=F32)


def tile_rows(i):
    return pl.ds(pl.multiple_of(i * TILE, TILE), TILE)


def fwd_attention(q3, k3, vt3, out_t, lse, heads, query_block, key_blocks, tiles, kmask, between):
    hd = q3.shape[2]

    def qblock(u, _):
        ri = tile_rows(u)
        I = query_block(u)

        def kblock(J, carry):
            rj = tile_rows(J)
            new = []
            for h in range(heads):
                m, l, acc = carry[h]
                s = mm(k3[h, rj, :], q3[h, ri, :], NT)
                if tiles is not None:
                    s = s + tiles[h, jnp.minimum(I - J, 2)].astype(F32) + kmask[rj, :1]
                m2 = jnp.maximum(m, jnp.max(s, axis=0, keepdims=True))
                a = jnp.exp(m - m2)
                p = jnp.exp(s - m2)
                l2 = l * a + jnp.sum(p, axis=0, keepdims=True)
                new.append((m2, l2, acc * a + mm(vt3[h, :, rj], p.astype(BF16))))
            return tuple(new)

        init = tuple(
            (jnp.full((1, TILE), NEG, F32), jnp.zeros((1, TILE), F32), jnp.zeros((hd, TILE), F32)) for _ in range(heads)
        )
        res = lax.fori_loop(0, key_blocks(I), kblock, init)
        for h in range(heads):
            m, l, acc = res[h]
            out_t[h * hd : (h + 1) * hd, ri] = acc / l
            lse[h : h + 1, ri] = m + jnp.log(l)
        between(u)
        return 0

    lax.fori_loop(0, 2, qblock, 0)


def bwd_attention(
    q3, k3, v3, kt3, do3, lse, delta, dqt, dk, dv, put, heads, query_block, first_query, key_end, tiles, kmask, dtile, dfar, between
):
    hd = q3.shape[2]
    dqt[...] = jnp.zeros_like(dqt)

    def kblock(J, _):
        rj = tile_rows(J)
        dk[...] = jnp.zeros_like(dk)
        dv[...] = jnp.zeros_like(dv)

        def qblock(u, _):
            ri = tile_rows(u)
            apart = query_block(u) - J
            for h in range(heads):
                s = mm(k3[h, rj, :], q3[h, ri, :], NT)
                if tiles is not None:
                    s = s + tiles[h, jnp.minimum(apart, 2)].astype(F32) + kmask[rj, :1]
                p = jnp.exp(s - lse[h : h + 1, ri])
                dp = mm(v3[h, rj, :], do3[h, ri, :], NT)
                ds = (p * (dp - delta[h : h + 1, ri])).astype(BF16)
                dv[h] += mm(p.astype(BF16), do3[h, ri, :])
                dk[h] += mm(ds, q3[h, ri, :])
                dqt[h * hd : (h + 1) * hd, ri] += mm(kt3[h, :, rj], ds)
                if tiles is not None:
                    wide = ds.astype(F32)

                    @pl.when(apart < 2)
                    def _():
                        dtile[h, apart] += wide

                    @pl.when(apart >= 2)
                    def _():
                        dfar[h : h + 1, :] += jnp.sum(wide, axis=0, keepdims=True)

            return 0

        lax.fori_loop(first_query(J), 2, qblock, 0)
        put(J)
        between(J)
        return 0

    lax.fori_loop(0, key_end, kblock, 0)


def layer_kernel(dims, names, *refs):
    D, Hl, hd, FFL, N, NE, g, part = dims
    s = types.SimpleNamespace(**dict(zip(names, refs)))
    hw = Hl * hd
    H2 = 2 * Hl
    NC, NQ, NK = 2 * N, 4 * N, 4 * NE
    dp, z = lax.axis_index("dp"), lax.axis_index("mp")
    a, low = dp // g, dp % g
    c, r = a % 2, a // 2
    p, zb = z // 2, z % 2
    j = 2 * c + zb
    rx, ry, rd = r + 1 - 2 * (r % 2), (r + 2) % 4, 3 - r
    z1, z2 = z + 1 - 2 * zb, (z + 2) % 4
    stay, moved = c == p, c != p
    own = jnp.where(stay, z, 3 - z)
    beyond = jnp.where(stay, z1, 3 - z1)
    u_own = own // 2
    lo_block = jnp.minimum(own, 3 - own)
    hi_block = 3 - lo_block

    def device(r_, c_, z_):
        return {"dp": (2 * r_ + c_) * g + low, "mp": z_}

    sibling, across = device(r, 1 - c, z), device(r, c, z1)
    home = device(r, p, 3 - z)
    x_chip, y_chip = device(rx, c, z), device(ry, c, z)
    counter = [0]

    def slots(k):
        counter[0] += k
        return counter[0] - k

    def remote(src, dst, dev, send=None, recv=None):
        send = slots(1) if send is None else send
        recv = slots(1) if recv is None else recv
        return pltpu.make_async_remote_copy(
            src_ref=src, dst_ref=dst, send_sem=s.sems.at[send], recv_sem=s.sems.at[recv],
            device_id=dev, device_id_type=MESH_ID,
        )

    def local(src, dst, sem=None):
        return pltpu.make_async_copy(src, dst, s.sems.at[slots(1) if sem is None else sem])

    def either(cond, yes, no):
        @pl.when(cond)
        def _():
            yes()

        @pl.when(jnp.logical_not(cond))
        def _():
            no()

    unsent = []

    def go(copy):
        copy.start()
        unsent.append(copy)
        return copy

    def block(i, n):
        return pl.ds(pl.multiple_of(i * n, n), n)

    def order(k):
        first = jnp.where(k < 2, own, beyond)
        return jnp.where(k % 2 == 0, first, 3 - first)

    def query_block(u):
        return jnp.where(u == 0, lo_block, hi_block)

    barrier = pltpu.get_barrier_semaphore()
    peers = [device(r, (c + dc) % 2, (z + dz) % 4) for dz in range(4) for dc in range(2) if dz or dc] + [x_chip, y_chip]
    for peer in peers:
        pl.semaphore_signal(barrier, inc=1, device_id=peer, device_id_type=MESH_ID)
    pl.semaphore_wait(barrier, len(peers))

    def swap(src, dst):
        far, near = remote(src, dst, home), local(src, dst)
        either(moved, far.start, near.start)
        return lambda: either(moved, far.wait, near.wait)

    rows_a = D // 8
    chip = 2 * rows_a

    def spread(A, B):
        def at(ref, w):
            buf, slot, cols = ref
            return buf.at[w, cols] if slot is None else buf.at[slot, w, cols]

        def hop(ref, w, dev):
            return remote(at(ref, w), at(ref, w), dev)

        first = [hop(A, block(r, chip), x_chip), hop(B, block(r, chip), y_chip)]
        last = [hop(A, block(r // 2, 2 * chip), y_chip)] + [hop(B, block(q, chip), x_chip) for q in (r, ry)]

        def first_hop():
            go(first[0])
            go(first[1])

        def second_hop():
            first[0].wait_recv()
            go(last[0])
            first[1].wait_recv()
            go(last[1])
            go(last[2])

        def finish():
            for copy in last:
                copy.wait_recv()

        return first_hop, second_hop, finish

    def attn_weights(col, wide):
        C = pl.ds(col, wide)
        src = s.wpack.at[:, C]
        base = slots(4)
        dst = s.W2.at[zb, block(a, rows_a), C]
        for dz in range(1, 4):
            go(remote(src, dst, device(r, p, (z + dz) % 4), None, base + 2 * zb + c))
        near = local(src, dst)
        beside = remote(src, dst, sibling, None, base + 2 * zb + c)
        either(stay, near.start, beside.start)
        got = [
            (jnp.logical_and(z == 2 * c + k, c == c_), remote(src, s.W2.at[k, block(2 * r + c_, rows_a), C], sibling, 0, base + 2 * k + c_))
            for k in range(2)
            for c_ in range(2)
        ]
        first_hop, second_hop, finish = spread((s.W2, 0, C), (s.W2, 1, C))

        def start():
            for mine, copy in got:
                either(mine, near.wait, copy.wait_recv)
            pl.when(moved)(beside.wait_send)
            first_hop()

        return start, second_hop, finish

    def ff_weights(col, wide):
        src = s.wpack.at[:, pl.ds(col, wide)]
        dst = s.WF.at[block(a, rows_a), :]
        near, beside = local(src, dst), remote(src, dst, sibling)
        base = slots(2)
        go(remote(src, dst, device(r, p, z2), None, base + c))
        either(stay, near.start, beside.start)
        got = [remote(src, s.WF.at[block(2 * r + k, rows_a), :], sibling, 0, base + k) for k in range(2)]
        half = wide // 2
        first_hop, second_hop, finish = spread((s.WF, None, pl.ds(0, half)), (s.WF, None, pl.ds(half, half)))

        def start():
            @pl.when(stay)
            def _():
                near.wait()
                beside.wait_recv()

            @pl.when(moved)
            def _():
                beside.wait_send()
                for copy in got:
                    copy.wait_recv()

            first_hop()

        return start, second_hop, finish

    def collect(A, B, bufs, send_home):
        ra1, rb1, ra2, rb2 = bufs

        def at(ref, w):
            buf, slot, cols = ref
            return buf.at[w, cols] if slot is None else buf.at[slot, w, cols]

        one = [
            go(remote(at(A, block(ry // 2, 2 * chip)), ra1, y_chip)),
            go(remote(at(B, block(rx, chip)), rb1.at[0], x_chip)),
            go(remote(at(B, block(rd, chip)), rb1.at[1], x_chip)),
        ]
        two = [remote(at(A, block(rx, chip)), ra2, x_chip), remote(at(B, block(ry, chip)), rb2, y_chip)]
        send, finish = send_home()

        def add(dst, src):
            n = 96
            for q in range(src.shape[0] // n):
                w = pl.ds(q * n, n)
                dst[w, :] = (dst[w, :].astype(F32) + src[w, :].astype(F32)).astype(BF16)

        def second():
            one[0].wait_recv()
            add(at(A, block(r // 2, 2 * chip)), ra1)
            go(two[0])
            one[2].wait_recv()
            add(at(B, block(ry, chip)), rb1.at[1])
            go(two[1])
            one[1].wait_recv()
            add(at(B, block(r, chip)), rb1.at[0])

        def third():
            two[0].wait_recv()
            add(at(A, block(r, chip)), ra2)
            two[1].wait_recv()
            add(at(B, block(r, chip)), rb2)
            send()

        return second, third, finish

    def attn_home(col, wide):
        C = pl.ds(col, wide)

        def build():
            base, near_sem = slots(4), slots(1)
            pending = []
            for k in range(2):
                for c_ in range(2):
                    src = s.dW2.at[k, block(2 * r + c_, rows_a), C]
                    dst = s.gz2.at[z, :, C]
                    mine = jnp.logical_and(2 * c + k == z, c == c_)
                    far = remote(src, dst, device(r, c_, 2 * c + k), None, base + z)
                    pending.append((mine, local(src, dst, near_sem), far))
            src = s.dW2.at[0, block(2 * r, rows_a), C]
            got = [(stay & (z == k), remote(src, s.gz2.at[k, :, C], sibling, 0, base + k)) for k in range(4)]

            def send():
                for mine, near, far in pending:
                    either(mine, near.start, far.start)

            def finish():
                for mine, near, far in pending:
                    either(mine, near.wait, far.wait_send)
                for here, copy in got:
                    pl.when(jnp.logical_not(here))(copy.wait_recv)

            return send, finish

        return build

    def ff_home():
        recv, near_recv, near_sem = slots(1), slots(1), slots(1)
        beside = remote(s.dWF.at[block(2 * r + 1 - c, rows_a), :], s.gzf.at[0], sibling, None, near_recv)
        near = local(s.dWF.at[block(a, rows_a), :], s.gzf.at[0], near_sem)
        far = [
            remote(s.dWF.at[block(2 * r + k, rows_a), :], s.gzf.at[1], device(r, k, z2), None, recv) for k in range(2)
        ]

        def send():
            @pl.when(stay)
            def _():
                beside.start()
                near.start()

            @pl.when(moved)
            def _():
                for copy in far:
                    copy.start()

        def finish():
            @pl.when(stay)
            def _():
                beside.wait_send()
                near.wait()

            @pl.when(moved)
            def _():
                beside.wait_recv()
                for copy in far:
                    copy.wait_send()

            far[0].wait_recv()

        return send, finish

    def gather(buf, n):
        mine = buf.at[block(own, n), :]
        there = buf.at[block(beyond, n), :]
        cross, side, fwd = remote(mine, mine, across), remote(mine, mine, sibling), remote(there, there, sibling)
        cross.start()
        side.start()

        def forward():
            cross.wait_recv()
            fwd.start()

        def far():
            fwd.wait_recv()
            for copy in (side, cross, fwd):
                copy.wait_send()

        return types.SimpleNamespace(side=side.wait_recv, forward=forward, far=far)

    def each_block(h, body):
        h.side()
        lax.fori_loop(0, 2, lambda k, _: (body(order(k)), 0)[1], 0)
        h.forward()
        h.far()
        lax.fori_loop(2, 4, lambda k, _: (body(order(k)), 0)[1], 0)

    def gather_chip(buf):
        mine = buf.at[block(u_own, N), :]
        return go(remote(mine, mine, sibling)).wait_recv

    def scatter(fn, bufs, res):
        s0, s1, zs, r0, r1, rz = bufs
        s0[...] = fn(order(3)).astype(BF16)
        d0 = remote(s0, r0, sibling)
        d0.start()
        res[...] = fn(order(2))
        d0.wait_recv()
        zs[...] = (res[...] + r0[...].astype(F32)).astype(BF16)
        dz = remote(zs, rz, across)
        dz.start()
        s1[...] = fn(order(1)).astype(BF16)
        d1 = remote(s1, r1, sibling)
        d1.start()
        res[...] = fn(order(0))

        def finish():
            d1.wait_recv()
            dz.wait_recv()
            res[...] += r1[...].astype(F32) + rz[...].astype(F32)
            for copy in (d0, d1, dz):
                copy.wait_send()

        return finish

    def scatter_chip(fn, s0, r0, res):
        s0[...] = fn(1 - u_own).astype(BF16)
        d0 = remote(s0, r0, sibling)
        d0.start()
        res[...] = fn(u_own)

        def finish():
            d0.wait()
            res[...] += r0[...].astype(F32)

        return finish

    CH = 64

    def chunks(n, body, init=0):
        return lax.fori_loop(0, n // CH, lambda i, v: body(pl.ds(pl.multiple_of(i * CH, CH), CH), v), init)

    gains = [s.gains[k : k + 1, :].astype(F32) for k in range(3)]

    def norm_rows(v, which, inv_ref, w, dst, dst_at):
        inv = lax.rsqrt(jnp.sum(v * v, axis=1, keepdims=True) / D + EPS)
        inv_ref[w, :] = jnp.broadcast_to(inv, (CH, 128))
        dst[dst_at, :] = (v * inv * gains[which]).astype(BF16)

    def rows_in(i, w):
        return pl.ds(pl.multiple_of(i * N + w.start, CH), CH)

    def norm_back_rows(d, v, which, inv):
        scaled = d * gains[which]
        dotted = jnp.sum(scaled * v, axis=1, keepdims=True)
        back = inv * scaled - v * (inv * inv * inv * dotted / D)
        return back, jnp.sum(d * v * inv, axis=0, keepdims=True)

    zero_gain = jnp.zeros((1, D), F32)
    o_ff = 8 * hw
    c_q, c_o, c_ckv, c_cq, c_co = 2 * hw, 3 * hw, 4 * hw, 6 * hw, 7 * hw

    wait_x = swap(s.x, s.XN)
    w_kv = attn_weights(0, 2 * hw)
    w_qo = attn_weights(2 * hw, 2 * hw)
    s.tab[z] = jnp.zeros_like(s.tab[z])
    s.tab[z, :NB, :Hl] = s.rel_bias[...].astype(F32)
    tab_base = slots(4)
    tab_out = [
        remote(s.tab.at[z], s.tab.at[z], device(r, c, (z + dz) % 4), None, tab_base + z) for dz in range(1, 4)
    ]
    for copy in tab_out:
        go(copy)
    s.len_out[...] = jnp.full(s.len_out.shape, s.seq_lengths[0], jnp.int32).astype(F32)
    lens = go(remote(s.len_out, s.len_in, sibling))
    wait_e = swap(s.enc, s.EN)
    lens.wait_recv()
    s.len_row[...] = jnp.where(stay, s.len_out[...], s.len_in[...])
    for dz in range(1, 4):
        other = s.tab.at[(z + dz) % 4]
        remote(other, other, sibling, 0, tab_base + (z + dz) % 4).wait_recv()
    span = 2 * TILE
    ids = lax.broadcasted_iota(jnp.int32, (NB, span), 0)
    buckets = s.rel_buckets[...]
    last = jnp.broadcast_to(buckets[:, -1:], (1, span))
    near = buckets[:, :span]
    after = jnp.concatenate([buckets[:, TILE:span], buckets[:, :TILE]], axis=1)

    def onehot(row):
        return (ids == row).astype(F32)

    key_at = lax.broadcasted_iota(jnp.int32, (TILE, TILE), 0)
    query_at = lax.broadcasted_iota(jnp.int32, (TILE, TILE), 1)
    for q in range(2):
        table = s.tab[2 * c + q, :NB, :].T[:8, :]
        for k, row in enumerate((near, after, last)):
            s.vecs[8 * k : 8 * k + 8, :] = mm(table, onehot(row))

        def build(h, _):
            for k in range(3):
                wide = jnp.broadcast_to(s.vecs[pl.ds(8 * k + h, 1), :], (TILE, span))
                tile = pltpu.roll(wide, 0, 1, stride=1, stride_axis=0)[:, :TILE]
                s.tiles[Hl * q + h, k] = (jnp.where(query_at >= key_at, tile, NEG) if k == 0 else tile).astype(BF16)
            return 0

        lax.fori_loop(0, Hl, build, 0)
    length = s.len_row[0:1, :]
    s.kmask[...] = jnp.where(
        lax.broadcasted_iota(jnp.int32, s.kmask.shape, 0).astype(F32) < length, 0.0, NEG
    )
    wait_x()
    w_c = attn_weights(4 * hw, 4 * hw)

    def norm_one(w, _):
        norm_rows(s.XN[w, :].astype(F32), 0, s.inv1, w, s.FIRST, rows_in(own, w))
        return 0

    chunks(N, norm_one)
    ga = gather(s.FIRST, N)
    w_kv[0]()
    w_qo[0]()
    w_f = ff_weights(o_ff, 3 * FFL)
    wait_o = swap(s.og, s.ON)
    w_kv[1]()
    ga.side()
    ga.forward()
    w_c[0]()
    w_qo[1]()
    wait_e()
    s.ENC[block(own, NE), :] = s.EN[...]
    ge = gather(s.ENC, NE)
    ga.far()
    w_kv[2]()
    w_qo[2]()

    def split(dst, h0, value, rows):
        for h in range(Hl):
            dst[h0 + h, rows, :] = value[:, h * hd : (h + 1) * hd]

    def project_one(k, _):
        i = order(k)
        w = block(i, N)
        f = s.FIRST[w, :]
        for q in range(2):
            y = mm(f, s.W2[q, :, : 2 * hw]).astype(BF16)
            split(s.k3, Hl * q, y[:, :hw], w)
            split(s.v3, Hl * q, y[:, hw:], w)

        @pl.when(k < 2)
        def _():
            for q in range(2):
                split(s.q3, Hl * q, mm(f, s.W2[q, :, c_q : c_q + hw]).astype(BF16), block(i // 2, N))

        return 0

    lax.fori_loop(0, 4, project_one, 0)

    def turn(dst, src):
        def one(h, _):
            dst[h] = src[h].T
            return 0

        lax.fori_loop(0, H2, one, 0)

    turn(s.t3, s.v3)
    s.WO[...] = s.W2[:, :, c_o : c_o + hw]

    def after_first(u):
        @pl.when(u == 0)
        def _():
            ge.side()
            ge.forward()
            w_c[1]()
            w_f[0]()

    fwd_attention(s.q3, s.k3, s.t3, s.out_t, s.lse, H2, query_block, lambda I: I + 1, s.tiles, s.kmask, after_first)
    s.MIX[...] = s.out_t[...].T.astype(BF16)

    def out_proj(mix, weight):
        def fn(u):
            w = block(u, N)
            return mm(mix[w, :hw], weight[0], NT) + mm(mix[w, hw:], weight[1], NT)

        return fn

    end = scatter_chip(out_proj(s.MIX, s.WO), s.s0, s.i0, s.res)
    wait_o()
    own_pos = lax.broadcasted_iota(jnp.int32, (N, 128), 0) + own * N
    s.ok[...] = (own_pos.astype(F32) < length).astype(F32)

    def mask_rows(w, _):
        s.GF[rows_in(own, w), :] = (s.ON[w, :].astype(F32) * s.ok[w, :1]).astype(BF16)
        return 0

    chunks(N, mask_rows)
    gg = gather(s.GF, N)
    end()

    def norm_two(w, _):
        v = s.XN[w, :].astype(F32) + s.res[w, :]
        s.MID[w, :] = v
        norm_rows(v, 1, s.inv2, w, s.SECOND, rows_in(u_own, w))
        return 0

    chunks(N, norm_two)
    second_ready = gather_chip(s.SECOND)
    ge.far()
    w_c[2]()
    s.WCO[...] = s.W2[:, :, c_co : c_co + hw]

    def project_enc(i, _):
        w = block(i, N)
        e = s.ENC[w, :]
        for q in range(2):
            y = mm(e, s.W2[q, :, c_ckv : c_ckv + 2 * hw]).astype(BF16)
            split(s.ck3, Hl * q, y[:, :hw], w)
            split(s.cv3, Hl * q, y[:, hw:], w)
        return 0

    lax.fori_loop(0, NK // N, project_enc, 0)
    turn(s.ct3, s.cv3)
    second_ready()

    def project_two(u, _):
        w = block(u, N)
        t = s.SECOND[w, :]
        for q in range(2):
            split(s.cq3, Hl * q, mm(t, s.W2[q, :, c_cq : c_cq + hw]).astype(BF16), w)
        return 0

    lax.fori_loop(0, 2, project_two, 0)

    def after_cross(u):
        @pl.when(u == 0)
        def _():
            gg.side()
            gg.forward()
            w_f[1]()

    fwd_attention(
        s.cq3, s.ck3, s.ct3, s.out_t2, s.lse2, H2, query_block, lambda I: NK // TILE, None, None, after_cross
    )
    s.MIX2[...] = s.out_t2[...].T.astype(BF16)
    scatter_chip(out_proj(s.MIX2, s.WCO), s.s0, s.i1, s.res)()

    def norm_three(w, _):
        v = s.MID[w, :] + s.res[w, :]
        s.LAT[w, :] = v
        norm_rows(v, 2, s.inv3, w, s.THIRD, rows_in(own, w))
        return 0

    chunks(N, norm_three)
    gt = gather(s.THIRD, N)
    gg.far()
    w_f[2]()
    root = 0.7978845608028654
    SUB = 128

    def feed(i):
        def sub(u, _):
            w = pl.ds(pl.multiple_of(i * N + u * SUB, SUB), SUB)
            t = s.THIRD[w, :]
            gate = mm(t, s.WF[:, :FFL])
            up = mm(t, s.WF[:, FFL : 2 * FFL])
            dh = mm(s.GF[w, :], s.WF[:, 2 * FFL :])
            sq = gate * gate
            th = jnp.tanh(root * gate * (1.0 + 0.044715 * sq))
            half = 0.5 * (1.0 + th)
            act = gate * half
            slope = half + 0.5 * gate * (1.0 - th * th) * root * (1.0 + 3 * 0.044715 * sq)
            s.HID[w, :] = (act * up).astype(BF16)
            s.DGU[w, :FFL] = (dh * up * slope).astype(BF16)
            s.DGU[w, FFL:] = (dh * act).astype(BF16)
            return 0

        lax.fori_loop(0, N // SUB, sub, 0)

    each_block(gt, feed)
    end = scatter(
        lambda i: mm(s.DGU[block(i, N), :], s.WF[:, : 2 * FFL], NT), (s.s0, s.s1, s.zs, s.a0, s.a1, s.az), s.res
    )

    def weight_grad(put, parts):
        def step(q, _):
            m = pl.ds(pl.multiple_of(q * 256, 256), 256)
            total = None
            for left, right in parts:
                y = mm(left(m), right, TN)
                total = y if total is None else total + y
            put(m, total.astype(BF16))
            return 0

        lax.fori_loop(0, D // 256, step, 0)

    def put_f(col, n):
        def put(m, v):
            s.dWF[m, col : col + n] = v

        return put

    def put_slots(col, n):
        def put(m, v):
            for q in range(2):
                s.dW2[q, m, col : col + n] = v[:, q * n : (q + 1) * n]

        return put

    weight_grad(put_f(2 * FFL, FFL), [(lambda m: s.GF[:, m], s.HID[...])])
    weight_grad(put_f(0, 2 * FFL), [(lambda m: s.THIRD[:, m], s.DGU[...])])
    half_f = 3 * FFL // 2
    grad_f = collect(
        (s.dWF, None, pl.ds(0, half_f)), (s.dWF, None, pl.ds(half_f, half_f)), (s.ra1, s.rb1, s.ra2, s.rb2), ff_home
    )
    end()

    def back_three(w, acc):
        back, part_gain = norm_back_rows(s.res[w, :], s.LAT[w, :], 2, s.inv3[w, :1])
        d = s.GF[rows_in(own, w), :].astype(F32) + back
        s.GR[w, :] = d
        s.DL[rows_in(u_own, w), :] = d.astype(BF16)
        return acc + part_gain

    gain_three = chunks(N, back_three, zero_gain)
    dl_ready = gather_chip(s.DL)
    end_out = scatter(
        lambda i: mm(s.HID[block(i, N), :], s.WF[:, 2 * FFL :], NT), (s.s0, s.s1, s.zs, s.b0, s.b1, s.bz), s.res
    )

    turn(s.ct3, s.ck3)

    def back_heads(src, weight, out_t):
        def body(u, _):
            w = block(u, N)
            for q in range(2):
                y = mm(src[w, :], weight[q]).astype(BF16)
                split(s.do3, Hl * q, y, w)
                yt = y.astype(F32).T
                for h in range(Hl):
                    g_h = Hl * q + h
                    both = yt[h * hd : (h + 1) * hd, :] * out_t[g_h * hd : (g_h + 1) * hd, w]
                    s.delta[g_h : g_h + 1, w] = jnp.sum(both, axis=0, keepdims=True)
            return 0

        lax.fori_loop(0, 2, body, 0)

    dl_ready()
    back_heads(s.DL, s.WCO, s.out_t2)

    def put_cross(J):
        w = tile_rows(J)
        for h in range(H2):
            q, hh = h // Hl, h % Hl
            at = 2 * hw * q + hh * hd
            s.DGU[w, at : at + hd] = s.dk[h].astype(BF16)
            s.DGU[w, at + hw : at + hw + hd] = s.dv[h].astype(BF16)

    def cross_between(J):
        @pl.when(J == 0)
        def _():
            grad_f[0]()

    bwd_attention(
        s.cq3, s.ck3, s.cv3, s.ct3, s.do3, s.lse2, s.delta, s.out_t2, s.dk, s.dv, put_cross, H2, query_block,
        lambda J: 0, NK // TILE, None, None, None, None, cross_between,
    )
    s.DQ[...] = s.out_t2[...].T.astype(BF16)

    def query_grad(col):
        def fn(u):
            w = block(u, N)
            return mm(s.DQ[w, :hw], s.W2[0, :, col : col + hw], NT) + mm(s.DQ[w, hw:], s.W2[1, :, col : col + hw], NT)

        return fn

    def put_out(w, _):
        s.ON[w, :] = (s.LAT[w, :] + s.res[w, :]).astype(BF16)
        return 0

    end_out()
    chunks(N, put_out)
    wait_lo = swap(s.ON, s.lo)
    end = scatter_chip(query_grad(c_cq), s.s0, s.i2, s.res)
    grad_f[1]()

    def kv_grad(n, col):
        def fn(i):
            w = block(i, n)
            return (
                mm(s.DGU[w, : 2 * hw], s.W2[0, :, col : col + 2 * hw], NT)
                + mm(s.DGU[w, 2 * hw : 4 * hw], s.W2[1, :, col : col + 2 * hw], NT)
            )

        return fn

    end()

    def back_two(w, acc):
        back, part_gain = norm_back_rows(s.res[w, :], s.MID[w, :], 1, s.inv2[w, :1])
        d = s.GR[w, :] + back
        s.GR[w, :] = d
        s.DM[rows_in(u_own, w), :] = d.astype(BF16)
        return acc + part_gain

    gain_two = chunks(N, back_two, zero_gain)
    dm_ready = gather_chip(s.DM)
    end_enc = scatter(kv_grad(NE, c_ckv), (s.e0, s.e1, s.es, s.f0, s.f1, s.fz), s.rese)
    weight_grad(put_slots(c_cq, hw), [(lambda m: s.SECOND[:, m], s.DQ[...])])
    weight_grad(put_slots(c_co, hw), [(lambda m: s.DL[:, m], s.MIX2[...])])
    weight_grad(put_slots(c_ckv, 2 * hw), [(lambda m: s.ENC[:, m], s.DGU[:NK, : 4 * hw])])
    C4 = pl.ds(4 * hw, 4 * hw)
    grad_c = collect((s.dW2, 0, C4), (s.dW2, 1, C4), (s.qa1, s.qb1, s.qa2, s.qb2), attn_home(4 * hw, 4 * hw))
    end_enc()
    s.EN[...] = s.rese[...].astype(BF16)
    wait_eo = swap(s.EN, s.eg)
    turn(s.t3, s.k3)

    dm_ready()
    back_heads(s.DM, s.WO, s.out_t)
    s.dtile[...] = jnp.zeros_like(s.dtile)
    s.dfar[...] = jnp.zeros_like(s.dfar)

    def self_between(J):
        @pl.when(J == 0)
        def _():
            grad_c[0]()

    bwd_attention(
        s.q3, s.k3, s.v3, s.t3, s.do3, s.lse, s.delta, s.out_t, s.dk, s.dv, put_cross, H2, query_block,
        lambda J: jnp.where(J <= lo_block, 0, 1), hi_block + 1, s.tiles, s.kmask, s.dtile, s.dfar, self_between,
    )

    def clear(J, _):
        s.DGU[tile_rows(J), :] = jnp.zeros((TILE, s.DGU.shape[1]), BF16)
        return 0

    lax.fori_loop(hi_block + 1, 4, clear, 0)
    s.DQ[...] = s.out_t[...].T.astype(BF16)
    own_part = query_grad(c_q)
    other_part = kv_grad(N, 0)

    def scatter_first(bufs, res):
        s0, s1, zs, r0, r1, rz = bufs
        s0[...] = other_part(order(3)).astype(BF16)
        d0 = remote(s0, r0, sibling)
        d0.start()
        res[...] = other_part(order(2))
        d0.wait_recv()
        zs[...] = (res[...] + r0[...].astype(F32)).astype(BF16)
        dz = remote(zs, rz, across)
        dz.start()
        s1[...] = (other_part(3 - own) + own_part(1 - u_own)).astype(BF16)
        d1 = remote(s1, r1, sibling)
        d1.start()
        res[...] = other_part(own) + own_part(u_own)

        def finish():
            d1.wait_recv()
            dz.wait_recv()
            res[...] += r1[...].astype(F32) + rz[...].astype(F32)
            for copy in (d0, d1, dz):
                copy.wait_send()

        return finish

    end = scatter_first((s.s0, s.s1, s.zs, s.a0, s.a1, s.az), s.res)
    weight_grad(put_slots(0, 2 * hw), [(lambda m: s.FIRST[:, m], s.DGU[:, : 4 * hw])])
    weight_grad(
        put_slots(c_q, hw),
        [(lambda m: s.FIRST[tile_rows(lo_block), m], s.DQ[:N, :]), (lambda m: s.FIRST[tile_rows(hi_block), m], s.DQ[N:, :])],
    )
    weight_grad(put_slots(c_o, hw), [(lambda m: s.DM[:, m], s.MIX[...])])
    S4 = pl.ds(0, 4 * hw)
    grad_s = collect((s.dW2, 0, S4), (s.dW2, 1, S4), (s.ra1, s.rb1, s.ra2, s.rb2), attn_home(0, 4 * hw))
    grad_c[1]()
    s.small[...] = jnp.zeros_like(s.small)
    flip = (key_at + query_at == TILE - 1).astype(F32)
    blank = jnp.zeros((TILE, TILE), F32)
    head_row = lax.broadcasted_iota(jnp.int32, (16, span), 0)
    gap = lax.broadcasted_iota(jnp.int32, (1, span), 1)
    near_back = jnp.where(gap >= TILE - 1, pltpu.roll(near, TILE - 1, 1), -1)
    next_back = jnp.where(gap < span - 1, pltpu.roll(near, span - 1, 1), -1)
    for k, row in enumerate((near_back, next_back)):

        def line_up(h, diag):
            turned = lax.dot_general(
                flip, s.dtile[h, k], NN, precision=lax.Precision.HIGHEST, preferred_element_type=F32
            )
            lined = pltpu.roll(jnp.concatenate([turned, blank], axis=1), 0, 1, stride=1, stride_axis=0)
            return jnp.where(head_row == H2 * c + h, jnp.sum(lined, axis=0, keepdims=True), diag)

        diag = lax.fori_loop(0, H2, line_up, jnp.zeros((16, span), F32))
        s.small[:, D : D + NB] += lax.dot_general(
            diag, onehot(row), NT, precision=lax.Precision.HIGHEST, preferred_element_type=F32
        )
    far_sum = jnp.sum(s.dfar[...], axis=1, keepdims=True)
    bucket_at = lax.broadcasted_iota(jnp.int32, (1, NB), 1)
    is_last = (bucket_at == buckets[:, -1:]).astype(F32)
    bias_row = lax.broadcasted_iota(jnp.int32, (16, NB), 0)
    for h in range(H2):
        s.small[:, D : D + NB] += jnp.where(bias_row == H2 * c + h, far_sum[h : h + 1, :] * is_last, 0.0)
    end()

    def back_one(w, acc):
        back, part_gain = norm_back_rows(s.res[w, :], s.XN[w, :].astype(F32), 0, s.inv1[w, :1])
        s.s0[w, :] = (s.GR[w, :] + back).astype(BF16)
        return acc + part_gain

    gain_one = chunks(N, back_one, zero_gain)
    wait_dg = swap(s.s0, s.dg)
    for k, row in enumerate((gain_one, gain_two, gain_three)):
        s.small[k : k + 1, :D] = row
    for k, peer in enumerate((sibling, across, device(r, c, z2), x_chip, y_chip)):
        s.small_out[k] = s.small[...]
        hop = remote(s.small_out.at[k], s.small_in.at[k], peer)
        hop.start()
        if k == 1:
            grad_s[0]()
        if k == 4:
            grad_s[1]()
        hop.wait()
        s.small[...] += s.small_in[k]
    s.sm[...] = s.small[...]
    wait_lo()
    wait_eo()
    grad_f[2]()
    grad_c[2]()
    wait_dg()
    grad_s[2]()
    for copy in unsent:
        copy.wait_send()
    assert counter[0] <= part, counter[0]


def layer_call(wpack, x, enc, og, gains, rel_bias, seq_lengths, rel_buckets, dims):
    D, Hl, hd, FFL, N, NE, g, part = dims
    hw = Hl * hd
    H2, NC, NQ, NK = 2 * Hl, 2 * N, 4 * N, 4 * NE
    ra = D // 8
    vm, any_ = pl.BlockSpec(memory_space=pltpu.VMEM), pl.BlockSpec(memory_space=pl.ANY)
    sm_ = pl.BlockSpec(memory_space=pltpu.SMEM)
    ins = dict(wpack=any_, x=any_, enc=any_, og=any_, gains=vm, rel_bias=vm, seq_lengths=sm_, rel_buckets=vm)
    outs = dict(
        lo=((N, D), BF16, any_), dg=((N, D), BF16, any_), eg=((NE, D), BF16, any_),
        gz2=((4, ra, 8 * hw), BF16, any_), gzf=((2, ra, 3 * FFL), BF16, any_), sm=((16, D + 128), F32, vm),
    )
    sc = {}

    def add(dtype, **shapes):
        for name, shape in shapes.items():
            sc[name] = pltpu.VMEM(shape, dtype)

    add(BF16, W2=(2, D, 8 * hw), dW2=(2, D, 8 * hw), WF=(D, 3 * FFL), dWF=(D, 3 * FFL), WO=(2, D, hw), WCO=(2, D, hw))
    for k in "rq":
        add(BF16, **{k + "a1": (D // 2, 4 * hw), k + "b1": (2, D // 4, 4 * hw), k + "a2": (D // 4, 4 * hw), k + "b2": (D // 4, 4 * hw)})
    add(BF16, FIRST=(NQ, D), THIRD=(NQ, D), GF=(NQ, D), SECOND=(NC, D), DL=(NC, D), DM=(NC, D), ENC=(NK, D))
    add(BF16, **{k: (N, D) for k in ("s0", "s1", "zs", "a0", "a1", "az", "b0", "b1", "bz", "i0", "i1", "i2", "XN", "ON")})
    add(BF16, **{k: (NE, D) for k in ("e0", "e1", "es", "f0", "f1", "fz", "EN")})
    add(F32, **{k: (N, D) for k in ("MID", "LAT", "GR", "res")}, rese=(NE, D))
    add(F32, inv1=(N, 128), inv2=(N, 128), inv3=(N, 128), ok=(N, 128))
    add(BF16, q3=(H2, NC, hd), k3=(H2, NQ, hd), v3=(H2, NQ, hd), cq3=(H2, NC, hd), ck3=(H2, NK, hd), cv3=(H2, NK, hd))
    add(BF16, do3=(H2, NC, hd), t3=(H2, hd, NQ), ct3=(H2, hd, NK))
    add(F32, out_t=(2 * hw, NC), out_t2=(2 * hw, NC), lse=(8, NC), lse2=(8, NC), delta=(8, NC))
    add(F32, dk=(H2, TILE, hd), dv=(H2, TILE, hd))
    add(BF16, MIX=(NC, 2 * hw), MIX2=(NC, 2 * hw), HID=(NQ, FFL), DGU=(NQ, 2 * FFL), DQ=(NC, 2 * hw))
    add(BF16, tiles=(H2, 3, TILE, TILE))
    add(F32, dtile=(H2, 2, TILE, TILE), dfar=(8, TILE), kmask=(NQ, 128), vecs=(24, 2 * TILE))
    add(F32, tab=(4, NB, 128), len_out=(8, 128), len_in=(8, 128), len_row=(8, 128))
    add(F32, small=(16, D + 128), small_out=(5, 16, D + 128), small_in=(5, 16, D + 128))
    names = list(ins) + list(outs) + list(sc) + ["sems"]
    return pl.pallas_call(
        functools.partial(layer_kernel, dims, names),
        out_shape=[jax.ShapeDtypeStruct(o[0], o[1]) for o in outs.values()],
        in_specs=list(ins.values()),
        out_specs=[o[2] for o in outs.values()],
        scratch_shapes=list(sc.values()) + [pltpu.SemaphoreType.DMA((part,))],
        compiler_params=pltpu.CompilerParams(collective_id=0, has_side_effects=True, vmem_limit_bytes=67043328),
        name="layer",
    )(wpack, x, enc, og, gains, rel_bias, seq_lengths, rel_buckets)


def finish_kernel(dims, lo, dg, eg, gz2, gzf, sm, *outs):
    D, Hl, hd, FFL, N, NE, g, part = dims
    hw = Hl * hd
    o_lo, o_dg, o_eg, o_gains, o_bias, sq, sk, sv, so, cq, ck, cv, co, gg, gu, gd = outs
    o_lo[...] = lo[...]
    o_dg[...] = dg[...].astype(F32)
    o_eg[...] = eg[...].astype(F32)
    o_gains[...] = sm[:3, :D]
    o_bias[...] = sm[:, D:].T[:NB, : 4 * Hl]

    def total(col, n):
        w = pl.ds(col, n)
        return (gz2[0, :, w].astype(F32) + gz2[1, :, w].astype(F32)) + (gz2[2, :, w].astype(F32) + gz2[3, :, w].astype(F32))

    for base, parts in ((0, (sk, sv, sq, so)), (4 * hw, (ck, cv, cq, co))):
        y = total(base, 4 * hw)
        for k, out in enumerate(parts):
            v = y[:, k * hw : (k + 1) * hw]
            out[...] = v if k < 3 else v.T
    f = gzf[0].astype(F32) + gzf[1].astype(F32)
    gg[...] = f[:, :FFL]
    gu[...] = f[:, FFL : 2 * FFL]
    gd[...] = f[:, 2 * FFL :].T


def finish_call(dims, lo, dg, eg, gz2, gzf, sm):
    D, Hl, hd, FFL, N, NE, g, part = dims
    hw, ra = Hl * hd, D // 8
    vm = pl.BlockSpec(memory_space=pltpu.VMEM)
    shapes = [((N, D), BF16), ((N, D), F32), ((NE, D), F32), ((3, D), F32), ((NB, 4 * Hl), F32)]
    shapes += [((ra, hw), F32)] * 3 + [((hw, ra), F32)] + [((ra, hw), F32)] * 3 + [((hw, ra), F32)]
    shapes += [((ra, FFL), F32)] * 2 + [((FFL, ra), F32)]
    return pl.pallas_call(
        functools.partial(finish_kernel, dims),
        out_shape=[jax.ShapeDtypeStruct(*v) for v in shapes],
        in_specs=[vm] * 6,
        out_specs=[vm] * len(shapes),
        name="finish",
    )(lo, dg, eg, gz2, gzf, sm)


def exchange(value, step, size):
    return lax.ppermute(value, "dp", [(i, i ^ step) for i in range(size)])


def per_device(
    decoder_in, encoder_out, seq_lengths, rel_buckets, norm_gains, rel_bias,
    self_query, self_key, self_value, self_out, cross_query, cross_key, cross_value, cross_out,
    gate_weight, up_weight, down_weight, out_grad,
):
    width = decoder_in.shape[1]
    heads, w, f = rel_bias.shape[1], self_query.shape[1], gate_weight.shape[1]
    size = lax.axis_size("dp")
    g = size // 8
    rows, erows = decoder_in.shape[0], encoder_out.shape[0]
    wpack = jnp.concatenate(
        [self_key, self_value, self_query, self_out.T, cross_key, cross_value, cross_query, cross_out.T,
         gate_weight, up_weight, down_weight.T], axis=1,
    )
    step = 1
    while step < g:
        other = exchange(wpack, step, size)
        upper = (lax.axis_index("dp") // step) % 2
        wpack = jnp.where(upper == 1, jnp.concatenate([other, wpack], 0), jnp.concatenate([wpack, other], 0))
        step *= 2
    dims = (width, heads, w // heads, f, rows, erows, g, 320)
    lo, dg, eg, gz2, gzf, sm = layer_call(
        wpack, decoder_in, encoder_out, out_grad, norm_gains, rel_bias, seq_lengths, rel_buckets.reshape(1, -1), dims
    )
    if g == 1:
        return tuple(finish_call(dims, lo, dg, eg, gz2, gzf, sm))
    gw = jnp.concatenate([jnp.sum(gz2.astype(F32), axis=0), jnp.sum(gzf.astype(F32), axis=0)], axis=1)
    step = g // 2
    while step >= 1:
        upper = (lax.axis_index("dp") // step) % 2
        n = gw.shape[0] // 2
        keep = jnp.where(upper == 1, gw[n:], gw[:n])
        give = jnp.where(upper == 1, gw[:n], gw[n:])
        gw = keep + exchange(give, step, size)
        sm = sm + exchange(sm, step, size)
        step //= 2
    col = lambda k: gw[:, k * w : (k + 1) * w]
    return (
        lo, dg.astype(F32), eg.astype(F32), sm[:3, :width], sm[: 4 * heads, width : width + NB].T,
        col(2), col(0), col(1), col(3).T, col(6), col(4), col(5), col(7).T,
        gw[:, 8 * w : 8 * w + f], gw[:, 8 * w + f : 8 * w + 2 * f], gw[:, 8 * w + 2 * f :].T,
    )


def solution(mesh):
    return jax.shard_map(
        per_device,
        mesh=mesh,
        in_specs=(
            P(("dp", "mp"), None),
            P(("dp", "mp"), None),
            P("dp"),
            P(),
            P(),
            P(None, "mp"),
            P("dp", "mp"),
            P("dp", "mp"),
            P("dp", "mp"),
            P("mp", "dp"),
            P("dp", "mp"),
            P("dp", "mp"),
            P("dp", "mp"),
            P("mp", "dp"),
            P("dp", "mp"),
            P("dp", "mp"),
            P("mp", "dp"),
            P(("dp", "mp"), None),
        ),
        out_specs=(
            P(("dp", "mp"), None),
            P(("dp", "mp"), None),
            P(("dp", "mp"), None),
            P(),
            P(),
            P("dp", "mp"),
            P("dp", "mp"),
            P("dp", "mp"),
            P("mp", "dp"),
            P("dp", "mp"),
            P("dp", "mp"),
            P("dp", "mp"),
            P("mp", "dp"),
            P("dp", "mp"),
            P("dp", "mp"),
            P("mp", "dp"),
        ),
        check_vma=False,
    )
```

time: 270 us -> 243 us (0.900)
  Pallas kernels: 250 us -> 231 us
  local copies, waits for them, and re-layouts: 16.6 us -> 8.22 us
    pallas_call x1, Pallas kernels: 250 us -> 228 us  [layer_call(): pl.pallas_call(functools.partial(layer_kernel, dims, names), out_shape=[j...]
    transpose x3 -> x0, local copies, waits for them, and re-layouts: 4.31 us -> none  [the longest x1 2.19 us: per_device_fast(): gw[:, 5 * hw:6 * hw]]
    pallas_call x0 -> x1, Pallas kernels: none -> 3.45 us  [finish_call(): pl.pallas_call(functools.partial(finish_kernel, dims), out_shape=[jax.Sha...]
    pallas_call x0 -> x2, local copies, waits for them, and re-layouts: none -> 3.14 us  [finish_call(): pl.pallas_call(functools.partial(finish_kernel, dims), out_shape=[jax.Sha...]
    unnamed x21 -> x3, local copies, waits for them, and re-layouts: 5.68 us -> 3.14 us
where the time goes in v4:
time: 243 us; the launch traced here: 241 us
  Pallas kernels  231 us (95%)
  local copies, waits for them, and re-layouts  8.22 us (3%)
    pallas_call x1, Pallas kernels, layer_call(): pl.pallas_call(functools.partial(layer_kernel, dims, names), out_shape=[j...  228 us

profile of v4, /device:TPU:1, one launch (start us, length us, event | category | flops | bytes accessed | tf_op | source)
XLA Modules:
  0.0 241.0 jit_solution(6920586189349159146)
XLA Ops:
  1.3 1.4 copy.36.refs_5_
  2.7 0.9 copy.34
  3.6 0.9 copy.35
  4.4 1.9 concatenate.3.refs_0_
  6.4 228.0 %layer.1 = (bf16[256,768]{1,0:T(8,128)(2,1)}, bf16[256,768]{1,0:T(8,128)(2,1)}, bf16[128,768]{1,0:T(8,128)(2,1)}, bf16[4,96,1536]{2,1,0:T(8,128)(2,1)}, bf16[2,96,1536]{2,1,0:T(8,128)(2,1)}, /*index=5*/f32[16,896]{1,0:T(8,128)}) custom-call(bf16[96,3072]{1,0:T(8,128)(2,1)} %concatenate.3.refs_0_, bf16[256,768]{1,0:T(8,128)(2,1)} %refs_1_.1, ...), custom_call_target="tpu_custom_call" | custom-call | tf_op jit(solution)/shard_map/layer/pallas_call | solution.py:977
  234.4 3.5 %finish.1 = (bf16[256,768]{1,0:T(8,128)(2,1)}, f32[256,768]{1,0:T(8,128)}, f32[128,768]{1,0:T(8,128)}, f32[3,768]{1,0:T(4,128)}, f32[32,12]{1,0:T(8,128)}, /*ind...) custom-call(bf16[256,768]{1,0:T(8,128)(2,1)} %get-tuple-element.22.l, ...), custom_call_target="tpu_custom_call" | custom-call | tf_op jit(solution)/shard_map/finish/pallas_call | solution.py:1020
  237.9 1.4 copy.37
  239.3 1.8 copy.38

commit v5 on v4

--- a/solution.py
+++ b/solution.py
@@ -28,8 +28,8 @@
     return pl.ds(pl.multiple_of(i * TILE, TILE), TILE)
 
 
-def fwd_attention(q3, k3, vt3, out_t, lse, heads, query_block, key_blocks, tiles, kmask, between):
-    hd = q3.shape[2]
+def fwd_attention(q3, k3, vt3, out_t, lse, heads, query_block, key_blocks, tiles, between):
+    hd = vt3.shape[1]
 
     def qblock(u, _):
         ri = tile_rows(u)
@@ -42,7 +42,7 @@
                 m, l, acc = carry[h]
                 s = mm(k3[h, rj, :], q3[h, ri, :], NT)
                 if tiles is not None:
-                    s = s + tiles[h, jnp.minimum(I - J, 2)].astype(F32) + kmask[rj, :1]
+                    s = s + tiles[h, jnp.minimum(I - J, 2)].astype(F32)
                 m2 = jnp.maximum(m, jnp.max(s, axis=0, keepdims=True))
                 a = jnp.exp(m - m2)
                 p = jnp.exp(s - m2)
@@ -65,9 +65,9 @@
 
 
 def bwd_attention(
-    q3, k3, v3, kt3, do3, lse, delta, dqt, dk, dv, put, heads, query_block, first_query, key_end, tiles, kmask, dtile, dfar, between
+    q3, k3, v3, kt3, do3, lse, delta, dqt, dk, dv, put, heads, query_block, first_query, key_end, tiles, dtile, between
 ):
-    hd = q3.shape[2]
+    hd = kt3.shape[1]
     dqt[...] = jnp.zeros_like(dqt)
 
     def kblock(J, _):
@@ -81,24 +81,15 @@
             for h in range(heads):
                 s = mm(k3[h, rj, :], q3[h, ri, :], NT)
                 if tiles is not None:
-                    s = s + tiles[h, jnp.minimum(apart, 2)].astype(F32) + kmask[rj, :1]
+                    s = s + tiles[h, jnp.minimum(apart, 2)].astype(F32)
                 p = jnp.exp(s - lse[h : h + 1, ri])
                 dp = mm(v3[h, rj, :], do3[h, ri, :], NT)
                 ds = (p * (dp - delta[h : h + 1, ri])).astype(BF16)
                 dv[h] += mm(p.astype(BF16), do3[h, ri, :])
-                dk[h] += mm(ds, q3[h, ri, :])
+                dk[h, :, : q3.shape[2]] += mm(ds, q3[h, ri, :])
                 dqt[h * hd : (h + 1) * hd, ri] += mm(kt3[h, :, rj], ds)
                 if tiles is not None:
-                    wide = ds.astype(F32)
-
-                    @pl.when(apart < 2)
-                    def _():
-                        dtile[h, apart] += wide
-
-                    @pl.when(apart >= 2)
-                    def _():
-                        dfar[h : h + 1, :] += jnp.sum(wide, axis=0, keepdims=True)
-
+                    dtile[h, jnp.minimum(apart, 2)] += ds.astype(F32)
             return 0
 
         lax.fori_loop(first_query(J), 2, qblock, 0)
@@ -163,6 +154,9 @@
 
     unsent = []
 
+    def chain(*steps):
+        return steps
+
     def go(copy):
         copy.start()
         unsent.append(copy)
@@ -178,16 +172,38 @@
     def query_block(u):
         return jnp.where(u == 0, lo_block, hi_block)
 
+    pieces = (s.p_sk, s.p_sv, s.p_sq, s.p_so, s.p_ck, s.p_cv, s.p_cq, s.p_co)
+    loads = []
+    for k, piece in enumerate(pieces):
+        loads.append(local(piece, s.raw_t.at[k // 4] if k % 4 == 3 else s.raw.at[k - k // 4]))
+    for k, piece in enumerate((s.p_gate, s.p_up, s.p_down)):
+        loads.append(local(piece, s.wpack.at[:, pl.ds(8 * hw + k * FFL, FFL)]))
+    for copy in loads:
+        copy.start()
+
     barrier = pltpu.get_barrier_semaphore()
-    peers = [device(r, (c + dc) % 2, (z + dz) % 4) for dz in range(4) for dc in range(2) if dz or dc] + [x_chip, y_chip]
+    peers = [device(r, (c + dc) % 2, (z + dz) % 4) for dz in range(4) for dc in range(2) if dz or dc] + [x_chip, y_chip, device(rd, c, z)]
     for peer in peers:
         pl.semaphore_signal(barrier, inc=1, device_id=peer, device_id_type=MESH_ID)
+    for copy in loads:
+        copy.wait()
+    for k in range(8):
+        piece = s.raw_t[k // 4].T if k % 4 == 3 else s.raw[k - k // 4]
+        s.wpack[:, k * hw : (k + 1) * hw] = piece
     pl.semaphore_wait(barrier, len(peers))
 
+    def swap_halves(src, dst):
+        n = src.shape[0] // 2
+        return [swap_of(src.at[pl.ds(k * n, n), :], dst.at[pl.ds(k * n, n), :]) for k in range(2)]
+
     def swap(src, dst):
+        start, wait = swap_of(src, dst)
+        start()
+        return wait
+
+    def swap_of(src, dst):
         far, near = remote(src, dst, home), local(src, dst)
-        either(moved, far.start, near.start)
-        return lambda: either(moved, far.wait, near.wait)
+        return chain(lambda: either(moved, far.start, near.start), lambda: either(moved, far.wait, near.wait))
 
     rows_a = D // 8
     chip = 2 * rows_a
@@ -225,38 +241,58 @@
         src = s.wpack.at[:, C]
         base = slots(4)
         dst = s.W2.at[zb, block(a, rows_a), C]
-        for dz in range(1, 4):
-            go(remote(src, dst, device(r, p, (z + dz) % 4), None, base + 2 * zb + c))
+        out = [remote(src, dst, device(r, p, z_), None, base + 2 * zb + c) for z_ in (z2, z1)]
         near = local(src, dst)
         beside = remote(src, dst, sibling, None, base + 2 * zb + c)
-        either(stay, near.start, beside.start)
-        got = [
-            (jnp.logical_and(z == 2 * c + k, c == c_), remote(src, s.W2.at[k, block(2 * r + c_, rows_a), C], sibling, 0, base + 2 * k + c_))
-            for k in range(2)
-            for c_ in range(2)
-        ]
+        at = [s.W2.at[zb, block(2 * r + c_, rows_a), C] for c_ in range(2)]
+        pass_on = [remote(at[c_], at[c_], across, None, base + 2 * zb + c_) for c_ in range(2)]
+        here = [remote(src, at[0], sibling, 0, base + 2 * zb + c_) for c_ in range(2)]
+        there = [remote(src, at[0], sibling, 0, base + 2 * (1 - zb) + c_) for c_ in range(2)]
         first_hop, second_hop, finish = spread((s.W2, 0, C), (s.W2, 1, C))
 
         def start():
-            for mine, copy in got:
-                either(mine, near.wait, copy.wait_recv)
-            pl.when(moved)(beside.wait_send)
+            for copy in out:
+                go(copy)
+            either(stay, near.start, beside.start)
+
+        def relay():
+            def forward():
+                beside.wait_send()
+                for c_ in range(2):
+                    here[c_].wait_recv()
+                    pass_on[c_].start()
+
+            def settle():
+                near.wait()
+                remote_side.wait_recv()
+
+            either(moved, forward, settle)
+
+        remote_side = remote(src, at[0], sibling, 0, base + 2 * zb + 1 - c)
+
+        def first():
+            for c_ in range(2):
+                there[c_].wait_recv()
+            pl.when(moved)(lambda: [copy.wait_send() for copy in pass_on] and None)
             first_hop()
 
-        return start, second_hop, finish
+        return chain(start, relay, first, second_hop, finish)
 
     def ff_weights(col, wide):
         src = s.wpack.at[:, pl.ds(col, wide)]
         dst = s.WF.at[block(a, rows_a), :]
         near, beside = local(src, dst), remote(src, dst, sibling)
         base = slots(2)
-        go(remote(src, dst, device(r, p, z2), None, base + c))
-        either(stay, near.start, beside.start)
-        got = [remote(src, s.WF.at[block(2 * r + k, rows_a), :], sibling, 0, base + k) for k in range(2)]
+        out = remote(src, dst, device(r, p, z2), None, base + c)
+        got = [remote(src, dst, sibling, 0, base + k) for k in range(2)]
         half = wide // 2
         first_hop, second_hop, finish = spread((s.WF, None, pl.ds(0, half)), (s.WF, None, pl.ds(half, half)))
 
         def start():
+            go(out)
+            either(stay, near.start, beside.start)
+
+        def first():
             @pl.when(stay)
             def _():
                 near.wait()
@@ -270,7 +306,7 @@
 
             first_hop()
 
-        return start, second_hop, finish
+        return chain(start, first, second_hop, finish)
 
     def collect(A, B, bufs, send_home):
         ra1, rb1, ra2, rb2 = bufs
@@ -285,7 +321,7 @@
             go(remote(at(B, block(rd, chip)), rb1.at[1], x_chip)),
         ]
         two = [remote(at(A, block(rx, chip)), ra2, x_chip), remote(at(B, block(ry, chip)), rb2, y_chip)]
-        send, finish = send_home()
+        home_steps = send_home()
 
         def add(dst, src):
             n = 96
@@ -308,47 +344,15 @@
             add(at(A, block(r, chip)), ra2)
             two[1].wait_recv()
             add(at(B, block(r, chip)), rb2)
-            send()
-
-        return second, third, finish
-
-    def attn_home(col, wide):
-        C = pl.ds(col, wide)
-
-        def build():
-            base, near_sem = slots(4), slots(1)
-            pending = []
-            for k in range(2):
-                for c_ in range(2):
-                    src = s.dW2.at[k, block(2 * r + c_, rows_a), C]
-                    dst = s.gz2.at[z, :, C]
-                    mine = jnp.logical_and(2 * c + k == z, c == c_)
-                    far = remote(src, dst, device(r, c_, 2 * c + k), None, base + z)
-                    pending.append((mine, local(src, dst, near_sem), far))
-            src = s.dW2.at[0, block(2 * r, rows_a), C]
-            got = [(stay & (z == k), remote(src, s.gz2.at[k, :, C], sibling, 0, base + k)) for k in range(4)]
-
-            def send():
-                for mine, near, far in pending:
-                    either(mine, near.start, far.start)
-
-            def finish():
-                for mine, near, far in pending:
-                    either(mine, near.wait, far.wait_send)
-                for here, copy in got:
-                    pl.when(jnp.logical_not(here))(copy.wait_recv)
-
-            return send, finish
-
-        return build
-
-    def ff_home():
+            home_steps[0]()
+
+        return chain(second, third, *home_steps[1:])
+
+    def to_home(grad, out):
         recv, near_recv, near_sem = slots(1), slots(1), slots(1)
-        beside = remote(s.dWF.at[block(2 * r + 1 - c, rows_a), :], s.gzf.at[0], sibling, None, near_recv)
-        near = local(s.dWF.at[block(a, rows_a), :], s.gzf.at[0], near_sem)
-        far = [
-            remote(s.dWF.at[block(2 * r + k, rows_a), :], s.gzf.at[1], device(r, k, z2), None, recv) for k in range(2)
-        ]
+        beside = remote(grad(2 * r + 1 - c), out(0), sibling, None, near_recv)
+        near = local(grad(a), out(0), near_sem)
+        far = [remote(grad(2 * r + k), out(1), device(r, k, z2), None, recv) for k in range(2)]
 
         def send():
             @pl.when(stay)
@@ -377,23 +381,100 @@
 
         return send, finish
 
+    def attn_home(col, wide, buf):
+        C = pl.ds(col, wide)
+
+        def build():
+            pair = remote(s.dW2.at[1 - zb, block(r, chip), C], buf, across)
+            send, finish = to_home(
+                lambda i: s.dW2.at[zb, block(i, rows_a), C], lambda k: s.gz2.at[k, :, C]
+            )
+
+            def add_pair():
+                pair.wait()
+                for q in range(2):
+                    w = pl.ds(q * rows_a, rows_a)
+                    at = s.dW2.at[zb, block(2 * r + q, rows_a), C]
+                    at[...] = (at[...].astype(F32) + buf[w, :].astype(F32)).astype(BF16)
+                send()
+
+            return pair.start, add_pair, finish
+
+        return build
+
+    def ff_home():
+        return to_home(lambda i: s.dWF.at[block(i, rows_a), :], lambda k: s.gzf.at[k])
+
+    def all_sum(buf, in1, in2):
+        base1, base2 = slots(8), slots(4)
+        me = 4 * c + z
+        one, two = [], []
+        for dz in range(4):
+            for dc in range(2):
+                if dz or dc:
+                    c_, z_ = (c + dc) % 2, (z + dz) % 4
+                    one.append((remote(in1.at[me], in1.at[me], device(r, c_, z_), None, base1 + me), base1 + 4 * c_ + z_))
+        for dr in range(1, 4):
+            r_ = (r + dr) % 4
+            two.append((remote(in2.at[r], in2.at[r], device(r_, c, z), None, base2 + r), base2 + r_))
+
+        def waits(copies, ref):
+            for copy, recv in copies:
+                copy.wait_send()
+                remote(ref, ref, sibling, 0, recv).wait_recv()
+
+        def start():
+            in1[me] = buf[...]
+            for copy, _ in one:
+                copy.start()
+
+        def middle():
+            waits(one, in1.at[0])
+            in2[r] = jnp.sum(in1[...], axis=0)
+            for copy, _ in two:
+                copy.start()
+
+        def finish():
+            waits(two, in2.at[0])
+            buf[...] = jnp.sum(in2[...], axis=0)
+
+        return chain(start, middle, finish)
+
     def gather(buf, n):
-        mine = buf.at[block(own, n), :]
-        there = buf.at[block(beyond, n), :]
-        cross, side, fwd = remote(mine, mine, across), remote(mine, mine, sibling), remote(there, there, sibling)
-        cross.start()
-        side.start()
+        half = n // 2
+        copies = []
+        for k in range(2):
+            mine = buf.at[block(2 * own + k, half), :]
+            there = buf.at[block(2 * beyond + k, half), :]
+            copies.append((remote(mine, mine, across), remote(mine, mine, sibling), remote(there, there, sibling)))
+
+        def start(k):
+            copies[k][0].start()
+            copies[k][1].start()
+
+        def side():
+            for copy in copies:
+                copy[1].wait_recv()
 
         def forward():
-            cross.wait_recv()
-            fwd.start()
+            for copy in copies:
+                copy[0].wait_recv()
+                copy[2].start()
 
         def far():
-            fwd.wait_recv()
-            for copy in (side, cross, fwd):
-                copy.wait_send()
-
-        return types.SimpleNamespace(side=side.wait_recv, forward=forward, far=far)
+            for copy in copies:
+                copy[2].wait_recv()
+                for one in copy:
+                    one.wait_send()
+
+        first, second, side, forward, far = chain(lambda: start(0), lambda: start(1), side, forward, far)
+        return types.SimpleNamespace(start=lambda k: (first, second)[k](), side=side, forward=forward, far=far)
+
+    def gather_all(buf, n):
+        h = gather(buf, n)
+        h.start(0)
+        h.start(1)
+        return h
 
     def each_block(h, body):
         h.side()
@@ -403,8 +484,17 @@
         lax.fori_loop(2, 4, lambda k, _: (body(order(k)), 0)[1], 0)
 
     def gather_chip(buf):
-        mine = buf.at[block(u_own, N), :]
-        return go(remote(mine, mine, sibling)).wait_recv
+        copies = []
+        for k in range(2):
+            mine = buf.at[block(2 * u_own + k, N // 2), :]
+            copies.append(remote(mine, mine, sibling))
+
+        def ready():
+            for copy in copies:
+                copy.wait_recv()
+
+        first, second, ready = chain(lambda: go(copies[0]), lambda: go(copies[1]), ready)
+        return (lambda k: (first, second)[k]()), ready
 
     def scatter(fn, bufs, res):
         s0, s1, zs, r0, r1, rz = bufs
@@ -414,21 +504,29 @@
         res[...] = fn(order(2))
         d0.wait_recv()
         zs[...] = (res[...] + r0[...].astype(F32)).astype(BF16)
-        dz = remote(zs, rz, across)
-        dz.start()
+        n = res.shape[0] // 2
+        parts = [pl.ds(k * n, n) for k in range(2)]
+        dz = [remote(zs.at[w, :], rz.at[w, :], across) for w in parts]
+        for copy in dz:
+            copy.start()
         s1[...] = fn(order(1)).astype(BF16)
         d1 = remote(s1, r1, sibling)
         d1.start()
         res[...] = fn(order(0))
 
-        def finish():
-            d1.wait_recv()
-            dz.wait_recv()
-            res[...] += r1[...].astype(F32) + rz[...].astype(F32)
-            for copy in (d0, d1, dz):
-                copy.wait_send()
-
-        return finish
+        def finish(k=None):
+            for q in (0, 1) if k is None else (k,):
+                if q == 0:
+                    d1.wait_recv()
+                w = parts[q]
+                dz[q].wait_recv()
+                res[w, :] += r1[w, :].astype(F32) + rz[w, :].astype(F32)
+                if q == 1:
+                    for copy in (d0, d1, *dz):
+                        copy.wait_send()
+
+        steps = chain(lambda: finish(0), lambda: finish(1))
+        return lambda k=None: [step() for step in (steps if k is None else steps[k : k + 1])]
 
     def scatter_chip(fn, s0, r0, res):
         s0[...] = fn(1 - u_own).astype(BF16)
@@ -440,12 +538,13 @@
             d0.wait()
             res[...] += r0[...].astype(F32)
 
-        return finish
+        return chain(finish)[0]
 
     CH = 64
 
-    def chunks(n, body, init=0):
-        return lax.fori_loop(0, n // CH, lambda i, v: body(pl.ds(pl.multiple_of(i * CH, CH), CH), v), init)
+    def chunks(n, body, init=0, half=None):
+        lo, hi = (0, n // CH) if half is None else (half * n // (2 * CH), (half + 1) * n // (2 * CH))
+        return lax.fori_loop(lo, hi, lambda i, v: body(pl.ds(pl.multiple_of(i * CH, CH), CH), v), init)
 
     gains = [s.gains[k : k + 1, :].astype(F32) for k in range(3)]
 
@@ -467,11 +566,15 @@
     o_ff = 8 * hw
     c_q, c_o, c_ckv, c_cq, c_co = 2 * hw, 3 * hw, 4 * hw, 6 * hw, 7 * hw
 
-    wait_x = swap(s.x, s.XN)
     w_kv = attn_weights(0, 2 * hw)
     w_qo = attn_weights(2 * hw, 2 * hw)
+    swap_x = swap_halves(s.x, s.XN)
+    w_kv[0]()
+    for k in range(2):
+        swap_x[k][0]()
+    w_qo[0]()
     s.tab[z] = jnp.zeros_like(s.tab[z])
-    s.tab[z, :NB, :Hl] = s.rel_bias[...].astype(F32)
+    s.tab[z, :Hl, :NB] = s.rel_bias[...].astype(F32)
     tab_base = slots(4)
     tab_out = [
         remote(s.tab.at[z], s.tab.at[z], device(r, c, (z + dz) % 4), None, tab_base + z) for dz in range(1, 4)
@@ -480,7 +583,6 @@
         go(copy)
     s.len_out[...] = jnp.full(s.len_out.shape, s.seq_lengths[0], jnp.int32).astype(F32)
     lens = go(remote(s.len_out, s.len_in, sibling))
-    wait_e = swap(s.enc, s.EN)
     lens.wait_recv()
     s.len_row[...] = jnp.where(stay, s.len_out[...], s.len_in[...])
     for dz in range(1, 4):
@@ -498,8 +600,9 @@
 
     key_at = lax.broadcasted_iota(jnp.int32, (TILE, TILE), 0)
     query_at = lax.broadcasted_iota(jnp.int32, (TILE, TILE), 1)
+    w_kv[1]()
     for q in range(2):
-        table = s.tab[2 * c + q, :NB, :].T[:8, :]
+        table = s.tab[2 * c + q, :, :NB]
         for k, row in enumerate((near, after, last)):
             s.vecs[8 * k : 8 * k + 8, :] = mm(table, onehot(row))
 
@@ -512,37 +615,58 @@
 
         lax.fori_loop(0, Hl, build, 0)
     length = s.len_row[0:1, :]
-    s.kmask[...] = jnp.where(
-        lax.broadcasted_iota(jnp.int32, s.kmask.shape, 0).astype(F32) < length, 0.0, NEG
-    )
-    wait_x()
-    w_c = attn_weights(4 * hw, 4 * hw)
+    lane = lax.broadcasted_iota(jnp.int32, (TILE, 128), 1)
+
+    def extra_lane(i, _):
+        w = tile_rows(i)
+        at = lax.broadcasted_iota(jnp.int32, (TILE, 128), 0) + i * TILE
+        mask = jnp.where((lane == hd) & (at.astype(F32) >= length), NEG, 0.0).astype(BF16)
+        for h in range(H2):
+            s.k3[h, w, :] = mask
+
+        @pl.when(i < 2)
+        def _():
+            for h in range(H2):
+                s.q3[h, w, :] = jnp.where(lane == hd, 1.0, 0.0).astype(BF16)
+
+        return 0
+
+    lax.fori_loop(0, 4, extra_lane, 0)
+    ga = gather(s.FIRST, N)
 
     def norm_one(w, _):
         norm_rows(s.XN[w, :].astype(F32), 0, s.inv1, w, s.FIRST, rows_in(own, w))
         return 0
 
-    chunks(N, norm_one)
-    ga = gather(s.FIRST, N)
-    w_kv[0]()
-    w_qo[0]()
+    for k in range(2):
+        swap_x[k][1]()
+        chunks(N, norm_one, 0, k)
+        ga.start(k)
+    w_kv[2]()
+    w_c = attn_weights(4 * hw, 4 * hw)
     w_f = ff_weights(o_ff, 3 * FFL)
-    wait_o = swap(s.og, s.ON)
-    w_kv[1]()
+    w_c[0]()
+    w_qo[1]()
+    w_kv[3]()
+    w_qo[2]()
+    wait_e = swap(s.enc, s.EN)
     ga.side()
     ga.forward()
-    w_c[0]()
-    w_qo[1]()
+    w_c[1]()
+    w_f[0]()
+    w_qo[3]()
+    w_c[2]()
+    wait_o = swap(s.og, s.ON)
     wait_e()
     s.ENC[block(own, NE), :] = s.EN[...]
-    ge = gather(s.ENC, NE)
+    ge = gather_all(s.ENC, NE)
     ga.far()
-    w_kv[2]()
-    w_qo[2]()
+    w_kv[4]()
+    w_qo[4]()
 
     def split(dst, h0, value, rows):
         for h in range(Hl):
-            dst[h0 + h, rows, :] = value[:, h * hd : (h + 1) * hd]
+            dst[h0 + h, rows, :hd] = value[:, h * hd : (h + 1) * hd]
 
     def project_one(k, _):
         i = order(k)
@@ -564,7 +688,7 @@
 
     def turn(dst, src):
         def one(h, _):
-            dst[h] = src[h].T
+            dst[h] = src[h, :, :hd].T
             return 0
 
         lax.fori_loop(0, H2, one, 0)
@@ -575,12 +699,12 @@
     def after_first(u):
         @pl.when(u == 0)
         def _():
+            w_c[3]()
+            w_f[1]()
             ge.side()
             ge.forward()
-            w_c[1]()
-            w_f[0]()
-
-    fwd_attention(s.q3, s.k3, s.t3, s.out_t, s.lse, H2, query_block, lambda I: I + 1, s.tiles, s.kmask, after_first)
+
+    fwd_attention(s.q3, s.k3, s.t3, s.out_t, s.lse, H2, query_block, lambda I: I + 1, s.tiles, after_first)
     s.MIX[...] = s.out_t[...].T.astype(BF16)
 
     def out_proj(mix, weight):
@@ -591,16 +715,6 @@
         return fn
 
     end = scatter_chip(out_proj(s.MIX, s.WO), s.s0, s.i0, s.res)
-    wait_o()
-    own_pos = lax.broadcasted_iota(jnp.int32, (N, 128), 0) + own * N
-    s.ok[...] = (own_pos.astype(F32) < length).astype(F32)
-
-    def mask_rows(w, _):
-        s.GF[rows_in(own, w), :] = (s.ON[w, :].astype(F32) * s.ok[w, :1]).astype(BF16)
-        return 0
-
-    chunks(N, mask_rows)
-    gg = gather(s.GF, N)
     end()
 
     def norm_two(w, _):
@@ -609,10 +723,12 @@
         norm_rows(v, 1, s.inv2, w, s.SECOND, rows_in(u_own, w))
         return 0
 
-    chunks(N, norm_two)
-    second_ready = gather_chip(s.SECOND)
+    second_go, second_ready = gather_chip(s.SECOND)
+    for k in range(2):
+        chunks(N, norm_two, 0, k)
+        second_go(k)
     ge.far()
-    w_c[2]()
+    w_c[4]()
     s.WCO[...] = s.W2[:, :, c_co : c_co + hw]
 
     def project_enc(i, _):
@@ -636,16 +752,24 @@
         return 0
 
     lax.fori_loop(0, 2, project_two, 0)
+    wait_o()
+    own_pos = lax.broadcasted_iota(jnp.int32, (N, 128), 0) + own * N
+    s.ok[...] = (own_pos.astype(F32) < length).astype(F32)
+
+    def mask_rows(w, _):
+        s.GF[rows_in(own, w), :] = (s.ON[w, :].astype(F32) * s.ok[w, :1]).astype(BF16)
+        return 0
+
+    chunks(N, mask_rows)
+    gg = gather_all(s.GF, N)
 
     def after_cross(u):
         @pl.when(u == 0)
         def _():
-            gg.side()
-            gg.forward()
-            w_f[1]()
+            w_f[2]()
 
     fwd_attention(
-        s.cq3, s.ck3, s.ct3, s.out_t2, s.lse2, H2, query_block, lambda I: NK // TILE, None, None, after_cross
+        s.cq3, s.ck3, s.ct3, s.out_t2, s.lse2, H2, query_block, lambda I: NK // TILE, None, after_cross
     )
     s.MIX2[...] = s.out_t2[...].T.astype(BF16)
     scatter_chip(out_proj(s.MIX2, s.WCO), s.s0, s.i1, s.res)()
@@ -656,10 +780,14 @@
         norm_rows(v, 2, s.inv3, w, s.THIRD, rows_in(own, w))
         return 0
 
-    chunks(N, norm_three)
     gt = gather(s.THIRD, N)
+    for k in range(2):
+        chunks(N, norm_three, 0, k)
+        gt.start(k)
+    gg.side()
+    gg.forward()
     gg.far()
-    w_f[2]()
+    w_f[3]()
     root = 0.7978845608028654
     SUB = 128
 
@@ -718,8 +846,6 @@
     grad_f = collect(
         (s.dWF, None, pl.ds(0, half_f)), (s.dWF, None, pl.ds(half_f, half_f)), (s.ra1, s.rb1, s.ra2, s.rb2), ff_home
     )
-    end()
-
     def back_three(w, acc):
         back, part_gain = norm_back_rows(s.res[w, :], s.LAT[w, :], 2, s.inv3[w, :1])
         d = s.GF[rows_in(own, w), :].astype(F32) + back
@@ -727,8 +853,12 @@
         s.DL[rows_in(u_own, w), :] = d.astype(BF16)
         return acc + part_gain
 
-    gain_three = chunks(N, back_three, zero_gain)
-    dl_ready = gather_chip(s.DL)
+    dl_go, dl_ready = gather_chip(s.DL)
+    gain_three = zero_gain
+    for k in range(2):
+        end(k)
+        gain_three = chunks(N, back_three, gain_three, k)
+        dl_go(k)
     end_out = scatter(
         lambda i: mm(s.HID[block(i, N), :], s.WF[:, 2 * FFL :], NT), (s.s0, s.s1, s.zs, s.b0, s.b1, s.bz), s.res
     )
@@ -758,7 +888,7 @@
         for h in range(H2):
             q, hh = h // Hl, h % Hl
             at = 2 * hw * q + hh * hd
-            s.DGU[w, at : at + hd] = s.dk[h].astype(BF16)
+            s.DGU[w, at : at + hd] = s.dk[h, :, :hd].astype(BF16)
             s.DGU[w, at + hw : at + hw + hd] = s.dv[h].astype(BF16)
 
     def cross_between(J):
@@ -768,7 +898,7 @@
 
     bwd_attention(
         s.cq3, s.ck3, s.cv3, s.ct3, s.do3, s.lse2, s.delta, s.out_t2, s.dk, s.dv, put_cross, H2, query_block,
-        lambda J: 0, NK // TILE, None, None, None, None, cross_between,
+        lambda J: 0, NK // TILE, None, None, cross_between,
     )
     s.DQ[...] = s.out_t2[...].T.astype(BF16)
 
@@ -787,7 +917,6 @@
     chunks(N, put_out)
     wait_lo = swap(s.ON, s.lo)
     end = scatter_chip(query_grad(c_cq), s.s0, s.i2, s.res)
-    grad_f[1]()
 
     def kv_grad(n, col):
         def fn(i):
@@ -799,6 +928,12 @@
 
         return fn
 
+    weight_grad(put_slots(c_cq, hw), [(lambda m: s.SECOND[:, m], s.DQ[...])])
+    weight_grad(put_slots(c_co, hw), [(lambda m: s.DL[:, m], s.MIX2[...])])
+    weight_grad(put_slots(c_ckv, 2 * hw), [(lambda m: s.ENC[:, m], s.DGU[:NK, : 4 * hw])])
+    grad_f[1]()
+    C4 = pl.ds(4 * hw, 4 * hw)
+    grad_c = collect((s.dW2, 0, C4), (s.dW2, 1, C4), (s.qa1, s.qb1, s.qa2, s.qb2), attn_home(4 * hw, 4 * hw, s.pair1))
     end()
 
     def back_two(w, acc):
@@ -808,14 +943,12 @@
         s.DM[rows_in(u_own, w), :] = d.astype(BF16)
         return acc + part_gain
 
-    gain_two = chunks(N, back_two, zero_gain)
-    dm_ready = gather_chip(s.DM)
+    dm_go, dm_ready = gather_chip(s.DM)
+    gain_two = zero_gain
+    for k in range(2):
+        gain_two = chunks(N, back_two, gain_two, k)
+        dm_go(k)
     end_enc = scatter(kv_grad(NE, c_ckv), (s.e0, s.e1, s.es, s.f0, s.f1, s.fz), s.rese)
-    weight_grad(put_slots(c_cq, hw), [(lambda m: s.SECOND[:, m], s.DQ[...])])
-    weight_grad(put_slots(c_co, hw), [(lambda m: s.DL[:, m], s.MIX2[...])])
-    weight_grad(put_slots(c_ckv, 2 * hw), [(lambda m: s.ENC[:, m], s.DGU[:NK, : 4 * hw])])
-    C4 = pl.ds(4 * hw, 4 * hw)
-    grad_c = collect((s.dW2, 0, C4), (s.dW2, 1, C4), (s.qa1, s.qb1, s.qa2, s.qb2), attn_home(4 * hw, 4 * hw))
     end_enc()
     s.EN[...] = s.rese[...].astype(BF16)
     wait_eo = swap(s.EN, s.eg)
@@ -823,8 +956,8 @@
 
     dm_ready()
     back_heads(s.DM, s.WO, s.out_t)
+    weight_grad(put_slots(c_o, hw), [(lambda m: s.DM[:, m], s.MIX[...])])
     s.dtile[...] = jnp.zeros_like(s.dtile)
-    s.dfar[...] = jnp.zeros_like(s.dfar)
 
     def self_between(J):
         @pl.when(J == 0)
@@ -833,7 +966,7 @@
 
     bwd_attention(
         s.q3, s.k3, s.v3, s.t3, s.do3, s.lse, s.delta, s.out_t, s.dk, s.dv, put_cross, H2, query_block,
-        lambda J: jnp.where(J <= lo_block, 0, 1), hi_block + 1, s.tiles, s.kmask, s.dtile, s.dfar, self_between,
+        lambda J: jnp.where(J <= lo_block, 0, 1), hi_block + 1, s.tiles, s.dtile, self_between,
     )
 
     def clear(J, _):
@@ -853,34 +986,49 @@
         res[...] = other_part(order(2))
         d0.wait_recv()
         zs[...] = (res[...] + r0[...].astype(F32)).astype(BF16)
-        dz = remote(zs, rz, across)
-        dz.start()
+        n = res.shape[0] // 2
+        parts = [pl.ds(k * n, n) for k in range(2)]
+        dz = [remote(zs.at[w, :], rz.at[w, :], across) for w in parts]
+        for copy in dz:
+            copy.start()
         s1[...] = (other_part(3 - own) + own_part(1 - u_own)).astype(BF16)
         d1 = remote(s1, r1, sibling)
         d1.start()
         res[...] = other_part(own) + own_part(u_own)
 
-        def finish():
-            d1.wait_recv()
-            dz.wait_recv()
-            res[...] += r1[...].astype(F32) + rz[...].astype(F32)
-            for copy in (d0, d1, dz):
-                copy.wait_send()
-
-        return finish
-
-    end = scatter_first((s.s0, s.s1, s.zs, s.a0, s.a1, s.az), s.res)
+        def finish(k=None):
+            for q in (0, 1) if k is None else (k,):
+                if q == 0:
+                    d1.wait_recv()
+                w = parts[q]
+                dz[q].wait_recv()
+                res[w, :] += r1[w, :].astype(F32) + rz[w, :].astype(F32)
+                if q == 1:
+                    for copy in (d0, d1, *dz):
+                        copy.wait_send()
+
+        steps = chain(lambda: finish(0), lambda: finish(1))
+        return lambda k=None: [step() for step in (steps if k is None else steps[k : k + 1])]
+
+    KV, QO = pl.ds(0, 2 * hw), pl.ds(2 * hw, 2 * hw)
+    bufs = (s.ra1, s.rb1, s.ra2, s.rb2)
+    cut = lambda k: tuple(x.at[..., pl.ds(k * 2 * hw, 2 * hw)] for x in bufs)
+    grad_c[1]()
     weight_grad(put_slots(0, 2 * hw), [(lambda m: s.FIRST[:, m], s.DGU[:, : 4 * hw])])
+    grad_kv = collect((s.dW2, 0, KV), (s.dW2, 1, KV), cut(0), attn_home(0, 2 * hw, s.pair2))
     weight_grad(
         put_slots(c_q, hw),
-        [(lambda m: s.FIRST[tile_rows(lo_block), m], s.DQ[:N, :]), (lambda m: s.FIRST[tile_rows(hi_block), m], s.DQ[N:, :])],
+        [
+            (lambda m: s.FIRST[tile_rows(lo_block), m], s.DQ[:N, :]),
+            (lambda m: s.FIRST[tile_rows(hi_block), m], s.DQ[N:, :]),
+        ],
     )
-    weight_grad(put_slots(c_o, hw), [(lambda m: s.DM[:, m], s.MIX[...])])
-    S4 = pl.ds(0, 4 * hw)
-    grad_s = collect((s.dW2, 0, S4), (s.dW2, 1, S4), (s.ra1, s.rb1, s.ra2, s.rb2), attn_home(0, 4 * hw))
-    grad_c[1]()
+    grad_qo = collect((s.dW2, 0, QO), (s.dW2, 1, QO), cut(1), attn_home(2 * hw, 2 * hw, s.pair3))
+    end = scatter_first((s.s0, s.s1, s.zs, s.a0, s.a1, s.az), s.res)
+    grad_c[2]()
+    grad_kv[0]()
     s.small[...] = jnp.zeros_like(s.small)
-    flip = (key_at + query_at == TILE - 1).astype(F32)
+    flip = (key_at + query_at == TILE - 1).astype(BF16)
     blank = jnp.zeros((TILE, TILE), F32)
     head_row = lax.broadcasted_iota(jnp.int32, (16, span), 0)
     gap = lax.broadcasted_iota(jnp.int32, (1, span), 1)
@@ -889,66 +1037,94 @@
     for k, row in enumerate((near_back, next_back)):
 
         def line_up(h, diag):
-            turned = lax.dot_general(
-                flip, s.dtile[h, k], NN, precision=lax.Precision.HIGHEST, preferred_element_type=F32
-            )
+            full = s.dtile[h, k]
+            high = full.astype(BF16)
+            rest = full - high.astype(F32)
+            mid = rest.astype(BF16)
+            turned = mm(flip, high) + mm(flip, mid) + mm(flip, (rest - mid.astype(F32)).astype(BF16))
             lined = pltpu.roll(jnp.concatenate([turned, blank], axis=1), 0, 1, stride=1, stride_axis=0)
             return jnp.where(head_row == H2 * c + h, jnp.sum(lined, axis=0, keepdims=True), diag)
 
         diag = lax.fori_loop(0, H2, line_up, jnp.zeros((16, span), F32))
-        s.small[:, D : D + NB] += lax.dot_general(
+        s.small[:16, :NB] += lax.dot_general(
             diag, onehot(row), NT, precision=lax.Precision.HIGHEST, preferred_element_type=F32
         )
-    far_sum = jnp.sum(s.dfar[...], axis=1, keepdims=True)
-    bucket_at = lax.broadcasted_iota(jnp.int32, (1, NB), 1)
-    is_last = (bucket_at == buckets[:, -1:]).astype(F32)
-    bias_row = lax.broadcasted_iota(jnp.int32, (16, NB), 0)
-    for h in range(H2):
-        s.small[:, D : D + NB] += jnp.where(bias_row == H2 * c + h, far_sum[h : h + 1, :] * is_last, 0.0)
-    end()
-
+    far_row = lax.broadcasted_iota(jnp.int32, (16, 1), 0)
+
+    def far_total(h, acc):
+        total = jnp.sum(jnp.sum(s.dtile[h, 2], axis=0, keepdims=True), axis=1, keepdims=True)
+        return jnp.where(far_row == H2 * c + h, total, acc)
+
+    far_sum = lax.fori_loop(0, H2, far_total, jnp.zeros((16, 1), F32))
+    is_last = (lax.broadcasted_iota(jnp.int32, (1, NB), 1) == buckets[:, -1:]).astype(F32)
+    s.small[:16, :NB] += far_sum * is_last
+
+    def put_rows(buf, at, row):
+        for k in range(D // 128):
+            buf[at + k : at + k + 1, :] = row[:, 128 * k : 128 * (k + 1)]
+
+    put_rows(s.small, 16, gain_two)
+    put_rows(s.small, 24, gain_three)
+    sum_small = all_sum(s.small, s.small1, s.small2)
+    sum_small[0]()
     def back_one(w, acc):
         back, part_gain = norm_back_rows(s.res[w, :], s.XN[w, :].astype(F32), 0, s.inv1[w, :1])
-        s.s0[w, :] = (s.GR[w, :] + back).astype(BF16)
+        s.i0[w, :] = (s.GR[w, :] + back).astype(BF16)
         return acc + part_gain
 
-    gain_one = chunks(N, back_one, zero_gain)
-    wait_dg = swap(s.s0, s.dg)
-    for k, row in enumerate((gain_one, gain_two, gain_three)):
-        s.small[k : k + 1, :D] = row
-    for k, peer in enumerate((sibling, across, device(r, c, z2), x_chip, y_chip)):
-        s.small_out[k] = s.small[...]
-        hop = remote(s.small_out.at[k], s.small_in.at[k], peer)
-        hop.start()
-        if k == 1:
-            grad_s[0]()
-        if k == 4:
-            grad_s[1]()
-        hop.wait()
-        s.small[...] += s.small_in[k]
-    s.sm[...] = s.small[...]
+    swap_dg = swap_halves(s.i0, s.dg)
+    wait_dg = [pair[1] for pair in swap_dg]
+    gain_one = zero_gain
+    for k in range(2):
+        end(k)
+        gain_one = chunks(N, back_one, gain_one, k)
+        swap_dg[k][0]()
+        if k == 0:
+            grad_qo[0]()
+    s.late[...] = jnp.zeros_like(s.late)
+    put_rows(s.late, 0, gain_one)
+    sum_late = all_sum(s.late, s.late1, s.late2)
+    sum_late[0]()
+    grad_kv[1]()
+    sum_small[1]()
+    grad_qo[1]()
+    sum_late[1]()
+    grad_kv[2]()
+    sum_small[2]()
+    grad_qo[2]()
+    sum_late[2]()
+    s.sm[...] = jnp.zeros_like(s.sm)
+    for k in range(D // 128):
+        w = slice(128 * k, 128 * (k + 1))
+        s.sm[0:1, w] = s.late[k : k + 1, :]
+        s.sm[1:2, w] = s.small[16 + k : 17 + k, :]
+        s.sm[2:3, w] = s.small[24 + k : 25 + k, :]
+    s.sm[:, D:] = s.small[:16, :]
     wait_lo()
     wait_eo()
     grad_f[2]()
-    grad_c[2]()
-    wait_dg()
-    grad_s[2]()
+    grad_c[3]()
+    grad_kv[3]()
+    for wait in wait_dg:
+        wait()
+    grad_qo[3]()
     for copy in unsent:
         copy.wait_send()
     assert counter[0] <= part, counter[0]
 
 
-def layer_call(wpack, x, enc, og, gains, rel_bias, seq_lengths, rel_buckets, dims):
+def layer_call(pieces, x, enc, og, gains, rel_bias, seq_lengths, rel_buckets, dims):
     D, Hl, hd, FFL, N, NE, g, part = dims
     hw = Hl * hd
     H2, NC, NQ, NK = 2 * Hl, 2 * N, 4 * N, 4 * NE
     ra = D // 8
     vm, any_ = pl.BlockSpec(memory_space=pltpu.VMEM), pl.BlockSpec(memory_space=pl.ANY)
     sm_ = pl.BlockSpec(memory_space=pltpu.SMEM)
-    ins = dict(wpack=any_, x=any_, enc=any_, og=any_, gains=vm, rel_bias=vm, seq_lengths=sm_, rel_buckets=vm)
+    piece_names = ("p_sk", "p_sv", "p_sq", "p_so", "p_ck", "p_cv", "p_cq", "p_co", "p_gate", "p_up", "p_down")
+    ins = dict({k: any_ for k in piece_names}, x=any_, enc=any_, og=any_, gains=vm, rel_bias=vm, seq_lengths=sm_, rel_buckets=vm)
     outs = dict(
         lo=((N, D), BF16, any_), dg=((N, D), BF16, any_), eg=((NE, D), BF16, any_),
-        gz2=((4, ra, 8 * hw), BF16, any_), gzf=((2, ra, 3 * FFL), BF16, any_), sm=((16, D + 128), F32, vm),
+        gz2=((2, ra, 8 * hw), BF16, any_), gzf=((2, ra, 3 * FFL), BF16, any_), sm=((16, D + 128), F32, vm),
     )
     sc = {}
 
@@ -956,6 +1132,8 @@
         for name, shape in shapes.items():
             sc[name] = pltpu.VMEM(shape, dtype)
 
+    add(BF16, wpack=(ra, 8 * hw + 3 * FFL), raw=(6, ra, hw), raw_t=(2, hw, ra))
+    add(BF16, pair1=(D // 4, 4 * hw), pair2=(D // 4, 2 * hw), pair3=(D // 4, 2 * hw))
     add(BF16, W2=(2, D, 8 * hw), dW2=(2, D, 8 * hw), WF=(D, 3 * FFL), dWF=(D, 3 * FFL), WO=(2, D, hw), WCO=(2, D, hw))
     for k in "rq":
         add(BF16, **{k + "a1": (D // 2, 4 * hw), k + "b1": (2, D // 4, 4 * hw), k + "a2": (D // 4, 4 * hw), k + "b2": (D // 4, 4 * hw)})
@@ -964,15 +1142,16 @@
     add(BF16, **{k: (NE, D) for k in ("e0", "e1", "es", "f0", "f1", "fz", "EN")})
     add(F32, **{k: (N, D) for k in ("MID", "LAT", "GR", "res")}, rese=(NE, D))
     add(F32, inv1=(N, 128), inv2=(N, 128), inv3=(N, 128), ok=(N, 128))
-    add(BF16, q3=(H2, NC, hd), k3=(H2, NQ, hd), v3=(H2, NQ, hd), cq3=(H2, NC, hd), ck3=(H2, NK, hd), cv3=(H2, NK, hd))
+    add(BF16, q3=(H2, NC, 128), k3=(H2, NQ, 128), v3=(H2, NQ, hd), cq3=(H2, NC, hd), ck3=(H2, NK, hd), cv3=(H2, NK, hd))
     add(BF16, do3=(H2, NC, hd), t3=(H2, hd, NQ), ct3=(H2, hd, NK))
     add(F32, out_t=(2 * hw, NC), out_t2=(2 * hw, NC), lse=(8, NC), lse2=(8, NC), delta=(8, NC))
-    add(F32, dk=(H2, TILE, hd), dv=(H2, TILE, hd))
+    add(F32, dk=(H2, TILE, 128), dv=(H2, TILE, hd))
     add(BF16, MIX=(NC, 2 * hw), MIX2=(NC, 2 * hw), HID=(NQ, FFL), DGU=(NQ, 2 * FFL), DQ=(NC, 2 * hw))
     add(BF16, tiles=(H2, 3, TILE, TILE))
-    add(F32, dtile=(H2, 2, TILE, TILE), dfar=(8, TILE), kmask=(NQ, 128), vecs=(24, 2 * TILE))
-    add(F32, tab=(4, NB, 128), len_out=(8, 128), len_in=(8, 128), len_row=(8, 128))
-    add(F32, small=(16, D + 128), small_out=(5, 16, D + 128), small_in=(5, 16, D + 128))
+    add(F32, dtile=(H2, 3, TILE, TILE), vecs=(24, 2 * TILE))
+    add(F32, tab=(4, 8, 128), len_out=(8, 128), len_in=(8, 128), len_row=(8, 128))
+    add(F32, small=(32, 128), small1=(8, 32, 128), small2=(4, 32, 128))
+    add(F32, late=(8, 128), late1=(8, 8, 128), late2=(4, 8, 128))
     names = list(ins) + list(outs) + list(sc) + ["sems"]
     return pl.pallas_call(
         functools.partial(layer_kernel, dims, names),
@@ -982,7 +1161,7 @@
         scratch_shapes=list(sc.values()) + [pltpu.SemaphoreType.DMA((part,))],
         compiler_params=pltpu.CompilerParams(collective_id=0, has_side_effects=True, vmem_limit_bytes=67043328),
         name="layer",
-    )(wpack, x, enc, og, gains, rel_bias, seq_lengths, rel_buckets)
+    )(*pieces, x, enc, og, gains, rel_bias, seq_lengths, rel_buckets)
 
 
 def finish_kernel(dims, lo, dg, eg, gz2, gzf, sm, *outs):
@@ -993,11 +1172,11 @@
     o_dg[...] = dg[...].astype(F32)
     o_eg[...] = eg[...].astype(F32)
     o_gains[...] = sm[:3, :D]
-    o_bias[...] = sm[:, D:].T[:NB, : 4 * Hl]
+    o_bias[...] = sm[: 4 * Hl, D : D + NB]
 
     def total(col, n):
         w = pl.ds(col, n)
-        return (gz2[0, :, w].astype(F32) + gz2[1, :, w].astype(F32)) + (gz2[2, :, w].astype(F32) + gz2[3, :, w].astype(F32))
+        return gz2[0, :, w].astype(F32) + gz2[1, :, w].astype(F32)
 
     for base, parts in ((0, (sk, sv, sq, so)), (4 * hw, (ck, cv, cq, co))):
         y = total(base, 4 * hw)
@@ -1007,16 +1186,16 @@
     f = gzf[0].astype(F32) + gzf[1].astype(F32)
     gg[...] = f[:, :FFL]
     gu[...] = f[:, FFL : 2 * FFL]
-    gd[...] = f[:, 2 * FFL :].T
+    gd[...] = f[:, 2 * FFL :]
 
 
 def finish_call(dims, lo, dg, eg, gz2, gzf, sm):
     D, Hl, hd, FFL, N, NE, g, part = dims
     hw, ra = Hl * hd, D // 8
     vm = pl.BlockSpec(memory_space=pltpu.VMEM)
-    shapes = [((N, D), BF16), ((N, D), F32), ((NE, D), F32), ((3, D), F32), ((NB, 4 * Hl), F32)]
+    shapes = [((N, D), BF16), ((N, D), F32), ((NE, D), F32), ((3, D), F32), ((4 * Hl, NB), F32)]
     shapes += [((ra, hw), F32)] * 3 + [((hw, ra), F32)] + [((ra, hw), F32)] * 3 + [((hw, ra), F32)]
-    shapes += [((ra, FFL), F32)] * 2 + [((FFL, ra), F32)]
+    shapes += [((ra, FFL), F32)] * 3
     return pl.pallas_call(
         functools.partial(finish_kernel, dims),
         out_shape=[jax.ShapeDtypeStruct(*v) for v in shapes],
@@ -1040,22 +1219,29 @@
     size = lax.axis_size("dp")
     g = size // 8
     rows, erows = decoder_in.shape[0], encoder_out.shape[0]
-    wpack = jnp.concatenate(
-        [self_key, self_value, self_query, self_out.T, cross_key, cross_value, cross_query, cross_out.T,
-         gate_weight, up_weight, down_weight.T], axis=1,
+    pieces = (
+        self_key, self_value, self_query, self_out, cross_key, cross_value, cross_query, cross_out,
+        gate_weight, up_weight, down_weight.T,
     )
-    step = 1
-    while step < g:
-        other = exchange(wpack, step, size)
-        upper = (lax.axis_index("dp") // step) % 2
-        wpack = jnp.where(upper == 1, jnp.concatenate([other, wpack], 0), jnp.concatenate([wpack, other], 0))
-        step *= 2
-    dims = (width, heads, w // heads, f, rows, erows, g, 320)
+    if g > 1:
+        wpack = jnp.concatenate([x.T if k in (3, 7) else x for k, x in enumerate(pieces)], axis=1)
+        step = 1
+        while step < g:
+            other = exchange(wpack, step, size)
+            upper = (lax.axis_index("dp") // step) % 2
+            wpack = jnp.where(upper == 1, jnp.concatenate([other, wpack], 0), jnp.concatenate([wpack, other], 0))
+            step *= 2
+        cols = [wpack[:, k * w : (k + 1) * w] for k in range(8)]
+        cols[3], cols[7] = cols[3].T, cols[7].T
+        pieces = (*cols, *(wpack[:, 8 * w + k * f : 8 * w + (k + 1) * f] for k in range(3)))
+    dims = (width, heads, w // heads, f, rows, erows, g, 480)
     lo, dg, eg, gz2, gzf, sm = layer_call(
-        wpack, decoder_in, encoder_out, out_grad, norm_gains, rel_bias, seq_lengths, rel_buckets.reshape(1, -1), dims
+        pieces, decoder_in, encoder_out, out_grad, norm_gains, rel_bias.T, seq_lengths, rel_buckets.reshape(1, -1), dims
     )
     if g == 1:
-        return tuple(finish_call(dims, lo, dg, eg, gz2, gzf, sm))
+        outs = list(finish_call(dims, lo, dg, eg, gz2, gzf, sm))
+        outs[4], outs[15] = outs[4].T, outs[15].T
+        return tuple(outs)
     gw = jnp.concatenate([jnp.sum(gz2.astype(F32), axis=0), jnp.sum(gzf.astype(F32), axis=0)], axis=1)
     step = g // 2
     while step >= 1:

time: 243 us -> 219 us (0.901)
  Pallas kernels: 231 us -> 217 us
  local copies, waits for them, and re-layouts: 8.22 us -> 0 us
    pallas_call x1, Pallas kernels: 228 us -> 214 us  [layer_call(): pl.pallas_call(functools.partial(layer_kernel, dims, names), out_shape=[j...]
    pallas_call x2 -> x0, local copies, waits for them, and re-layouts: 3.14 us -> none  [finish_call(): pl.pallas_call(functools.partial(finish_kernel, dims), out_shape=[jax.Sha...]
    unnamed x3 -> x0, local copies, waits for them, and re-layouts: 3.14 us -> none
where the time goes in v5:
time: 219 us
  Pallas kernels  217 us (99%)
    pallas_call x1, Pallas kernels, layer_call(): pl.pallas_call(functools.partial(layer_kernel, dims, names), out_shape=[j...  214 us

profile of v5, /device:TPU:1, one launch (start us, length us, event | category | flops | bytes accessed | tf_op | source)
XLA Modules:
  0.0 218.6 jit_solution(3637951908653767847)
XLA Ops:
  1.3 214.0 %layer.1 = (bf16[256,768]{1,0:T(8,128)(2,1)}, bf16[256,768]{1,0:T(8,128)(2,1)}, bf16[128,768]{1,0:T(8,128)(2,1)}, bf16[2,96,1536]{2,1,0:T(8,128)(2,1)}, bf16[2,96,1536]{2,1,0:T(8,128)(2,1)}, /*index=5*/f32[16,896]{1,0:T(8,128)}) custom-call(bf16[96,192]{1,0:T(8,128)(2,1)} %refs_0_.1, bf16[96,192]{1,0:T(8,128)(2,1)} %refs_1_.1, bf16[96,192]{1,0:T(8,128)(2,1)} %refs_2_.1, ...), custom_call_target="tpu_custom_call" | custom-call | tf_op jit(solution)/shard_map/layer/pallas_call | solution.py:1156
  215.3 3.2 %finish.1 = (bf16[256,768]{1,0:T(8,128)(2,1)}, f32[256,768]{1,0:T(8,128)}, f32[128,768]{1,0:T(8,128)}, f32[3,768]{1,0:T(4,128)}, f32[12,32]{1,0:T(8,128)}, /*ind...) custom-call(bf16[256,768]{1,0:T(8,128)(2,1)} %get-tuple-element.38.l, ...), custom_call_target="tpu_custom_call" | custom-call | tf_op jit(solution)/shard_map/finish/pallas_call | solution.py:1199

commit v6 on v5

--- a/solution.py
+++ b/solution.py
@@ -48,6 +48,7 @@
                 p = jnp.exp(s - m2)
                 l2 = l * a + jnp.sum(p, axis=0, keepdims=True)
                 new.append((m2, l2, acc * a + mm(vt3[h, :, rj], p.astype(BF16))))
+            between(u, J)
             return tuple(new)
 
         init = tuple(
@@ -58,7 +59,6 @@
             m, l, acc = res[h]
             out_t[h * hd : (h + 1) * hd, ri] = acc / l
             lse[h : h + 1, ri] = m + jnp.log(l)
-        between(u)
         return 0
 
     lax.fori_loop(0, 2, qblock, 0)
@@ -570,9 +570,9 @@
     w_qo = attn_weights(2 * hw, 2 * hw)
     swap_x = swap_halves(s.x, s.XN)
     w_kv[0]()
+    w_qo[0]()
     for k in range(2):
         swap_x[k][0]()
-    w_qo[0]()
     s.tab[z] = jnp.zeros_like(s.tab[z])
     s.tab[z, :Hl, :NB] = s.rel_bias[...].astype(F32)
     tab_base = slots(4)
@@ -614,6 +614,7 @@
             return 0
 
         lax.fori_loop(0, Hl, build, 0)
+    w_qo[1]()
     length = s.len_row[0:1, :]
     lane = lax.broadcasted_iota(jnp.int32, (TILE, 128), 1)
 
@@ -633,6 +634,7 @@
 
     lax.fori_loop(0, 4, extra_lane, 0)
     ga = gather(s.FIRST, N)
+    w_kv[2]()
 
     def norm_one(w, _):
         norm_rows(s.XN[w, :].astype(F32), 0, s.inv1, w, s.FIRST, rows_in(own, w))
@@ -642,25 +644,27 @@
         swap_x[k][1]()
         chunks(N, norm_one, 0, k)
         ga.start(k)
-    w_kv[2]()
-    w_c = attn_weights(4 * hw, 4 * hw)
+        if k == 0:
+            w_qo[2]()
+    w_kv[3]()
+    w_ca = attn_weights(4 * hw, 2 * hw)
+    w_cb = attn_weights(6 * hw, 2 * hw)
     w_f = ff_weights(o_ff, 3 * FFL)
-    w_c[0]()
-    w_qo[1]()
-    w_kv[3]()
-    w_qo[2]()
+    w_ca[0]()
+    w_cb[0]()
+    w_qo[3]()
+    w_ca[1]()
     wait_e = swap(s.enc, s.EN)
+    w_cb[1]()
     ga.side()
     ga.forward()
-    w_c[1]()
     w_f[0]()
-    w_qo[3]()
-    w_c[2]()
+    w_ca[2]()
+    ga.far()
     wait_o = swap(s.og, s.ON)
     wait_e()
     s.ENC[block(own, NE), :] = s.EN[...]
     ge = gather_all(s.ENC, NE)
-    ga.far()
     w_kv[4]()
     w_qo[4]()
 
@@ -685,6 +689,8 @@
         return 0
 
     lax.fori_loop(0, 4, project_one, 0)
+    w_cb[2]()
+    w_ca[3]()
 
     def turn(dst, src):
         def one(h, _):
@@ -696,13 +702,13 @@
     turn(s.t3, s.v3)
     s.WO[...] = s.W2[:, :, c_o : c_o + hw]
 
-    def after_first(u):
-        @pl.when(u == 0)
+    def after_first(u, J):
+        @pl.when(jnp.logical_and(u == 1, J == 0))
         def _():
-            w_c[3]()
-            w_f[1]()
             ge.side()
             ge.forward()
+            w_cb[3]()
+            w_f[1]()
 
     fwd_attention(s.q3, s.k3, s.t3, s.out_t, s.lse, H2, query_block, lambda I: I + 1, s.tiles, after_first)
     s.MIX[...] = s.out_t[...].T.astype(BF16)
@@ -727,9 +733,18 @@
     for k in range(2):
         chunks(N, norm_two, 0, k)
         second_go(k)
+    wait_o()
+    own_pos = lax.broadcasted_iota(jnp.int32, (N, 128), 0) + own * N
+    s.ok[...] = (own_pos.astype(F32) < length).astype(F32)
+
+    def mask_rows(w, _):
+        s.GF[rows_in(own, w), :] = (s.ON[w, :].astype(F32) * s.ok[w, :1]).astype(BF16)
+        return 0
+
+    chunks(N, mask_rows)
+    gg = gather_all(s.GF, N)
     ge.far()
-    w_c[4]()
-    s.WCO[...] = s.W2[:, :, c_co : c_co + hw]
+    w_ca[4]()
 
     def project_enc(i, _):
         w = block(i, N)
@@ -742,6 +757,8 @@
 
     lax.fori_loop(0, NK // N, project_enc, 0)
     turn(s.ct3, s.cv3)
+    w_cb[4]()
+    s.WCO[...] = s.W2[:, :, c_co : c_co + hw]
     second_ready()
 
     def project_two(u, _):
@@ -752,19 +769,8 @@
         return 0
 
     lax.fori_loop(0, 2, project_two, 0)
-    wait_o()
-    own_pos = lax.broadcasted_iota(jnp.int32, (N, 128), 0) + own * N
-    s.ok[...] = (own_pos.astype(F32) < length).astype(F32)
-
-    def mask_rows(w, _):
-        s.GF[rows_in(own, w), :] = (s.ON[w, :].astype(F32) * s.ok[w, :1]).astype(BF16)
-        return 0
-
-    chunks(N, mask_rows)
-    gg = gather_all(s.GF, N)
-
-    def after_cross(u):
-        @pl.when(u == 0)
+    def after_cross(u, J):
+        @pl.when(jnp.logical_and(u == 0, J == 0))
         def _():
             w_f[2]()
 
@@ -846,6 +852,10 @@
     grad_f = collect(
         (s.dWF, None, pl.ds(0, half_f)), (s.dWF, None, pl.ds(half_f, half_f)), (s.ra1, s.rb1, s.ra2, s.rb2), ff_home
     )
+    turn(s.ct3, s.ck3)
+    turn(s.t3, s.k3)
+    s.dtile[...] = jnp.zeros_like(s.dtile)
+
     def back_three(w, acc):
         back, part_gain = norm_back_rows(s.res[w, :], s.LAT[w, :], 2, s.inv3[w, :1])
         d = s.GF[rows_in(own, w), :].astype(F32) + back
@@ -863,7 +873,6 @@
         lambda i: mm(s.HID[block(i, N), :], s.WF[:, 2 * FFL :], NT), (s.s0, s.s1, s.zs, s.b0, s.b1, s.bz), s.res
     )
 
-    turn(s.ct3, s.ck3)
 
     def back_heads(src, weight, out_t):
         def body(u, _):
@@ -952,12 +961,10 @@
     end_enc()
     s.EN[...] = s.rese[...].astype(BF16)
     wait_eo = swap(s.EN, s.eg)
-    turn(s.t3, s.k3)
 
     dm_ready()
     back_heads(s.DM, s.WO, s.out_t)
     weight_grad(put_slots(c_o, hw), [(lambda m: s.DM[:, m], s.MIX[...])])
-    s.dtile[...] = jnp.zeros_like(s.dtile)
 
     def self_between(J):
         @pl.when(J == 0)
@@ -1079,8 +1086,7 @@
         end(k)
         gain_one = chunks(N, back_one, gain_one, k)
         swap_dg[k][0]()
-        if k == 0:
-            grad_qo[0]()
+    grad_qo[0]()
     s.late[...] = jnp.zeros_like(s.late)
     put_rows(s.late, 0, gain_one)
     sum_late = all_sum(s.late, s.late1, s.late2)

time: 219 us -> 208 us (0.950)
  Pallas kernels: 217 us -> 207 us
    pallas_call x1, Pallas kernels: 214 us -> 203 us  [layer_call(): pl.pallas_call(functools.partial(layer_kernel, dims, names), out_shape=[j...]
where the time goes in v6:
time: 208 us
  Pallas kernels  207 us (100%)
    pallas_call x1, Pallas kernels, layer_call(): pl.pallas_call(functools.partial(layer_kernel, dims, names), out_shape=[j...  203 us

profile of v6, /device:TPU:1, one launch (start us, length us, event | category | flops | bytes accessed | tf_op | source)
XLA Modules:
  0.0 207.9 jit_solution(15186624451438997319)
XLA Ops:
  1.3 203.3 %layer.1 = (bf16[256,768]{1,0:T(8,128)(2,1)}, bf16[256,768]{1,0:T(8,128)(2,1)}, bf16[128,768]{1,0:T(8,128)(2,1)}, bf16[2,96,1536]{2,1,0:T(8,128)(2,1)}, bf16[2,96,1536]{2,1,0:T(8,128)(2,1)}, /*index=5*/f32[16,896]{1,0:T(8,128)}) custom-call(bf16[96,192]{1,0:T(8,128)(2,1)} %refs_0_.1, bf16[96,192]{1,0:T(8,128)(2,1)} %refs_1_.1, bf16[96,192]{1,0:T(8,128)(2,1)} %refs_2_.1, ...), custom_call_target="tpu_custom_call" | custom-call | tf_op jit(solution)/shard_map/layer/pallas_call | solution.py:1162
  204.6 3.2 %finish.1 = (bf16[256,768]{1,0:T(8,128)(2,1)}, f32[256,768]{1,0:T(8,128)}, f32[128,768]{1,0:T(8,128)}, f32[3,768]{1,0:T(4,128)}, f32[12,32]{1,0:T(8,128)}, /*ind...) custom-call(bf16[256,768]{1,0:T(8,128)(2,1)} %get-tuple-element.38.l, ...), custom_call_target="tpu_custom_call" | custom-call | tf_op jit(solution)/shard_map/finish/pallas_call | solution.py:1205

commit v7 on v6

--- a/solution.py
+++ b/solution.py
@@ -985,7 +985,7 @@
     own_part = query_grad(c_q)
     other_part = kv_grad(N, 0)
 
-    def scatter_first(bufs, res):
+    def scatter_first(bufs, res, filler):
         s0, s1, zs, r0, r1, rz = bufs
         s0[...] = other_part(order(3)).astype(BF16)
         d0 = remote(s0, r0, sibling)
@@ -998,6 +998,7 @@
         dz = [remote(zs.at[w, :], rz.at[w, :], across) for w in parts]
         for copy in dz:
             copy.start()
+        filler()
         s1[...] = (other_part(3 - own) + own_part(1 - u_own)).astype(BF16)
         d1 = remote(s1, r1, sibling)
         d1.start()
@@ -1023,15 +1024,20 @@
     grad_c[1]()
     weight_grad(put_slots(0, 2 * hw), [(lambda m: s.FIRST[:, m], s.DGU[:, : 4 * hw])])
     grad_kv = collect((s.dW2, 0, KV), (s.dW2, 1, KV), cut(0), attn_home(0, 2 * hw, s.pair2))
-    weight_grad(
-        put_slots(c_q, hw),
-        [
-            (lambda m: s.FIRST[tile_rows(lo_block), m], s.DQ[:N, :]),
-            (lambda m: s.FIRST[tile_rows(hi_block), m], s.DQ[N:, :]),
-        ],
-    )
-    grad_qo = collect((s.dW2, 0, QO), (s.dW2, 1, QO), cut(1), attn_home(2 * hw, 2 * hw, s.pair3))
-    end = scatter_first((s.s0, s.s1, s.zs, s.a0, s.a1, s.az), s.res)
+    query_part = []
+
+    def query_grads():
+        weight_grad(
+            put_slots(c_q, hw),
+            [
+                (lambda m: s.FIRST[tile_rows(lo_block), m], s.DQ[:N, :]),
+                (lambda m: s.FIRST[tile_rows(hi_block), m], s.DQ[N:, :]),
+            ],
+        )
+        query_part.append(collect((s.dW2, 0, QO), (s.dW2, 1, QO), cut(1), attn_home(2 * hw, 2 * hw, s.pair3)))
+
+    end = scatter_first((s.s0, s.s1, s.zs, s.a0, s.a1, s.az), s.res, query_grads)
+    grad_qo = query_part[0]
     grad_c[2]()
     grad_kv[0]()
     s.small[...] = jnp.zeros_like(s.small)

time: 208 us -> 207 us (level)
  no operation moved by 1% of the time
where the time goes in v7:
time: 207 us; the launch traced here: 206 us
  Pallas kernels  205 us (99%)
    pallas_call x1, Pallas kernels, layer_call(): pl.pallas_call(functools.partial(layer_kernel, dims, names), out_shape=[j...  202 us

profile of v7, /device:TPU:1, one launch (start us, length us, event | category | flops | bytes accessed | tf_op | source)
XLA Modules:
  0.0 206.5 jit_solution(10376465171867888278)
XLA Ops:
  1.3 201.8 %layer.1 = (bf16[256,768]{1,0:T(8,128)(2,1)}, bf16[256,768]{1,0:T(8,128)(2,1)}, bf16[128,768]{1,0:T(8,128)(2,1)}, bf16[2,96,1536]{2,1,0:T(8,128)(2,1)}, bf16[2,96,1536]{2,1,0:T(8,128)(2,1)}, /*index=5*/f32[16,896]{1,0:T(8,128)}) custom-call(bf16[96,192]{1,0:T(8,128)(2,1)} %refs_0_.1, bf16[96,192]{1,0:T(8,128)(2,1)} %refs_1_.1, bf16[96,192]{1,0:T(8,128)(2,1)} %refs_2_.1, ...), custom_call_target="tpu_custom_call" | custom-call | tf_op jit(solution)/shard_map/layer/pallas_call | solution.py:1168
  203.1 3.2 %finish.1 = (bf16[256,768]{1,0:T(8,128)(2,1)}, f32[256,768]{1,0:T(8,128)}, f32[128,768]{1,0:T(8,128)}, f32[3,768]{1,0:T(4,128)}, f32[12,32]{1,0:T(8,128)}, /*ind...) custom-call(bf16[256,768]{1,0:T(8,128)(2,1)} %get-tuple-element.38.l, ...), custom_call_target="tpu_custom_call" | custom-call | tf_op jit(solution)/shard_map/finish/pallas_call | solution.py:1211

commit v8 on v7

--- a/solution.py
+++ b/solution.py
@@ -1040,6 +1040,19 @@
     grad_qo = query_part[0]
     grad_c[2]()
     grad_kv[0]()
+    def back_one(w, acc):
+        back, part_gain = norm_back_rows(s.res[w, :], s.XN[w, :].astype(F32), 0, s.inv1[w, :1])
+        s.i0[w, :] = (s.GR[w, :] + back).astype(BF16)
+        return acc + part_gain
+
+    swap_dg = swap_halves(s.i0, s.dg)
+    wait_dg = [pair[1] for pair in swap_dg]
+    gain_one = zero_gain
+    for k in range(2):
+        end(k)
+        gain_one = chunks(N, back_one, gain_one, k)
+        swap_dg[k][0]()
+    grad_qo[0]()
     s.small[...] = jnp.zeros_like(s.small)
     flip = (key_at + query_at == TILE - 1).astype(BF16)
     blank = jnp.zeros((TILE, TILE), F32)
@@ -1080,19 +1093,6 @@
     put_rows(s.small, 24, gain_three)
     sum_small = all_sum(s.small, s.small1, s.small2)
     sum_small[0]()
-    def back_one(w, acc):
-        back, part_gain = norm_back_rows(s.res[w, :], s.XN[w, :].astype(F32), 0, s.inv1[w, :1])
-        s.i0[w, :] = (s.GR[w, :] + back).astype(BF16)
-        return acc + part_gain
-
-    swap_dg = swap_halves(s.i0, s.dg)
-    wait_dg = [pair[1] for pair in swap_dg]
-    gain_one = zero_gain
-    for k in range(2):
-        end(k)
-        gain_one = chunks(N, back_one, gain_one, k)
-        swap_dg[k][0]()
-    grad_qo[0]()
     s.late[...] = jnp.zeros_like(s.late)
     put_rows(s.late, 0, gain_one)
     sum_late = all_sum(s.late, s.late1, s.late2)

time: 207 us -> 208 us (level)
  no operation moved by 1% of the time
where the time goes in v8:
time: 208 us
  Pallas kernels  206 us (99%)
    pallas_call x1, Pallas kernels, layer_call(): pl.pallas_call(functools.partial(layer_kernel, dims, names), out_shape=[j...  203 us

profile of v8, /device:TPU:1, one launch (start us, length us, event | category | flops | bytes accessed | tf_op | source)
XLA Modules:
  0.0 207.8 jit_solution(2088296291013975683)
XLA Ops:
  1.3 203.2 %layer.1 = (bf16[256,768]{1,0:T(8,128)(2,1)}, bf16[256,768]{1,0:T(8,128)(2,1)}, bf16[128,768]{1,0:T(8,128)(2,1)}, bf16[2,96,1536]{2,1,0:T(8,128)(2,1)}, bf16[2,96,1536]{2,1,0:T(8,128)(2,1)}, /*index=5*/f32[16,896]{1,0:T(8,128)}) custom-call(bf16[96,192]{1,0:T(8,128)(2,1)} %refs_0_.1, bf16[96,192]{1,0:T(8,128)(2,1)} %refs_1_.1, bf16[96,192]{1,0:T(8,128)(2,1)} %refs_2_.1, ...), custom_call_target="tpu_custom_call" | custom-call | tf_op jit(solution)/shard_map/layer/pallas_call | solution.py:1168
  204.5 3.2 %finish.1 = (bf16[256,768]{1,0:T(8,128)(2,1)}, f32[256,768]{1,0:T(8,128)}, f32[128,768]{1,0:T(8,128)}, f32[3,768]{1,0:T(4,128)}, f32[12,32]{1,0:T(8,128)}, /*ind...) custom-call(bf16[256,768]{1,0:T(8,128)(2,1)} %get-tuple-element.38.l, ...), custom_call_target="tpu_custom_call" | custom-call | tf_op jit(solution)/shard_map/finish/pallas_call | solution.py:1211
